TPU v7x, 32 devices: a whole 2x2x4 slice. The times are simulated.
32 devices in a mesh: rep: 8 (over y, x, core), shard: 4 (over z).
Axes of the slice: x: 2, y: 2, z: 4, core: 2. Of those that a mesh axis runs over, the one named last changes fastest.
Arguments:
- tokens: bfloat16 [2, 8, 2048, 1536], P(None, 'rep', 'shard'), may hold values from -6 to 6
- cotangent: bfloat16 [2, 8, 2048, 1536], P(None, 'rep', 'shard'), may hold values from -6 to 6
- routes: int32 [2, 8, 2048, 2], P(None, 'rep', 'shard'), may hold values from 0 to 3, all different within a row; in each aligned block of 512 rows (0 to 511, 512 to 1023, ..., all dimensions but the last counted through in order) at most 384 rows name the same one
- lengths: int32 [2, 8, 3], replicated, may hold values from 1 to 2046, as said below
- attn_gain: bfloat16 [1536], P('shard'), may hold values from 0.5 to 1.5
- w_query: bfloat16 [1536, 1536], P('shard'), may hold values from -0.15625 to 0.15625
- w_key: bfloat16 [1536, 512], P('shard'), may hold values from -0.15625 to 0.15625
- w_value: bfloat16 [1536, 512], P('shard'), may hold values from -0.15625 to 0.15625
- w_out: bfloat16 [1536, 1536], P('shard'), may hold values from -2.5 to 2.5
- moe_gain: bfloat16 [1536], P('shard'), may hold values from 0.5 to 1.5
- w_router: bfloat16 [1536, 4], P('shard'), may hold values from -0.109375 to 0.109375
- w_gate: bfloat16 [4, 1536, 1024], P(None, 'shard'), may hold values from -0.15625 to 0.15625
- w_up: bfloat16 [4, 1536, 1024], P(None, 'shard'), may hold values from -0.15625 to 0.15625
- w_down: bfloat16 [4, 1024, 1536], P(None, 'shard'), may hold values from -0.25 to 0.25
Outputs:
- block_out: bfloat16 [2, 8, 2048, 1536], P(None, 'rep', 'shard')
- input_grad: bfloat16 [2, 8, 2048, 1536], P(None, 'rep', 'shard')
- grad_attn_gain: float32 [1536], P('shard')
- grad_query: float32 [1536, 1536], P('shard')
- grad_key: float32 [1536, 512], P('shard')
- grad_value: float32 [1536, 512], P('shard')
- grad_out: float32 [1536, 1536], P('shard')
- grad_moe_gain: float32 [1536], P('shard')
- grad_router: float32 [1536, 4], P('shard')
- grad_gate: float32 [4, 1536, 1024], P(None, 'shard')
- grad_up: float32 [4, 1536, 1024], P(None, 'shard')
- grad_down: float32 [4, 1024, 1536], P(None, 'shard')
Inputs may be any that keep to these rules, and one draw needn't show every extreme that they name: `routes`: each row names 2 different experts. Within the rows of one device for one micro-batch (aligned blocks of 512 rows) no expert is named more than 384 times, a bound that some block reaches. Each row holds 3 document lengths in order that sum to 2048; its largest is 2048 / 3 or more, and some row's largest is 2046.
All inputs are finite; a program needn't handle non-finite values.
Results may differ from a plain program's by a relative error of at most 0.023.
Values may be sent and summed in bfloat16 or wider, within the bound.
No kernel may reach another device: no remote copies, remote signals or barrier semaphores. Data moves between devices by JAX's collectives and lax.ppermute only.
A program may use at most 384 MiB of HBM per device.

v0:
```python
import jax
import jax.numpy as jnp
from jax import lax
from jax.sharding import PartitionSpec as P

HEAD = 64


EPSILON = 1e-05
NEGATIVE = -1e30


def rms_scale(rows_in):
    return lax.rsqrt(jnp.mean(rows_in * rows_in, axis=-1, keepdims=True) + EPSILON)


def norm_back(rows_in, row_scale, gain_row, grad_normed):
    grad_gain = jnp.sum(grad_normed * rows_in * row_scale, axis=0)
    scaled = grad_normed * gain_row
    scale_cubed = row_scale * row_scale * row_scale
    grad_rows = row_scale * scaled - rows_in * scale_cubed * jnp.mean(
        scaled * rows_in, axis=-1, keepdims=True
    )
    return (grad_rows, grad_gain)


def select_from(wanted, pieces):
    piece_count = pieces[0].shape[1]
    matches = jnp.arange(piece_count, dtype=jnp.int32)[None, :] == wanted[:, None]
    return tuple(
        (
            jnp.sum(
                jnp.where(matches[:, :, None, None], shard_piece, jnp.zeros_like(shard_piece)),
                axis=1,
            )
            for shard_piece in pieces
        )
    )


def document_ids(places, bounds):
    return jnp.sum((places[:, :, None] >= bounds[:, None, :]).astype(jnp.int32), axis=2)


def block_scores(q_heads, k_heads, v_heads, q_ids, q_pos, k_ids, index, head_scale):
    width = q_heads.shape[1]
    start = index * width
    k_block = lax.dynamic_slice_in_dim(k_heads, start, width, 1)
    v_block = lax.dynamic_slice_in_dim(v_heads, start, width, 1)
    id_block = lax.dynamic_slice_in_dim(k_ids, start, width, 0)
    positions = start + jnp.arange(width, dtype=jnp.int32)
    visible = (q_ids[:, None] == id_block[None, :]) & (q_pos[:, None] >= positions[None, :])
    scores = (
        jnp.einsum("ktgc,ksc->ktgs", q_heads, k_block, preferred_element_type=jnp.float32)
        * head_scale
    )
    return (jnp.where(visible[None, :, None, :], scores, NEGATIVE), k_block, v_block, start)


def attend_forward(
    q_heads, k_heads, v_heads, q_ids, q_pos, k_ids, first_block, last_block, head_scale
):
    stat_shape = q_heads.shape[:3]

    def gather_stats(index, carried):
        highest, totals = carried
        scores, k_block, v_block, start = block_scores(
            q_heads, k_heads, v_heads, q_ids, q_pos, k_ids, index, head_scale
        )
        new_high = jnp.maximum(highest, jnp.max(scores, axis=-1))
        totals = totals * jnp.exp(highest - new_high) + jnp.sum(
            jnp.exp(scores - new_high[..., None]), axis=-1
        )
        return (new_high, totals)

    highest, totals = lax.fori_loop(
        first_block,
        last_block + 1,
        gather_stats,
        (jnp.full(stat_shape, NEGATIVE, jnp.float32), jnp.zeros(stat_shape, jnp.float32)),
    )
    log_totals = highest + jnp.log(totals)

    def add_values(index, mixed):
        scores, k_block, v_block, start = block_scores(
            q_heads, k_heads, v_heads, q_ids, q_pos, k_ids, index, head_scale
        )
        weights = jnp.exp(scores - log_totals[..., None]).astype(jnp.bfloat16)
        return mixed + jnp.einsum(
            "ktgs,ksc->ktgc", weights, v_block, preferred_element_type=jnp.float32
        )

    mixed = lax.fori_loop(
        first_block, last_block + 1, add_values, jnp.zeros(q_heads.shape, jnp.float32)
    )
    return (mixed.astype(jnp.bfloat16), log_totals)


def attend_back(
    q_heads,
    k_heads,
    v_heads,
    g_heads,
    log_totals,
    q_ids,
    q_pos,
    k_ids,
    first_block,
    last_block,
    head_scale,
):

    def inner_terms(index, inner):
        scores, k_block, v_block, start = block_scores(
            q_heads, k_heads, v_heads, q_ids, q_pos, k_ids, index, head_scale
        )
        probabilities = jnp.exp(scores - log_totals[..., None])
        grad_probs = jnp.einsum(
            "ktgc,ksc->ktgs", g_heads, v_block, preferred_element_type=jnp.float32
        )
        return inner + jnp.sum(probabilities * grad_probs, axis=-1)

    inner = lax.fori_loop(
        first_block, last_block + 1, inner_terms, jnp.zeros(q_heads.shape[:3], jnp.float32)
    )

    def grad_terms(index, carried):
        grad_q, grad_k, grad_v = carried
        scores, k_block, v_block, start = block_scores(
            q_heads, k_heads, v_heads, q_ids, q_pos, k_ids, index, head_scale
        )
        probabilities = jnp.exp(scores - log_totals[..., None])
        grad_probs = jnp.einsum(
            "ktgc,ksc->ktgs", g_heads, v_block, preferred_element_type=jnp.float32
        )
        grad_scores = (probabilities * (grad_probs - inner[..., None])).astype(jnp.bfloat16)
        grad_q = (
            grad_q
            + jnp.einsum("ktgs,ksc->ktgc", grad_scores, k_block, preferred_element_type=jnp.float32)
            * head_scale
        )
        key_part = (
            jnp.einsum("ktgs,ktgc->ksc", grad_scores, q_heads, preferred_element_type=jnp.float32)
            * head_scale
        )
        value_part = jnp.einsum(
            "ktgs,ktgc->ksc",
            probabilities.astype(jnp.bfloat16),
            g_heads,
            preferred_element_type=jnp.float32,
        )
        grad_k = lax.dynamic_update_slice_in_dim(grad_k, key_part, start, 1)
        grad_v = lax.dynamic_update_slice_in_dim(grad_v, value_part, start, 1)
        return (grad_q, grad_k, grad_v)

    zero_q = jnp.zeros(q_heads.shape, jnp.float32)
    zero_kv = jnp.zeros(k_heads.shape, jnp.float32)
    grad_q, grad_k, grad_v = lax.fori_loop(
        first_block, last_block + 1, grad_terms, (zero_q, zero_kv, zero_kv)
    )
    return (grad_q.astype(jnp.bfloat16), grad_k, grad_v)


def local(
    tokens,
    cotangent,
    routes,
    lengths,
    attn_gain,
    w_query,
    w_key,
    w_value,
    w_out,
    moe_gain,
    w_router,
    w_gate,
    w_up,
    w_down,
):
    micro_count = tokens.shape[0]
    dev_rows = tokens.shape[2]
    features = tokens.shape[3]
    top_count = routes.shape[3]
    expert_count = w_gate.shape[0]
    groups = lengths.shape[1]
    stream_len = dev_rows * lax.axis_size("shard")
    capacity = dev_rows * 3 * top_count // (2 * expert_count)
    head_scale = HEAD ** (-0.5)
    my_group = lax.axis_index("rep")
    my_place = lax.axis_index("shard")
    all_rows = micro_count * dev_rows
    f32 = jnp.float32
    bf16 = jnp.bfloat16
    stream_costs = jnp.sum(lengths * lengths, axis=2)
    orders = jnp.stack(
        [
            jnp.argsort(
                stream_costs[batch_index] if batch_index % 2 == 0 else -stream_costs[batch_index],
                stable=True,
            )
            for batch_index in range(micro_count)
        ]
    )
    source = orders[:, my_group]
    target = jnp.sum(
        jnp.where(orders == my_group, jnp.arange(groups, dtype=jnp.int32)[None, :], 0), axis=1
    )
    inputs_here, grads_here, routes_packed = select_from(
        source,
        (
            lax.all_gather(tokens, "rep", axis=1, tiled=True),
            lax.all_gather(cotangent, "rep", axis=1, tiled=True),
            lax.all_gather(routes.astype(bf16), "rep", axis=1, tiled=True),
        ),
    )
    route_here = routes_packed.astype(jnp.int32)
    my_lengths = jnp.take_along_axis(lengths, source[:, None, None], axis=1)[:, 0]
    bounds = jnp.cumsum(my_lengths, axis=1)[:, :-1]
    first_query = my_place * dev_rows
    query_places = first_query + jnp.arange(dev_rows, dtype=jnp.int32)
    key_places = jnp.arange(stream_len, dtype=jnp.int32)
    query_ids = document_ids(
        jnp.broadcast_to(query_places[None, :], (micro_count, dev_rows)), bounds
    )
    key_ids = document_ids(jnp.broadcast_to(key_places[None, :], (micro_count, stream_len)), bounds)
    doc_starts = jnp.max(jnp.where(bounds <= first_query, bounds, 0), axis=1)
    first_blocks = doc_starts // dev_rows
    gain_one, query_w, key_w, value_w, out_w, gain_two, router_w = (
        lax.all_gather(attn_gain, "shard", axis=0, tiled=True),
        lax.all_gather(w_query, "shard", axis=0, tiled=True),
        lax.all_gather(w_key, "shard", axis=0, tiled=True),
        lax.all_gather(w_value, "shard", axis=0, tiled=True),
        lax.all_gather(w_out, "shard", axis=0, tiled=True),
        lax.all_gather(moe_gain, "shard", axis=0, tiled=True),
        lax.all_gather(w_router, "shard", axis=0, tiled=True),
    )
    gate_w, up_w, down_w = (
        lax.all_gather(w_gate, "shard", axis=1, tiled=True),
        lax.all_gather(w_up, "shard", axis=1, tiled=True),
        lax.all_gather(w_down, "shard", axis=1, tiled=True),
    )
    inputs_flat = inputs_here.reshape(all_rows, features).astype(f32)
    scale_one = rms_scale(inputs_flat)
    normed = (inputs_flat * scale_one * gain_one.astype(f32)).astype(bf16)
    queries = jnp.dot(normed, query_w, preferred_element_type=f32).astype(bf16)
    key_rows = jnp.dot(normed, key_w, preferred_element_type=f32).astype(bf16)
    value_rows = jnp.dot(normed, value_w, preferred_element_type=f32).astype(bf16)
    kv_width = key_rows.shape[1]
    kv_heads = kv_width // HEAD
    group_size = queries.shape[1] // kv_width
    key_all, value_all = (
        lax.all_gather(
            key_rows.reshape(micro_count, dev_rows, kv_width), "shard", axis=1, tiled=True
        ),
        lax.all_gather(
            value_rows.reshape(micro_count, dev_rows, kv_width), "shard", axis=1, tiled=True
        ),
    )
    q_split = queries.reshape(micro_count, dev_rows, kv_heads, group_size, HEAD)
    head_queries = []
    head_keys = []
    head_values = []
    mixed_rows = []
    log_parts = []
    for batch_index in range(micro_count):
        q_heads = jnp.transpose(q_split[batch_index], (1, 0, 2, 3))
        k_heads = jnp.transpose(key_all[batch_index].reshape(stream_len, kv_heads, HEAD), (1, 0, 2))
        v_heads = jnp.transpose(
            value_all[batch_index].reshape(stream_len, kv_heads, HEAD), (1, 0, 2)
        )
        head_mix, log_totals = attend_forward(
            q_heads,
            k_heads,
            v_heads,
            query_ids[batch_index],
            query_places,
            key_ids[batch_index],
            first_blocks[batch_index],
            my_place,
            head_scale,
        )
        head_queries.append(q_heads)
        head_keys.append(k_heads)
        head_values.append(v_heads)
        log_parts.append(log_totals)
        mixed_rows.append(
            jnp.transpose(head_mix, (1, 0, 2, 3)).reshape(dev_rows, kv_heads * group_size * HEAD)
        )
    attn_rows = jnp.concatenate(mixed_rows, axis=0)
    branch = jnp.dot(attn_rows, out_w, preferred_element_type=f32)
    residual = inputs_flat + branch
    scale_two = rms_scale(residual)
    normed_two = (residual * scale_two * gain_two.astype(f32)).astype(bf16)
    logits = jnp.dot(normed_two, router_w, preferred_element_type=f32)
    route_flat = route_here.reshape(all_rows, top_count)
    route_hot = (
        route_flat[:, :, None] == jnp.arange(expert_count, dtype=jnp.int32)[None, None, :]
    ).astype(f32)
    chosen = jnp.sum(logits[:, None, :] * route_hot, axis=2)
    gate_share = jax.nn.softmax(chosen, axis=1)
    assigned = route_here.reshape(micro_count, dev_rows * top_count)
    hot_int = (
        assigned[:, :, None] == jnp.arange(expert_count, dtype=jnp.int32)[None, None, :]
    ).astype(jnp.int32)
    earlier = jnp.cumsum(hot_int, axis=1) - hot_int
    position = jnp.sum(earlier * hot_int, axis=2)
    slot_ids = (
        assigned * (micro_count * capacity)
        + jnp.arange(micro_count, dtype=jnp.int32)[:, None] * capacity
        + position
    )
    slot_flat = slot_ids.reshape(-1)
    slot_pairs = slot_ids.reshape(all_rows, top_count)
    total_slots = expert_count * micro_count * capacity
    owners = jnp.repeat(jnp.arange(all_rows, dtype=jnp.int32), top_count)
    slot_owner = jnp.zeros((total_slots,), jnp.int32).at[slot_flat].set(owners)
    filled = jnp.zeros((total_slots,), f32).at[slot_flat].set(1.0)
    slot_gate = jnp.zeros((total_slots,), f32).at[slot_flat].set(gate_share.reshape(-1))
    dispatched = (normed_two[slot_owner] * filled[:, None].astype(bf16)).reshape(
        expert_count, micro_count * capacity, features
    )
    gate_vals = jnp.einsum("ecd,edf->ecf", dispatched, gate_w, preferred_element_type=f32).astype(
        bf16
    )
    up_vals = jnp.einsum("ecd,edf->ecf", dispatched, up_w, preferred_element_type=f32).astype(bf16)
    gate_wide = gate_vals.astype(f32)
    up_wide = up_vals.astype(f32)
    squashed = jax.nn.sigmoid(gate_wide)
    hidden = (gate_wide * squashed * up_wide).astype(bf16)
    expert_out = jnp.einsum("ecf,efd->ecd", hidden, down_w, preferred_element_type=f32).reshape(
        total_slots, features
    )
    picked = expert_out[slot_pairs]
    block_rows = residual + jnp.sum(gate_share[:, :, None] * picked, axis=1)
    out_rows = block_rows.astype(bf16).reshape(micro_count, dev_rows, features)
    gain_one, query_w, key_w, value_w, out_w, gain_two, router_w = (
        lax.all_gather(attn_gain, "shard", axis=0, tiled=True),
        lax.all_gather(w_query, "shard", axis=0, tiled=True),
        lax.all_gather(w_key, "shard", axis=0, tiled=True),
        lax.all_gather(w_value, "shard", axis=0, tiled=True),
        lax.all_gather(w_out, "shard", axis=0, tiled=True),
        lax.all_gather(moe_gain, "shard", axis=0, tiled=True),
        lax.all_gather(w_router, "shard", axis=0, tiled=True),
    )
    gate_w, up_w, down_w = (
        lax.all_gather(w_gate, "shard", axis=1, tiled=True),
        lax.all_gather(w_up, "shard", axis=1, tiled=True),
        lax.all_gather(w_down, "shard", axis=1, tiled=True),
    )
    grad_rows_out = grads_here.reshape(all_rows, features).astype(f32)
    grad_gates = jnp.sum(grad_rows_out[:, None, :] * picked, axis=2)
    grad_expert = (
        (slot_gate[:, None] * grad_rows_out[slot_owner] * filled[:, None])
        .astype(bf16)
        .reshape(expert_count, micro_count * capacity, features)
    )
    grad_down_w = jnp.einsum("ecf,ecd->efd", hidden, grad_expert, preferred_element_type=f32)
    grad_hidden = jnp.einsum("ecd,efd->ecf", grad_expert, down_w, preferred_element_type=f32)
    grad_gate_v = (grad_hidden * up_wide * squashed * (1.0 + gate_wide * (1.0 - squashed))).astype(
        bf16
    )
    grad_up_v = (grad_hidden * gate_wide * squashed).astype(bf16)
    grad_gate_w = jnp.einsum("ecd,ecf->edf", dispatched, grad_gate_v, preferred_element_type=f32)
    grad_up_w = jnp.einsum("ecd,ecf->edf", dispatched, grad_up_v, preferred_element_type=f32)
    grad_dispatch = jnp.einsum(
        "ecf,edf->ecd", grad_gate_v, gate_w, preferred_element_type=f32
    ) + jnp.einsum("ecf,edf->ecd", grad_up_v, up_w, preferred_element_type=f32)
    grad_normed_two = jnp.sum(grad_dispatch.reshape(total_slots, features)[slot_pairs], axis=1)
    grad_chosen = gate_share * (
        grad_gates - jnp.sum(gate_share * grad_gates, axis=1, keepdims=True)
    )
    grad_logits = jnp.sum(grad_chosen[:, :, None] * route_hot, axis=1).astype(bf16)
    grad_router_w = jnp.dot(normed_two.T, grad_logits, preferred_element_type=f32)
    grad_normed_two = grad_normed_two + jnp.dot(grad_logits, router_w.T, preferred_element_type=f32)
    grad_residual, grad_gain_two = norm_back(
        residual, scale_two, gain_two.astype(f32), grad_normed_two
    )
    grad_residual = grad_residual + grad_rows_out
    grad_branch = grad_residual.astype(bf16)
    grad_out_w = jnp.dot(attn_rows.T, grad_branch, preferred_element_type=f32)
    grad_attn_rows = jnp.dot(grad_branch, out_w.T, preferred_element_type=f32).astype(bf16)
    grad_split = grad_attn_rows.reshape(micro_count, dev_rows, kv_heads, group_size, HEAD)
    query_grads = []
    key_parts = []
    value_parts = []
    for batch_index in range(micro_count):
        g_heads = jnp.transpose(grad_split[batch_index], (1, 0, 2, 3))
        grad_q, grad_k, grad_v = attend_back(
            head_queries[batch_index],
            head_keys[batch_index],
            head_values[batch_index],
            g_heads,
            log_parts[batch_index],
            query_ids[batch_index],
            query_places,
            key_ids[batch_index],
            first_blocks[batch_index],
            my_place,
            head_scale,
        )
        query_grads.append(
            jnp.transpose(grad_q, (1, 0, 2, 3)).reshape(dev_rows, kv_heads * group_size * HEAD)
        )
        key_parts.append(jnp.transpose(grad_k, (1, 0, 2)).reshape(stream_len, kv_width))
        value_parts.append(jnp.transpose(grad_v, (1, 0, 2)).reshape(stream_len, kv_width))
    grad_key_rows, grad_value_rows = (
        lax.psum_scatter(
            jnp.stack(key_parts).astype(jnp.bfloat16), "shard", scatter_dimension=1, tiled=True
        ).astype(jnp.float32),
        lax.psum_scatter(
            jnp.stack(value_parts).astype(jnp.bfloat16), "shard", scatter_dimension=1, tiled=True
        ).astype(jnp.float32),
    )
    grad_key_rows = grad_key_rows.astype(bf16).reshape(all_rows, kv_width)
    grad_value_rows = grad_value_rows.astype(bf16).reshape(all_rows, kv_width)
    grad_queries = jnp.concatenate(query_grads, axis=0)
    grad_query_w = jnp.dot(normed.T, grad_queries, preferred_element_type=f32)
    grad_key_w = jnp.dot(normed.T, grad_key_rows, preferred_element_type=f32)
    grad_value_w = jnp.dot(normed.T, grad_value_rows, preferred_element_type=f32)
    grad_normed = jnp.dot(grad_queries, query_w.T, preferred_element_type=f32)
    grad_normed = grad_normed + jnp.dot(grad_key_rows, key_w.T, preferred_element_type=f32)
    grad_normed = grad_normed + jnp.dot(grad_value_rows, value_w.T, preferred_element_type=f32)
    grad_inputs, grad_gain_one = norm_back(
        inputs_flat, scale_one, gain_one.astype(f32), grad_normed
    )
    grad_inputs = (
        (grad_inputs + grad_residual).astype(bf16).reshape(micro_count, dev_rows, features)
    )
    final_out, final_grad = select_from(
        target,
        (
            lax.all_gather(out_rows[:, None], "rep", axis=1, tiled=True),
            lax.all_gather(grad_inputs[:, None], "rep", axis=1, tiled=True),
        ),
    )
    attn_parts = (
        lax.psum_scatter(
            grad_gain_one.astype(jnp.bfloat16), "shard", scatter_dimension=0, tiled=True
        ).astype(jnp.float32),
        lax.psum_scatter(
            grad_query_w.astype(jnp.bfloat16), "shard", scatter_dimension=0, tiled=True
        ).astype(jnp.float32),
        lax.psum_scatter(
            grad_key_w.astype(jnp.bfloat16), "shard", scatter_dimension=0, tiled=True
        ).astype(jnp.float32),
        lax.psum_scatter(
            grad_value_w.astype(jnp.bfloat16), "shard", scatter_dimension=0, tiled=True
        ).astype(jnp.float32),
        lax.psum_scatter(
            grad_out_w.astype(jnp.bfloat16), "shard", scatter_dimension=0, tiled=True
        ).astype(jnp.float32),
        lax.psum_scatter(
            grad_gain_two.astype(jnp.bfloat16), "shard", scatter_dimension=0, tiled=True
        ).astype(jnp.float32),
        lax.psum_scatter(
            grad_router_w.astype(jnp.bfloat16), "shard", scatter_dimension=0, tiled=True
        ).astype(jnp.float32),
    )
    expert_parts = (
        lax.psum_scatter(
            grad_gate_w.astype(jnp.bfloat16), "shard", scatter_dimension=1, tiled=True
        ).astype(jnp.float32),
        lax.psum_scatter(
            grad_up_w.astype(jnp.bfloat16), "shard", scatter_dimension=1, tiled=True
        ).astype(jnp.float32),
        lax.psum_scatter(
            grad_down_w.astype(jnp.bfloat16), "shard", scatter_dimension=1, tiled=True
        ).astype(jnp.float32),
    )
    summed = (
        lax.psum(attn_parts[0].astype(jnp.bfloat16), "rep").astype(jnp.float32),
        lax.psum(attn_parts[1].astype(jnp.bfloat16), "rep").astype(jnp.float32),
        lax.psum(attn_parts[2].astype(jnp.bfloat16), "rep").astype(jnp.float32),
        lax.psum(attn_parts[3].astype(jnp.bfloat16), "rep").astype(jnp.float32),
        lax.psum(attn_parts[4].astype(jnp.bfloat16), "rep").astype(jnp.float32),
        lax.psum(attn_parts[5].astype(jnp.bfloat16), "rep").astype(jnp.float32),
        lax.psum(attn_parts[6].astype(jnp.bfloat16), "rep").astype(jnp.float32),
        lax.psum(expert_parts[0].astype(jnp.bfloat16), "rep").astype(jnp.float32),
        lax.psum(expert_parts[1].astype(jnp.bfloat16), "rep").astype(jnp.float32),
        lax.psum(expert_parts[2].astype(jnp.bfloat16), "rep").astype(jnp.float32),
    )
    return (
        final_out[:, None],
        final_grad[:, None],
        summed[0],
        summed[1],
        summed[2],
        summed[3],
        summed[4],
        summed[5],
        summed[6],
        summed[7],
        summed[8],
        summed[9],
    )


def solution(mesh):
    in_specs = (
        P(None, "rep", "shard", None),
        P(None, "rep", "shard", None),
        P(None, "rep", "shard", None),
        P(),
        P("shard"),
        P("shard", None),
        P("shard", None),
        P("shard", None),
        P("shard", None),
        P("shard"),
        P("shard", None),
        P(None, "shard", None),
        P(None, "shard", None),
        P(None, "shard", None),
    )
    out_specs = (
        P(None, "rep", "shard", None),
        P(None, "rep", "shard", None),
        P("shard"),
        P("shard", None),
        P("shard", None),
        P("shard", None),
        P("shard", None),
        P("shard"),
        P("shard", None),
        P(None, "shard", None),
        P(None, "shard", None),
        P(None, "shard", None),
    )
    return jax.shard_map(local, mesh=mesh, in_specs=in_specs, out_specs=out_specs, check_vma=False)
```

profile of v0, /device:TPU:0, one launch (start us, length us, event | category | flops | bytes accessed | tf_op | source)
XLA Modules:
  0.0 3745.5 jit_solution(2177027742137735370)
XLA Ops:
  27.1 110.9 %all-gather.38.cloned.1.call-done = bf16[2,8,512,1536]{3,2,1,0:T(8,128)(2,1)} async-done(((bf16[2,1,512,1536]{3,2,1,0:T(8,128)(2,1)}), bf16[2,8,512,1536]{3,2,1,0:T(8,128)(2,1)}) %all-gather.38.cloned.1.call-update) | async-done | bytes 25165840 | tf_op jit(solution)/shard_map/all_gather | solution.py:212
  138.0 127.3 %all-gather.16.cloned.1.call-done = bf16[2,8,512,1536]{3,2,1,0:T(8,128)(2,1)} async-done(((bf16[2,1,512,1536]{3,2,1,0:T(8,128)(2,1)}), bf16[2,8,512,1536]{3,2,1,0:T(8,128)(2,1)}) %all-gather.16.cloned.1.call-update) | async-done | bytes 25165840 | tf_op jit(solution)/shard_map/all_gather | solution.py:211
  309.2 32.2 all-gather.24.cloned.1.call-done
  474.1 38.5 %all-gather.20.cloned.1.call-done = bf16[2,2048,512]{2,1,0:T(8,128)(2,1)} async-done(((bf16[2,512,512]{2,1,0:T(8,128)(2,1)}), bf16[2,2048,512]{2,1,0:T(8,128)(2,1)}) %all-gather.20.cloned.1.call-update) | async-done | bytes 4194320 | tf_op jit(solution)/shard_map/all_gather | solution.py:252
  530.5 63.6 %all-gather.26.cloned.1.call-done = bf16[2,2048,512]{2,1,0:T(8,128)(2,1)} async-done(((bf16[2,512,512]{2,1,0:T(8,128)(2,1)}), bf16[2,2048,512]{2,1,0:T(8,128)(2,1)}) %all-gather.26.cloned.1.call-update) | async-done | bytes 4194320 | tf_op jit(solution)/shard_map/all_gather | solution.py:255
  656.6 27.0 all-gather.28.cloned.1.call-done
  723.3 178.6 %all-gather.32.cloned.1.call-done = bf16[4,1536,1024]{2,1,0:T(8,128)(2,1)} async-done(((bf16[4,384,1024]{2,1,0:T(8,128)(2,1)}), bf16[4,1536,1024]{2,1,0:T(8,128)(2,1)}) %all-gather.32.cloned.1.call-update) | async-done | bytes 12582928 | tf_op jit(solution)/shard_map/all_gather | solution.py:239
  919.8 200.0 %all-gather.30.cloned.1.call-done = bf16[4,1536,1024]{2,1,0:T(8,128)(2,1)} async-done(((bf16[4,384,1024]{2,1,0:T(8,128)(2,1)}), bf16[4,1536,1024]{2,1,0:T(8,128)(2,1)}) %all-gather.30.cloned.1.call-update) | async-done | bytes 12582928 | tf_op jit(solution)/shard_map/all_gather | solution.py:238
  1137.8 200.0 %all-gather.34.cloned.1.call-done = bf16[4,1024,1536]{2,1,0:T(8,128)(2,1)} async-done(((bf16[4,256,1536]{2,1,0:T(8,128)(2,1)}), bf16[4,1024,1536]{2,1,0:T(8,128)(2,1)}) %all-gather.34.cloned.1.call-update) | async-done | bytes 12582928 | tf_op jit(solution)/shard_map/all_gather | solution.py:240
  1395.5 31.9 multiply_reduce_fusion
  1435.7 25.8 fusion.145
  1618.3 61.0 %while.107 = (s32[]{:T(128)}, f32[8,512,3,64]{1,3,2,0:T(8,128)}, bf16[8,2048,64]{1,2,0:T(8,128)(2,1)}, bf16[8,2048,64]{1,2,0:T(8,128)(2,1)}, s32[]{:T(128)}, /*i...) while((s32[]{:T(128)}, f32[8,512,3,64]{1,3,2,0:T(8,128)}, ...), condition=%wide.region_50.51_spmd.clone, body=%wide.region_49.50_spmd.clone.sunk | while | flops 4092068864 | bytes 130482424 | solution.py:158
  1710.6 62.4 %while.105 = (s32[]{:T(128)}, f32[8,512,3,64]{1,3,2,0:T(8,128)}, bf16[8,2048,64]{1,2,0:T(8,128)(2,1)}, bf16[8,2048,64]{1,2,0:T(8,128)(2,1)}, s32[]{:T(128)}, /*i...) while((s32[]{:T(128)}, f32[8,512,3,64]{1,3,2,0:T(8,128)}, ...), condition=%wide.region_45.46_spmd.clone, body=%wide.region_44.45_spmd.clone.sunk | while | flops 4092068864 | bytes 130449656 | solution.py:158
  1816.7 467.6 %reduce-scatter.13.cloned.1.call-done = bf16[2,512,512]{2,1,0:T(8,128)(2,1)} async-done(((bf16[2,2048,512]{2,1,0:T(8,128)(2,1)}), bf16[2,512,512]{2,1,0:T(8,128)(2,1)}) %reduce-scatter.13.cloned.1.call-update) | async-done | bytes 1048592 | tf_op jit(solution)/shard_map/reduce_scatter | solution.py:407
  2288.7 75.3 %reduce-scatter.15.cloned.1.call-done = bf16[2,512,512]{2,1,0:T(8,128)(2,1)} async-done(((bf16[2,2048,512]{2,1,0:T(8,128)(2,1)}), bf16[2,512,512]{2,1,0:T(8,128)(2,1)}) %reduce-scatter.15.cloned.1.call-update) | async-done | bytes 1048592 | tf_op jit(solution)/shard_map/reduce_scatter | solution.py:410
  2452.0 88.0 %reduce-scatter.23.cloned.1.call-done = bf16[384,1536]{1,0:T(8,128)(2,1)} async-done(((bf16[1536,1536]{1,0:T(8,128)(2,1)}), bf16[384,1536]{1,0:T(8,128)(2,1)}) %reduce-scatter.23.cloned.1.call-update) | async-done | bytes 1179664 | tf_op jit(solution)/shard_map/reduce_scatter | solution.py:449
  2539.9 38.6 %reduce-scatter.19.cloned.1.call-done = bf16[384,512]{1,0:T(8,128)(2,1)} async-done(((bf16[1536,512]{1,0:T(8,128)(2,1)}), bf16[384,512]{1,0:T(8,128)(2,1)}) %reduce-scatter.19.cloned.1.call-update) | async-done | bytes 393232 | tf_op jit(solution)/shard_map/reduce_scatter | solution.py:443
  2578.5 36.4 reduce-scatter.21.cloned.1.call-done
  2614.9 213.1 %reduce-scatter.25.cloned.1.call-done = bf16[4,384,1024]{2,1,0:T(8,128)(2,1)} async-done(((bf16[4,1536,1024]{2,1,0:T(8,128)(2,1)}), bf16[4,384,1024]{2,1,0:T(8,128)(2,1)}) %reduce-scatter.25.cloned.1.call-update) | async-done | bytes 3145744 | tf_op jit(solution)/shard_map/reduce_scatter | solution.py:460
  2828.0 215.3 %reduce-scatter.27.cloned.1.call-done = bf16[4,384,1024]{2,1,0:T(8,128)(2,1)} async-done(((bf16[4,1536,1024]{2,1,0:T(8,128)(2,1)}), bf16[4,384,1024]{2,1,0:T(8,128)(2,1)}) %reduce-scatter.27.cloned.1.call-update) | async-done | bytes 3145744 | tf_op jit(solution)/shard_map/reduce_scatter | solution.py:463
  3043.3 215.1 %reduce-scatter.29.cloned.1.call-done = bf16[4,256,1536]{2,1,0:T(8,128)(2,1)} async-done(((bf16[4,1024,1536]{2,1,0:T(8,128)(2,1)}), bf16[4,256,1536]{2,1,0:T(8,128)(2,1)}) %reduce-scatter.29.cloned.1.call-update) | async-done | bytes 3145744 | tf_op jit(solution)/shard_map/reduce_scatter | solution.py:466
  3310.2 151.7 %all-reduce.7.cloned.1.call-done = (bf16[384,1536]{1,0:T(8,128)(2,1)}, bf16[384,512]{1,0:T(8,128)(2,1)}, bf16[384,512]{1,0:T(8,128)(2,1)}, bf16[384,1536]{1,0:T(...) async-done(((bf16[384,1536]{1,0:T(8,128)(2,1)}, bf16[384,512]{1,0:T(8,128)(2,1)}, ...) | async-done | bytes 12582928 | tf_op jit(solution)/shard_map/psum | solution.py:472
  3482.3 107.6 %all-gather.36.cloned.1.call-done = bf16[2,8,512,1536]{3,2,1,0:T(8,128)(2,1)} async-done(((bf16[2,1,512,1536]{3,2,1,0:T(8,128)(2,1)}), bf16[2,8,512,1536]{3,2,1,0:T(8,128)(2,1)}) %all-gather.36.cloned.1.call-update) | async-done | bytes 25165840 | tf_op jit(solution)/shard_map/all_gather | solution.py:432
  3589.8 127.7 %all-gather.40.cloned.1.call-done = bf16[2,8,512,1536]{3,2,1,0:T(8,128)(2,1)} async-done(((bf16[2,1,512,1536]{3,2,1,0:T(8,128)(2,1)}), bf16[2,8,512,1536]{3,2,1,0:T(8,128)(2,1)}) %all-gather.40.cloned.1.call-update) | async-done | bytes 25165840 | tf_op jit(solution)/shard_map/all_gather | solution.py:433
  (456 shorter events, 1042.6 us)
Async XLA Ops:
  7.2 130.8 %all-gather.38.cloned.1.call-start = ((), (), s32[]{:S(2)}) async-start(), calls=%async_computation.21 | async-start | bytes 28311552 | tf_op jit(solution)/shard_map/all_gather | solution.py:212
  7.9 257.3 %all-gather.16.cloned.1.call-start = ((), (), s32[]{:S(2)}) async-start(), calls=%async_computation.10 | async-start | bytes 28311552 | tf_op jit(solution)/shard_map/all_gather | solution.py:211
  8.7 295.3 %all-gather.18.cloned.1.call-start = ((), (), s32[]{:S(2)}) async-start(), calls=%async_computation.11 | async-start | bytes 1966080 | tf_op jit(solution)/shard_map/all_gather | solution.py:231
  9.4 332.0 %all-gather.24.cloned.1.call-start = ((), (), s32[]{:S(2)}) async-start(), calls=%async_computation.14 | async-start | bytes 1966080 | tf_op jit(solution)/shard_map/all_gather | solution.py:232
  10.0 421.3 %all-gather.22.cloned.1.call-start = ((), (), s32[]{:S(2)}) async-start(), calls=%async_computation.13 | async-start | bytes 5898240 | tf_op jit(solution)/shard_map/all_gather | solution.py:230
  10.6 502.0 %all-gather.20.cloned.1.call-start = ((), (), s32[]{:S(2)}) async-start(), calls=%async_computation.12 | async-start | bytes 5242880 | tf_op jit(solution)/shard_map/all_gather | solution.py:252
  309.1 285.0 %all-gather.26.cloned.1.call-start = ((), (), s32[]{:S(2)}) async-start(), calls=%async_computation.15 | async-start | bytes 5242880 | tf_op jit(solution)/shard_map/all_gather | solution.py:255
  346.5 337.1 %all-gather.28.cloned.1.call-start = ((), (), s32[]{:S(2)}) async-start(), calls=%async_computation.16 | async-start | bytes 5898240 | tf_op jit(solution)/shard_map/all_gather | solution.py:233
  347.3 554.6 %all-gather.32.cloned.1.call-start = ((), (), s32[]{:S(2)}) async-start(), calls=%async_computation.18 | async-start | bytes 15728640 | tf_op jit(solution)/shard_map/all_gather | solution.py:239
  348.0 771.7 %all-gather.30.cloned.1.call-start = ((), (), s32[]{:S(2)}) async-start(), calls=%async_computation.17 | async-start | bytes 15728640 | tf_op jit(solution)/shard_map/all_gather | solution.py:238
  348.6 989.1 %all-gather.34.cloned.1.call-start = ((), (), s32[]{:S(2)}) async-start(), calls=%async_computation.19 | async-start | bytes 15728640 | tf_op jit(solution)/shard_map/all_gather | solution.py:240
  349.4 1935.0 %reduce-scatter.13.cloned.1.call-start = ((), (), s32[]{:S(2)}) async-start(), calls=%async_computation.22 | async-start | bytes 5242880 | tf_op jit(solution)/shard_map/reduce_scatter | solution.py:407
  1783.8 580.2 %reduce-scatter.15.cloned.1.call-start = ((), (), s32[]{:S(2)}) async-start(), calls=%async_computation.23 | async-start | bytes 5242880 | tf_op jit(solution)/shard_map/reduce_scatter | solution.py:410
  1795.3 656.7 %reduce-scatter.17.cloned.1.call-start = ((), (), s32[]{:S(2)}) async-start(), calls=%async_computation.25 | async-start | bytes 5898240 | tf_op jit(solution)/shard_map/reduce_scatter | solution.py:440
  1806.9 733.1 %reduce-scatter.23.cloned.1.call-start = ((), (), s32[]{:S(2)}) async-start(), calls=%async_computation.28 | async-start | bytes 5898240 | tf_op jit(solution)/shard_map/reduce_scatter | solution.py:449
  1816.7 761.8 %reduce-scatter.19.cloned.1.call-start = ((), (), s32[]{:S(2)}) async-start(), calls=%async_computation.26 | async-start | bytes 1966080 | tf_op jit(solution)/shard_map/reduce_scatter | solution.py:443
  2288.7 326.3 %reduce-scatter.21.cloned.1.call-start = ((), (), s32[]{:S(2)}) async-start(), calls=%async_computation.27 | async-start | bytes 1966080 | tf_op jit(solution)/shard_map/reduce_scatter | solution.py:446
  2368.5 459.5 %reduce-scatter.25.cloned.1.call-start = ((), (), s32[]{:S(2)}) async-start(), calls=%async_computation.29 | async-start | bytes 15728640 | tf_op jit(solution)/shard_map/reduce_scatter | solution.py:460
  2386.5 656.8 %reduce-scatter.27.cloned.1.call-start = ((), (), s32[]{:S(2)}) async-start(), calls=%async_computation.30 | async-start | bytes 15728640 | tf_op jit(solution)/shard_map/reduce_scatter | solution.py:463
  2404.8 853.6 %reduce-scatter.29.cloned.1.call-start = ((), (), s32[]{:S(2)}) async-start(), calls=%async_computation.31 | async-start | bytes 15728640 | tf_op jit(solution)/shard_map/reduce_scatter | solution.py:466
  2428.5 854.4 %reduce-scatter.31.cloned.1.call-start = ((), (), s32[]{:S(2)}) async-start(), calls=%async_computation.32 | async-start | bytes 491520
  2431.9 1029.9 %all-reduce.7.cloned.1.call-start = ((), (), s32[]{:S(2)}) async-start(), calls=%async_computation.33 | async-start | bytes 25165824 | tf_op jit(solution)/shard_map/psum | solution.py:472
  3258.5 331.3 %all-gather.36.cloned.1.call-start = ((), (), s32[]{:S(2)}) async-start(), calls=%async_computation.20 | async-start | bytes 28311552 | tf_op jit(solution)/shard_map/all_gather | solution.py:432
  3259.2 458.3 %all-gather.40.cloned.1.call-start = ((), (), s32[]{:S(2)}) async-start(), calls=%async_computation.24 | async-start | bytes 28311552 | tf_op jit(solution)/shard_map/all_gather | solution.py:433
  (78 other events, 3964.6 us)
Sparse Core Ops, SparseCore 0:
  9.9 128.0 all-gather.37
  139.9 125.3 all-gather.15
  266.8 37.0 all-gather.17
  305.4 35.9 all-gather.23
  342.8 88.4 all-gather.21
  433.3 79.2 all-gather.19
  514.7 79.2 all-gather.25
  595.6 87.9 all-gather.27
  685.2 216.6 all-gather.31
  903.3 216.3 all-gather.29
  1121.3 216.3 all-gather.33
  1783.9 500.3 reduce-scatter.12
  2286.7 77.2 reduce-scatter.14
  2366.2 85.7 reduce-scatter.16
  2454.1 85.7 reduce-scatter.22
  2542.7 35.7 reduce-scatter.18
  2580.6 34.2 reduce-scatter.20
  2617.1 210.8 reduce-scatter.24
  2830.4 212.8 reduce-scatter.26
  3045.5 212.8 reduce-scatter.28
  3261.3 21.6 reduce-scatter.30
  3288.5 173.3 all-reduce.6
  3464.3 125.4 all-gather.35
  3592.1 125.3 all-gather.39
where the time goes:
time: 3760 us; the launch traced here: 3750 us
  waiting for transfers between devices  2770 us (74%)
  matrix products  472 us (13%)
  local copies, waits for them, and re-layouts  231 us (6%)
  other arithmetic  171 us (5%)
  blocking collectives  72.6 us (2%)
    reduce_scatter x1, waiting for transfers between devices, local(): lax.psum_scatter(jnp.stack(key_parts).astype(jnp.bfloat16), 'shard', scat...  468 us
    reduce_scatter x1, waiting for transfers between devices, local(): lax.psum_scatter(grad_up_w.astype(jnp.bfloat16), 'shard', scatter_dimensi...  215 us
    reduce_scatter x1, waiting for transfers between devices, local(): lax.psum_scatter(grad_down_w.astype(jnp.bfloat16), 'shard', scatter_dimen...  215 us
    reduce_scatter x1, waiting for transfers between devices, local(): lax.psum_scatter(grad_gate_w.astype(jnp.bfloat16), 'shard', scatter_dimen...  213 us
    all_gather x1, waiting for transfers between devices, local(): lax.all_gather(w_down, 'shard', axis=1, tiled=True)  200 us
    all_gather x1, waiting for transfers between devices, local(): lax.all_gather(w_gate, 'shard', axis=1, tiled=True)  200 us
    all_gather x1, waiting for transfers between devices, local(): lax.all_gather(w_up, 'shard', axis=1, tiled=True)  179 us
    psum x1, waiting for transfers between devices, local(): lax.psum(attn_parts[1].astype(jnp.bfloat16), 'rep').astype(jnp.float32)  152 us
  transfers between devices with their start and end apart: 24, of which 24 were waited for; matrix products, arithmetic and copies ran while one was open for 11% of the time, Pallas kernels for 0%

commit v1 on v0

v1 whole, which is shorter than its diff:
```python
import functools
import math

import jax
import jax.numpy as jnp
from jax import lax
from jax.experimental import pallas as pl
from jax.experimental.pallas import tpu as pltpu
from jax.sharding import PartitionSpec as P

HEAD = 64
EPSILON = 1e-05
NEGATIVE = -1e30
F32 = jnp.float32
BF16 = jnp.bfloat16
LOG2_SCALE = HEAD ** (-0.5) * math.log2(math.e)
SCALE = HEAD ** (-0.5)
BOTH = ("rep", "shard")


def dot(left, right, left_dim, right_dim, kind=F32):
    return lax.dot_general(
        left, right, (((left_dim,), (right_dim,)), ((), ())), preferred_element_type=F32
    ).astype(kind)


def block_counts(length):
    return min(512, length), min(256, length)


def visible_mask(index, width, first_key, first_query, starts):
    rows = first_key + lax.broadcasted_iota(jnp.int32, (width, starts.shape[1]), 0)
    columns = first_query + lax.broadcasted_iota(jnp.int32, (1, starts.shape[1]), 1)
    return (rows >= starts) & (rows <= columns)


def side_by_side(block, group):
    return jnp.concatenate([block[g * HEAD : (g + 1) * HEAD, :] for g in range(group)], axis=1)


def three_loops(ranges, place, step, carry):
    low, full_low, full_high, high = (ranges[place, n] for n in range(4))
    carry = lax.fori_loop(low, full_low, functools.partial(step, True), carry)
    carry = lax.fori_loop(full_low, full_high, functools.partial(step, False), carry)
    return lax.fori_loop(full_high, high, functools.partial(step, True), carry)


def forward_kernel(ranges, q_ref, k_ref, v_ref, starts_ref, o_ref, stat_ref, k_rows, *, group, wide):
    place = pl.program_id(1)
    q_width = q_ref.shape[1]

    @pl.when(place == 0)
    def _():
        k_rows[...] = k_ref[...].T

    queries = side_by_side(q_ref[...], group)
    starts = starts_ref[...]

    def step(masked, index, carry):
        high, total, mixed = carry
        first = pl.multiple_of(index * wide, wide)
        scores = (
            jnp.dot(k_rows[pl.ds(first, wide), :], queries, preferred_element_type=F32)
            * LOG2_SCALE
        )
        if masked:
            seen = visible_mask(index, wide, first, place * q_width, starts)
            scores = jnp.where(jnp.concatenate([seen] * group, axis=1), scores, NEGATIVE)
        new_high = jnp.maximum(high, jnp.max(scores, axis=0, keepdims=True))
        weights = jnp.exp2(scores - new_high)
        fade = jnp.exp2(high - new_high)
        total = total * fade + jnp.sum(weights, axis=0, keepdims=True)
        mixed = mixed * fade + jnp.dot(
            v_ref[:, pl.ds(first, wide)], weights.astype(BF16), preferred_element_type=F32
        )
        return new_high, total, mixed

    columns = group * q_width
    high, total, mixed = three_loops(
        ranges,
        place,
        step,
        (
            jnp.full((1, columns), NEGATIVE, F32),
            jnp.zeros((1, columns), F32),
            jnp.zeros((HEAD, columns), F32),
        ),
    )
    mixed = (mixed / total).astype(BF16)
    stat = high + jnp.log2(total)
    for g in range(group):
        span = slice(g * q_width, (g + 1) * q_width)
        o_ref[g * HEAD : (g + 1) * HEAD, :] = mixed[:, span]
        stat_ref[0, g : g + 1, :] = stat[:, span]


def backward_kernel(
    ranges, q_ref, k_ref, v_ref, o_ref, g_ref, stat_ref, starts_ref,
    dq_ref, dk_ref, dv_ref, k_rows, v_rows, dk_sum, dv_sum, *, group, wide,
):
    place = pl.program_id(1)
    q_width = q_ref.shape[1]

    @pl.when(place == 0)
    def _():
        k_rows[...] = k_ref[...].T
        v_rows[...] = v_ref[...].T
        dk_sum[...] = jnp.zeros_like(dk_sum)
        dv_sum[...] = jnp.zeros_like(dv_sum)

    queries = side_by_side(q_ref[...], group)
    grads = side_by_side(g_ref[...], group)
    outs = side_by_side(o_ref[...], group)
    inner = jnp.sum(grads.astype(F32) * outs.astype(F32), axis=0, keepdims=True)
    stat = jnp.concatenate([stat_ref[0, g : g + 1, :] for g in range(group)], axis=1)
    starts = starts_ref[...]

    def step(masked, index, dq):
        first = pl.multiple_of(index * wide, wide)
        span = pl.ds(first, wide)
        scores = jnp.dot(k_rows[span, :], queries, preferred_element_type=F32) * LOG2_SCALE
        chances = jnp.exp2(scores - stat)
        if masked:
            seen = visible_mask(index, wide, first, place * q_width, starts)
            chances = jnp.where(jnp.concatenate([seen] * group, axis=1), chances, 0.0)
        slopes = jnp.dot(v_rows[span, :], grads, preferred_element_type=F32)
        pull = (chances * (slopes - inner)).astype(BF16)
        dv_sum[:, span] += dot(grads, chances.astype(BF16), 1, 1)
        dk_sum[:, span] += dot(queries, pull, 1, 1)
        return dq + jnp.dot(k_ref[:, span], pull, preferred_element_type=F32)

    dq = three_loops(ranges, place, step, jnp.zeros((HEAD, group * q_width), F32))
    dq = (dq * SCALE).astype(BF16)
    for g in range(group):
        dq_ref[g * HEAD : (g + 1) * HEAD, :] = dq[:, g * q_width : (g + 1) * q_width]

    @pl.when(place == pl.num_programs(1) - 1)
    def _():
        dk_ref[...] = (dk_sum[...] * SCALE).astype(BF16)
        dv_ref[...] = dv_sum[...].astype(BF16)


def block_ranges(starts, q_width, wide):
    length = starts.shape[1]
    count = length // q_width
    first_query = jnp.arange(count, dtype=jnp.int32) * q_width
    low = starts[0, ::q_width] // wide
    full_low = (starts[0, q_width - 1 :: q_width] + wide - 1) // wide
    full_high = (first_query + 1) // wide
    full_high = first_query // wide
    high = (first_query + q_width) // wide
    full_low = jnp.clip(full_low, low, jnp.maximum(full_high, low))
    full_high = jnp.maximum(full_high, full_low)
    return jnp.stack([low, full_low, full_high, high], axis=1)


def attention_specs(heads, group, length, q_width):
    per_query = pl.BlockSpec((group * HEAD, q_width), lambda h, i, r: (h, i))
    per_head = pl.BlockSpec((HEAD, length), lambda h, i, r: (h, 0))
    stat = pl.BlockSpec((1, group, q_width), lambda h, i, r: (h, 0, i))
    starts = pl.BlockSpec((1, q_width), lambda h, i, r: (0, i))
    return per_query, per_head, stat, starts


def attend_forward(q_t, k_t, v_t, starts):
    length = q_t.shape[1]
    heads = k_t.shape[0] // HEAD
    group = q_t.shape[0] // k_t.shape[0]
    q_width, wide = block_counts(length)
    per_query, per_head, stat, start_spec = attention_specs(heads, group, length, q_width)
    pairs = heads * group * length * length // 2
    return pl.pallas_call(
        functools.partial(forward_kernel, group=group, wide=wide),
        out_shape=(
            jax.ShapeDtypeStruct(q_t.shape, BF16),
            jax.ShapeDtypeStruct((heads, group, length), F32),
        ),
        grid_spec=pltpu.PrefetchScalarGridSpec(
            num_scalar_prefetch=1,
            grid=(heads, length // q_width),
            in_specs=[per_query, per_head, per_head, start_spec],
            out_specs=(per_query, stat),
            scratch_shapes=[pltpu.VMEM((length, HEAD), BF16)],
        ),
        compiler_params=pltpu.CompilerParams(
            dimension_semantics=("arbitrary", "arbitrary"), vmem_limit_bytes=48 << 20
        ),
        cost_estimate=pl.CostEstimate(
            flops=pairs * HEAD * 4 * 4, transcendentals=pairs, bytes_accessed=q_t.size * 8
        ),
        name="attend_forward",
    )(block_ranges(starts, q_width, wide), q_t, k_t, v_t, starts)


def attend_backward(q_t, k_t, v_t, o_t, g_t, stat_rows, starts):
    length = q_t.shape[1]
    heads = k_t.shape[0] // HEAD
    group = q_t.shape[0] // k_t.shape[0]
    q_width, wide = block_counts(length)
    per_query, per_head, stat, start_spec = attention_specs(heads, group, length, q_width)
    pairs = heads * group * length * length // 2
    return pl.pallas_call(
        functools.partial(backward_kernel, group=group, wide=wide),
        out_shape=(
            jax.ShapeDtypeStruct(q_t.shape, BF16),
            jax.ShapeDtypeStruct(k_t.shape, BF16),
            jax.ShapeDtypeStruct(k_t.shape, BF16),
        ),
        grid_spec=pltpu.PrefetchScalarGridSpec(
            num_scalar_prefetch=1,
            grid=(heads, length // q_width),
            in_specs=[per_query, per_head, per_head, per_query, per_query, stat, start_spec],
            out_specs=(per_query, per_head, per_head),
            scratch_shapes=[
                pltpu.VMEM((length, HEAD), BF16),
                pltpu.VMEM((length, HEAD), BF16),
                pltpu.VMEM((HEAD, length), F32),
                pltpu.VMEM((HEAD, length), F32),
            ],
        ),
        compiler_params=pltpu.CompilerParams(
            dimension_semantics=("arbitrary", "arbitrary"), vmem_limit_bytes=48 << 20
        ),
        cost_estimate=pl.CostEstimate(
            flops=pairs * HEAD * 10 * 4, transcendentals=pairs, bytes_accessed=q_t.size * 16
        ),
        name="attend_backward",
    )(block_ranges(starts, q_width, wide), q_t, k_t, v_t, o_t, g_t, stat_rows, starts)


class Place:
    def __init__(self):
        self.reps = lax.axis_size("rep")
        self.shards = lax.axis_size("shard")
        self.quarters = self.reps // 2
        self.chips = self.shards // 4
        rep = lax.axis_index("rep")
        self.core = rep % 2
        self.quarter = rep // 2
        self.shard = lax.axis_index("shard")
        self.stream = self.shard // self.chips
        self.batch = self.stream // 2
        self.source = self.quarter * 2 + self.stream % 2
        self.chip = self.shard % self.chips

    def across(self, array, bit):
        return lax.ppermute(array, "rep", [(i, i ^ bit) for i in range(self.reps)])

    def swap(self, array):
        return self.across(array, 1)

    def moves(self, turn, home):
        pairs = []
        for quarter in range(self.quarters):
            for core in range(2):
                for shard in range(self.shards):
                    batch = turn ^ (shard & 1)
                    member = shard // 2
                    stream = 2 * batch + core
                    start = (quarter * 2 + core) * self.shards + shard
                    end = (
                        (quarter * 2 + member % 2) * self.shards
                        + stream * self.chips
                        + member // 2
                    )
                    pairs.append((end, start) if home else (start, end))
        return pairs

    def to_streams(self, array):
        odd = self.shard % 2 == 1
        got = [
            lax.ppermute(
                jnp.where(odd, array[1 - turn], array[turn]), BOTH, self.moves(turn, False)
            )
            for turn in range(2)
        ]
        swapped = self.batch == 1
        return jnp.concatenate(
            [jnp.where(swapped, got[1], got[0]), jnp.where(swapped, got[0], got[1])], axis=0
        )

    def to_homes(self, array):
        half = array.shape[0] // 2
        swapped = self.batch == 1
        parts = [array[:half], array[half:]]
        got = [
            lax.ppermute(
                jnp.where(swapped, parts[1 - turn], parts[turn]), BOTH, self.moves(turn, True)
            )
            for turn in range(2)
        ]
        odd = self.shard % 2 == 1
        return jnp.stack([jnp.where(odd, got[1], got[0]), jnp.where(odd, got[0], got[1])])

    def ordered(self, mine, other, axis):
        return jnp.where(
            self.core == 0,
            jnp.concatenate([mine, other], axis=axis),
            jnp.concatenate([other, mine], axis=axis),
        )

    def halves(self, array, axis):
        size = array.shape[axis] // 2
        mine = lax.dynamic_slice_in_dim(array, self.core * size, size, axis)
        other = lax.dynamic_slice_in_dim(array, (1 - self.core) * size, size, axis)
        return mine, other

    def chip_exchange(self, array, split, join):
        if self.chips == 1:
            return array
        size = array.shape[split] // self.chips
        width = array.shape[join]
        shape = list(array.shape)
        shape[split] = size
        shape[join] = width * self.chips
        result = jnp.zeros(shape, array.dtype)
        for step in range(self.chips):
            other = self.chip ^ step
            piece = lax.dynamic_slice_in_dim(array, other * size, size, split)
            if step:
                piece = lax.ppermute(
                    piece, "shard", [(i, i ^ step) for i in range(self.shards)]
                )
            result = lax.dynamic_update_slice_in_dim(result, piece, other * width, join)
        return result

    def fetch(self, own, bits):
        piece = lax.dynamic_index_in_dim(own, self.quarter, 1, keepdims=False)
        count = self.shards
        ups, downs = [], []
        up = down = piece
        for step in range(1, count):
            up = lax.ppermute(up, "shard", [(i, i + 1) for i in range(step - 1, count - 1)])
            down = lax.ppermute(down, "shard", [(i, i - 1) for i in range(1, count - step + 1)])
            ups.append(up)
            downs.append(down)
        along = jnp.stack(
            [
                jnp.where(self.shard >= step, ups[step - 1], downs[count - step - 1])
                for step in range(1, count)
            ]
        )
        found = {0: along}
        for bit in bits:
            found.update(
                {key ^ bit: self.across(array, 2 * bit) for key, array in list(found.items())}
            )
        return [found[key] for key in range(self.quarters)]

    def assemble(self, own, found, swapped=None):
        parts, quarters, rows, columns = own.shape
        shards = self.shards
        sides = 1 if swapped is None else 2
        places = jnp.stack([self.shard, self.quarter, self.core]).astype(jnp.int32)

        def kernel(places_ref, *refs):
            out_ref, sem = refs[-2], refs[-1]
            shard, quarter, core = places_ref[0], places_ref[1], places_ref[2]
            copies = []
            for side in range(sides):
                own_ref = refs[side * (quarters + 1)]
                found_refs = refs[side * (quarters + 1) + 1 : (side + 1) * (quarters + 1)]
                if sides == 1:
                    span = slice(None)
                else:
                    at = core if side == 0 else 1 - core
                    span = pl.ds(pl.multiple_of(at * columns, 128), columns)
                for part in range(parts):
                    copies.append((own_ref.at[part], out_ref.at[part, shard, :, :, span]))
                    for key in range(quarters):
                        for step in range(1, shards):
                            end = out_ref.at[
                                part, (shard - step + shards) % shards, quarter ^ key, :, span
                            ]
                            copies.append((found_refs[key].at[step - 1, part], end))
            copies = [
                pltpu.make_async_copy(source, end, sem.at[n])
                for n, (source, end) in enumerate(copies)
            ]
            for copy in copies:
                copy.start()
            for copy in copies:
                copy.wait()

        operands = [own, *found]
        if swapped is not None:
            operands += [swapped[0], *swapped[1]]
        shape = (parts, shards, quarters, rows, sides * columns)
        total = parts * shards * quarters * rows * sides * columns
        return pl.pallas_call(
            kernel,
            out_shape=jax.ShapeDtypeStruct(shape, own.dtype),
            in_specs=[pl.BlockSpec(memory_space=pltpu.SMEM)]
            + [pl.BlockSpec(memory_space=pl.ANY)] * len(operands),
            out_specs=pl.BlockSpec(memory_space=pltpu.VMEM),
            scratch_shapes=[
                pltpu.SemaphoreType.DMA((sides * parts * (1 + quarters * (shards - 1)),))
            ],
            compiler_params=pltpu.CompilerParams(vmem_limit_bytes=24 << 20),
            cost_estimate=pl.CostEstimate(flops=0, transcendentals=0, bytes_accessed=total * 4),
            name="assemble",
        )(places, *operands)

    def reduce(self, grad, bits):
        parts, shards, quarters, rows, columns = grad.shape
        held = grad
        kept_bits = list(range(quarters.bit_length() - 1))
        shape = [2] * len(kept_bits)
        held = held.reshape(parts, shards, *shape, rows, columns)
        order = kept_bits[::-1]
        for bit in bits:
            number = bit.bit_length() - 1
            axis = 2 + order.index(number)
            mine = (self.quarter >> number) & 1
            keep = lax.dynamic_index_in_dim(held, mine, axis, keepdims=False)
            give = lax.dynamic_index_in_dim(held, 1 - mine, axis, keepdims=False)
            got = self.across(give.astype(BF16), 2 * bit)
            held = (keep.astype(F32) + got.astype(F32)).astype(BF16)
            order.remove(number)
        up = down = None
        for step in range(1, shards):
            index = jnp.minimum(self.shard + shards - step, shards - 1)
            send = lax.dynamic_index_in_dim(held, index, 1, keepdims=False)
            if up is not None:
                send = (send.astype(F32) + up.astype(F32)).astype(BF16)
            up = lax.ppermute(send, "shard", [(i, i + 1) for i in range(step)])
            index = jnp.maximum(self.shard - shards + step, 0)
            send = lax.dynamic_index_in_dim(held, index, 1, keepdims=False)
            if down is not None:
                send = (send.astype(F32) + down.astype(F32)).astype(BF16)
            down = lax.ppermute(
                send, "shard", [(i, i - 1) for i in range(shards - step, shards)]
            )
        own = lax.dynamic_index_in_dim(held, self.shard, 1, keepdims=False)
        total = (own.astype(F32) + up.astype(F32) + down.astype(F32)).astype(BF16)
        whole = lax.all_gather(total, "rep", axis=0, tiled=False)
        return whole.reshape(quarters, 2, parts, rows, columns)


def rms_scale(rows_in):
    return lax.rsqrt(jnp.mean(rows_in * rows_in, axis=-1, keepdims=True) + EPSILON)


def norm_back(rows_in, row_scale, gain_row, grad_normed):
    grad_gain = jnp.sum(grad_normed * rows_in * row_scale, axis=0)
    scaled = grad_normed * gain_row
    scale_cubed = row_scale * row_scale * row_scale
    grad_rows = row_scale * scaled - rows_in * scale_cubed * jnp.mean(
        scaled * rows_in, axis=-1, keepdims=True
    )
    return (grad_rows, grad_gain)


def local(
    tokens,
    cotangent,
    routes,
    lengths,
    attn_gain,
    w_query,
    w_key,
    w_value,
    w_out,
    moe_gain,
    w_router,
    w_gate,
    w_up,
    w_down,
):
    here = Place()
    core, shards, quarters = here.core, here.shards, here.quarters
    experts = w_gate.shape[0]
    features = tokens.shape[3]
    hidden_all = w_gate.shape[2]
    width_q = w_query.shape[1] // 2
    width_k = w_key.shape[1] // 2
    shard_rows = w_query.shape[0]
    rows_q = shard_rows // quarters
    hidden_part = hidden_all // shards // 2
    hidden_core = hidden_all // 2
    down_rows = hidden_part // quarters
    bit_list = [1 << n for n in range(quarters.bit_length() - 1)]
    bit_back = bit_list[::-1]

    x_own = here.to_streams(tokens[:, 0])
    rows = x_own.shape[0]

    def columns_of(weight, width):
        return lax.dynamic_slice_in_dim(weight, core * width, width, 1)

    def split(weight):
        return weight.reshape(1, quarters, rows_q, weight.shape[1])

    small = jnp.concatenate(
        [attn_gain[:, None], moe_gain[:, None], w_router], axis=1
    )
    small = jnp.pad(small, ((0, 0), (0, 128 - small.shape[1])))
    own_q = split(columns_of(w_query, width_q))
    own_kv = split(
        jnp.concatenate([columns_of(w_key, width_k), columns_of(w_value, width_k), small], axis=1)
    )
    own_out = split(columns_of(w_out, features // 2))

    def expert_columns(weight):
        parts = weight.reshape(experts, shard_rows, shards, 2, hidden_part)
        parts = lax.dynamic_index_in_dim(parts, core, 3, keepdims=False)
        return split(jnp.transpose(parts, (1, 0, 2, 3)).reshape(shard_rows, experts * hidden_core))

    own_gate = expert_columns(w_gate)
    own_up = expert_columns(w_up)
    own_down = lax.dynamic_slice_in_dim(w_down, core * hidden_part, hidden_part, 1).reshape(
        experts, quarters, down_rows, features
    )

    kv_w = here.assemble(own_kv, here.fetch(own_kv, bit_back)).reshape(features, -1)
    q_w = here.assemble(own_q, here.fetch(own_q, bit_list)).reshape(features, width_q)
    found_out = here.fetch(own_out, bit_back)
    out_w = here.assemble(
        own_out, found_out, (here.swap(own_out), [here.swap(part) for part in found_out])
    ).reshape(features, features)
    gate_w = here.assemble(own_gate, here.fetch(own_gate, bit_list)).reshape(features, -1)
    up_w = here.assemble(own_up, here.fetch(own_up, bit_back)).reshape(features, -1)
    down_w = here.assemble(own_down, here.fetch(own_down, bit_list)).reshape(-1, features)

    smalls = kv_w[:, 2 * width_k : 2 * width_k + 2 + experts].astype(F32)
    gain_one = smalls[:, 0][None, :]
    gain_two = smalls[:, 1][None, :]
    router_w = kv_w[:, 2 * width_k + 2 : 2 * width_k + 2 + experts]
    kv_w = kv_w[:, : 2 * width_k]

    x_wide = x_own.astype(F32)
    scale_one = rms_scale(x_wide)
    normed_own = (x_wide * scale_one * gain_one).astype(BF16)
    normed = here.ordered(normed_own, here.swap(normed_own), 0)
    q_t = dot(q_w, normed, 0, 1, BF16)
    kv_t = dot(kv_w, normed, 0, 1, BF16)
    k_t, v_t = kv_t[:width_k], kv_t[width_k:]
    q_t, k_t, v_t = (here.chip_exchange(part, 0, 1) for part in (q_t, k_t, v_t))
    length = q_t.shape[1]

    my_lengths = lax.dynamic_index_in_dim(
        lax.dynamic_index_in_dim(lengths, here.batch, 0, keepdims=False),
        here.source,
        0,
        keepdims=False,
    )
    ends = jnp.cumsum(my_lengths)[:-1]
    positions = jnp.arange(length, dtype=jnp.int32)
    starts = jnp.max(
        jnp.where(ends[:, None] <= positions[None, :], ends[:, None], 0), axis=0, keepdims=True
    ).astype(jnp.int32)
    o_t, stat = attend_forward(q_t, k_t, v_t, starts)
    o_back = here.chip_exchange(o_t, 1, 0)
    o_mine, o_other = here.halves(o_back, 1)
    o_own = here.ordered(o_mine, here.swap(o_other), 0)
    h_own = x_wide + dot(o_own, out_w, 0, 0)

    scale_two = rms_scale(h_own)
    b_own = (h_own * scale_two * gain_two).astype(BF16)
    b_all = jnp.concatenate([b_own, here.swap(b_own)], axis=0)
    route_own = here.to_streams(routes[:, 0])
    route_all = jnp.concatenate([route_own, here.swap(route_own)], axis=0)
    dy_own = here.to_streams(cotangent[:, 0])
    dy_all = jnp.concatenate([dy_own, here.swap(dy_own)], axis=0)

    logits = dot(b_all, router_w, 1, 0)
    route_hot = (
        route_all[:, :, None] == jnp.arange(experts, dtype=jnp.int32)[None, None, :]
    ).astype(F32)
    chosen = jnp.sum(logits[:, None, :] * route_hot, axis=2)
    gate_share = jax.nn.softmax(chosen, axis=1)
    shares = jnp.sum(gate_share[:, :, None] * route_hot, axis=1)
    share_wide = jnp.repeat(shares, hidden_core, axis=1)

    gate_v = dot(b_all, gate_w, 1, 0, BF16)
    up_v = dot(b_all, up_w, 1, 0, BF16)
    gate_f, up_f = gate_v.astype(F32), up_v.astype(F32)
    squashed = jax.nn.sigmoid(gate_f)
    mid = (gate_f * squashed * up_f * share_wide).astype(BF16)
    y_other = dot(mid[rows:], down_w, 1, 0, BF16)
    y_got = here.swap(y_other)
    y_own = dot(mid[:rows], down_w, 1, 0)
    block_own = (h_own + y_own + y_got.astype(F32)).astype(BF16)
    block_out = here.to_homes(block_own)

    slope = dot(dy_all, down_w, 1, 1)
    grad_down = dot(mid, dy_all, 0, 0, BF16)
    active = gate_f * squashed
    grad_share = jnp.sum((slope * active * up_f).reshape(2 * rows, experts, hidden_core), axis=2)
    scaled = slope * share_wide
    grad_gate_v = (scaled * up_f * squashed * (1.0 + gate_f * (1.0 - squashed))).astype(BF16)
    grad_up_v = (scaled * active).astype(BF16)
    share_got = here.swap(grad_share[rows:])
    grad_share = grad_share[:rows] + share_got
    db_other = (
        dot(grad_gate_v[rows:], gate_w, 1, 1) + dot(grad_up_v[rows:], up_w, 1, 1)
    ).astype(BF16)
    db_got = here.swap(db_other)
    db_own = dot(grad_gate_v[:rows], gate_w, 1, 1) + dot(grad_up_v[:rows], up_w, 1, 1)
    grad_gate = dot(b_all, grad_gate_v, 0, 0, BF16)
    grad_up = dot(b_all, grad_up_v, 0, 0, BF16)

    hot_own, share_own = route_hot[:rows], gate_share[:rows]
    grad_gates = jnp.sum(grad_share[:, None, :] * hot_own, axis=2)
    grad_chosen = share_own * (
        grad_gates - jnp.sum(share_own * grad_gates, axis=1, keepdims=True)
    )
    grad_logits = jnp.sum(grad_chosen[:, :, None] * hot_own, axis=1).astype(BF16)
    grad_router = dot(b_own, grad_logits, 0, 0)
    db = db_own + db_got.astype(F32) + dot(grad_logits, router_w, 1, 1)
    dh, grad_gain_two = norm_back(h_own, scale_two, gain_two, db)
    dh = dh + dy_own.astype(F32)
    dattn = dh.astype(BF16)

    do_t = dot(out_w, dattn, 1, 1, BF16)
    do_mine, do_other = here.halves(do_t, 0)
    do_t = here.ordered(do_mine, here.swap(do_other), 1)
    do_t = here.chip_exchange(do_t, 0, 1)
    grad_out = dot(o_own, dattn, 1, 0, BF16)
    out_mine, out_other = here.halves(grad_out, 1)
    grad_out = (out_mine.astype(F32) + here.swap(out_other).astype(F32)).astype(BF16)
    dq_t, dk_t, dv_t = attend_backward(q_t, k_t, v_t, o_t, do_t, stat, starts)
    dq_t, dk_t, dv_t = (here.chip_exchange(part, 1, 0) for part in (dq_t, dk_t, dv_t))
    back_t = jnp.concatenate([dq_t, dk_t, dv_t], axis=0)
    back_w = jnp.concatenate([q_w, kv_w], axis=1)
    back_w_got = here.swap(back_w)
    back_mine, back_other = here.halves(back_t, 1)
    back_got = here.swap(back_other)
    da = dot(back_mine, back_w, 0, 1) + dot(back_got, back_w_got, 0, 1)
    grad_qkv = dot(normed, back_t, 0, 1, BF16)
    dx, grad_gain_one = norm_back(x_wide, scale_one, gain_one, da)
    input_grad = here.to_homes((dx + dh).astype(BF16))

    def as_grad(grad, parts, part_rows):
        return grad.reshape(parts, shards, quarters, part_rows, grad.shape[-1])

    grad_small = jnp.concatenate(
        [grad_gain_one[:, None], grad_gain_two[:, None], grad_router], axis=1
    )
    grad_small = jnp.pad(grad_small, ((0, 0), (0, 128 - grad_small.shape[1]))).astype(BF16)
    sum_down = here.reduce(as_grad(grad_down, experts, down_rows), bit_list)
    sum_gate = here.reduce(as_grad(grad_gate, 1, rows_q), bit_back)
    sum_up = here.reduce(as_grad(grad_up, 1, rows_q), bit_list)
    sum_out = here.reduce(as_grad(grad_out, 1, rows_q), bit_back)
    sum_qkv = here.reduce(
        as_grad(jnp.concatenate([grad_qkv, grad_small], axis=1), 1, rows_q), bit_list
    )

    def both_cores(summed, first, width):
        piece = summed[:, :, 0, :, first : first + width].astype(F32)
        return jnp.transpose(piece, (0, 2, 1, 3)).reshape(shard_rows, 2 * width)

    out_query = both_cores(sum_qkv, 0, width_q)
    out_key = both_cores(sum_qkv, width_q, width_k)
    out_value = both_cores(sum_qkv, width_q + width_k, width_k)
    small_sum = sum_qkv[:, :, 0, :, width_q + 2 * width_k :].astype(F32).sum(axis=1)
    small_sum = small_sum.reshape(shard_rows, -1)
    out_out = both_cores(sum_out, 0, features // 2)

    def expert_grad(summed):
        piece = summed[:, :, 0].astype(F32)
        piece = piece.reshape(quarters, 2, rows_q, experts, shards, hidden_part)
        return jnp.transpose(piece, (3, 0, 2, 4, 1, 5)).reshape(experts, shard_rows, hidden_all)

    out_down = jnp.transpose(sum_down.astype(F32), (2, 1, 0, 3, 4)).reshape(
        experts, 2 * hidden_part, features
    )
    return (
        block_out[:, None],
        input_grad[:, None],
        small_sum[:, 0],
        out_query,
        out_key,
        out_value,
        out_out,
        small_sum[:, 1],
        small_sum[:, 2 : 2 + experts],
        expert_grad(sum_gate),
        expert_grad(sum_up),
        out_down,
    )


def solution(mesh):
    in_specs = (
        P(None, "rep", "shard", None),
        P(None, "rep", "shard", None),
        P(None, "rep", "shard", None),
        P(),
        P("shard"),
        P("shard", None),
        P("shard", None),
        P("shard", None),
        P("shard", None),
        P("shard"),
        P("shard", None),
        P(None, "shard", None),
        P(None, "shard", None),
        P(None, "shard", None),
    )
    out_specs = (
        P(None, "rep", "shard", None),
        P(None, "rep", "shard", None),
        P("shard"),
        P("shard", None),
        P("shard", None),
        P("shard", None),
        P("shard", None),
        P("shard"),
        P("shard", None),
        P(None, "shard", None),
        P(None, "shard", None),
        P(None, "shard", None),
    )
    return jax.shard_map(local, mesh=mesh, in_specs=in_specs, out_specs=out_specs, check_vma=False)
```

time: 3760 us -> 1610 us (0.43)
  waiting for transfers between devices: 2770 us -> 509 us
  starting transfers between devices: 1.75 us -> 276 us
  Pallas kernels: 0 us -> 209 us
  matrix products: 472 us -> 277 us
  blocking collectives: 72.6 us -> 0 us
  local copies, waits for them, and re-layouts: 231 us -> 174 us
  other arithmetic: 171 us -> 119 us
    reduce_scatter x9 -> x0, waiting for transfers between devices: 1370 us -> none  [the longest x1 468 us: local(): lax.psum_scatter(jnp.stack(key_parts).astype(jnp.bfloat16), 'shard', scat...]
    all_gather x13 -> x5, waiting for transfers between devices: 1240 us -> 0.01 us  [reduce(): whole = lax.all_gather(total, 'rep', axis=0, tiled=False)]
    ppermute x0 -> x121, waiting for transfers between devices: none -> 508 us  [the longest x45 279 us: across(): return lax.ppermute(array, 'rep', [(i, i ^ bit) for i in range(self.reps)])]
    ppermute x0 -> x121, starting transfers between devices: none -> 276 us  [the longest x15 61.2 us: reduce(): up = lax.ppermute(send, 'shard', [(i, i + 1) for i in range(step)])]
    pallas_call x0 -> x8, Pallas kernels: none -> 209 us  [the longest x1 110 us: attend_backward(): pl.pallas_call(functools.partial(backward_kernel, group=group, wide=wide)...]
    dot_general x42 -> x23, matrix products: 472 us -> 277 us  [dot(): lax.dot_general(left, right, (((left_dim,), (right_dim,)), ((), ())), pre...]
    psum x1 -> x0, waiting for transfers between devices: 152 us -> none  [local(): lax.psum(attn_parts[1].astype(jnp.bfloat16), 'rep').astype(jnp.float32)]
    gather x9 -> x0, local copies, waits for them, and re-layouts: 123 us -> none  [the longest x2 35.7 us: local(): grad_dispatch.reshape(total_slots, features)[slot_pairs]]
  transfers between devices with their start and end apart: 24 -> 126, of which waited for: 24 -> 37; matrix products, arithmetic and copies ran while one was open for 11% -> 34% of each run, Pallas kernels for 0% -> 13%
where the time goes in v1:
time: 1610 us; the launch traced here: 1580 us
  waiting for transfers between devices  509 us (32%)
  matrix products  277 us (17%)
  starting transfers between devices  276 us (17%)
  Pallas kernels  209 us (13%)
  local copies, waits for them, and re-layouts  174 us (11%)
  other arithmetic  119 us (7%)
  between operations  17.1 us (1%)
    ppermute x45, waiting for transfers between devices, across(): return lax.ppermute(array, 'rep', [(i, i ^ bit) for i in range(self.reps)])  279 us
    dot_general x23, matrix products, dot(): lax.dot_general(left, right, (((left_dim,), (right_dim,)), ((), ())), pre...  277 us
    ppermute x18, waiting for transfers between devices, fetch(): lax.ppermute(down, 'shard', [(i, i - 1) for i in range(1, count - step +...  134 us
    pallas_call x1, Pallas kernels, attend_backward(): pl.pallas_call(functools.partial(backward_kernel, group=group, wide=wide)...  110 us
    pallas_call x1, Pallas kernels, attend_forward(): pl.pallas_call(functools.partial(forward_kernel, group=group, wide=wide),...  76.4 us
    ppermute x15, starting transfers between devices, reduce(): up = lax.ppermute(send, 'shard', [(i, i + 1) for i in range(step)])  61.2 us
    ppermute x18, starting transfers between devices, fetch(): lax.ppermute(up, 'shard', [(i, i + 1) for i in range(step - 1, count - 1)])  57.5 us
    reshape x6, local copies, waits for them, and re-layouts, expert_grad(): jnp.transpose(piece, (3, 0, 2, 4, 1, 5))  55.5 us
  transfers between devices with their start and end apart: 126, of which 37 were waited for; matrix products, arithmetic and copies ran while one was open for 34% of the time, Pallas kernels for 13%

profile of v1, /device:TPU:0, one launch (start us, length us, event | category | flops | bytes accessed | tf_op | source)
XLA Modules:
  0.0 1581.1 jit_solution(10321377462869493839)
XLA Ops:
  164.9 35.6 %collective-permute-done.5 = bf16[1,96,768]{2,1,0:T(8,128)(2,1)S(1)} collective-permute-done((bf16[1,96,768]{2,1,0:T(8,128)(2,1)S(1)}, bf16[1,96,768]{2,1,0:T(8,128)(2,1)S(1)}, u32[]{:S(2)}, u32[]{:S(2)}) %collective-permute-start.5) | collective-permute-done | bytes 147488 | tf_op jit(solution)/shard_map/ppermute | solution.py:334
  215.6 19.1 %collective-permute-start.37 = (bf16[1,96,2048]{2,1,0:T(8,128)(2,1)S(1)}, bf16[1,96,2048]{2,1,0:T(8,128)(2,1)}, u32[]{:S(2)}, u32[]{:S(2)}) collective-permute-start(bf16[1,96,2048]{2,1,0:T(8,128)(2,1)S(1)} %dynamic-slice_bitcast_fusion.14), channel_id=1, source_target_pairs={{0,1},{1,2},{2,3},{4,5},{5,6},{6,7},{8,9},{9,10},{10,11},{12,13},{... | collective-permute-start | bytes 1179656 | tf_op jit(solution)/shard_map/ppermute | solution.py:333
  267.3 31.9 %collective-permute-done.39 = bf16[1,96,2048]{2,1,0:T(8,128)(2,1)S(1)} collective-permute-done((bf16[1,96,2048]{2,1,0:T(8,128)(2,1)}, bf16[1,96,2048]{2,1,0:T(8,128)(2,1)S(1)}, u32[]{:S(2)}, u32[]{:S(2)}) %collective-permute-start.39) | collective-permute-done | bytes 393248 | tf_op jit(solution)/shard_map/ppermute | solution.py:334
  346.2 13.3 collective-permute-start.71
  386.0 76.4 %attend_forward.1 = (bf16[768,2048]{1,0:T(8,128)(2,1)S(1)}, f32[4,3,2048]{2,1,0:T(4,128)S(1)}) custom-call(s32[4,4]{1,0:T(4,128)S(1)} %pad_add_fusion.2.ranges, bf16[768,2048]{1,0:T(8,128)(2,1)} %convolution_convert_fusion.8.q_ref, bf16[256,2048]{1,0:T(8,128)(2,1)S(1)} %get-tuple-element.129.k_ref, bf16[256,2048]{1,0:T(8,128)(2,1)S(1)} %get-tuple-element.128.v_ref, ...), custom_call_target="tpu_custom_call" | custom-call | flops 25769803776 | bytes 12582912 | tf_op jit(solution)/shard_map/attend_forward/pallas_call | solution.py:172
  489.6 16.7 %collective-permute-done.52.refs_2_ = bf16[3,1,96,2048]{3,2,1,0:T(8,128)(2,1)S(1)} collective-permute-done((bf16[3,1,96,2048]{3,2,1,0:T(8,128)(2,1)S(1)}, bf16[3,1,96,2048]{3,2,1,0:T(8,128)(2,1)S(1)}, u32[]{:S(2)}, u32[]{:S(2)}) %collective-permute-start.52) | collective-permute-done | bytes 1179680 | tf_op jit(solution)/shard_map/ppermute | solution.py:247
  533.6 23.2 %collective-permute-done.43.refs_2_ = bf16[3,1,96,2048]{3,2,1,0:T(8,128)(2,1)S(1)} collective-permute-done((bf16[3,1,96,2048]{3,2,1,0:T(8,128)(2,1)S(1)}, bf16[3,1,96,2048]{3,2,1,0:T(8,128)(2,1)S(1)}, u32[]{:S(2)}, u32[]{:S(2)}) %collective-permute-start.43) | collective-permute-done | bytes 1179680 | tf_op jit(solution)/shard_map/ppermute | solution.py:247
  560.4 20.4 %collective-permute-done.54.refs_4_ = bf16[3,1,96,2048]{3,2,1,0:T(8,128)(2,1)S(1)} collective-permute-done((bf16[3,1,96,2048]{3,2,1,0:T(8,128)(2,1)S(1)}, bf16[3,1,96,2048]{3,2,1,0:T(8,128)(2,1)S(1)}, u32[]{:S(2)}, u32[]{:S(2)}) %collective-permute-start.54) | collective-permute-done | bytes 1179680 | tf_op jit(solution)/shard_map/ppermute | solution.py:247
  613.3 19.0 %fusion.40 = f32[2048,2048]{0,1:T(8,128)} fusion(bf16[2048,1536]{1,0:T(8,128)(2,1)S(1)} %bitcast.361, bf16[1024,1536]{1,0:T(8,128)(2,1)} %collective-permute-done.72, bf16[512,1536]{1,0:T(8,128)(2,1)S(1)} %copy-done.44, bf16[512,1536]{1,0:T(8,128)(2,1)S(1)} %copy-done.40), kind=kOutput, calls=%fused_computation.99 | convolution fusion | flops 12903776256 | bytes 29360128 | tf_op jit(solution)/shard_map/dot_general | solution.py:22
  636.5 20.1 %convolution_convert_fusion.2 = bf16[2048,2048]{0,1:T(8,128)(2,1)} fusion(bf16[1536,2048]{1,0:T(8,128)(2,1)} %bitcast.366, bf16[1024,1536]{1,0:T(8,128)(2,1)} %collective-permute-done.36, bf16[1024,1536]{1,0:T(8,128)(2,1)} %copy-done.28), kind=kOutput, calls=%fused_computation.26 | convolution fusion | flops 12901679104 | bytes 20971520 | tf_op jit(solution)/shard_map/dot_general | solution.py:22
  656.6 33.0 %fusion.5 = (bf16[2048,2048]{0,1:T(8,128)(2,1)}, bf16[2048,2048]{0,1:T(8,128)(2,1)}, bf16[2048,2048]{0,1:T(8,128)(2,1)}, bf16[2048,2048]{0,1:T(8,128)(2,1)}) fusion(bf16[2048,2048]{0,1:T(8,128)(2,1)} %convolution_convert_fusion.2, f32[2048,2048]{0,1:T(8,128)} %fusion.40, f32[2048,4]{0,1:T(4,128)S(1)} %select_reduce_fusion, ...), kind=kOutput, calls=%fused_computation.13 | convolution fusion | flops 12981370880 | bytes 71335936 | tf_op jit(solution)/shard_map/dot_general | solution.py:22
  758.4 18.4 %convolution_convert_fusion.6 = bf16[1536,2048]{1,0:T(8,128)(2,1)} fusion(bf16[2048,2048]{0,1:T(8,128)(2,1)} %get-tuple-element.93, bf16[1024,1536]{1,0:T(8,128)(2,1)} %collective-permute-done.36, bf16[1024,1536]{1,0:T(8,128)(2,1)S(1)} %copy-done.29), kind=kOutput, calls=%fused_computation.30 | convolution fusion | flops 12900630528 | bytes 20971520 | tf_op jit(solution)/shard_map/dot_general | solution.py:22
  784.2 19.1 %convolution_convert_fusion.5 = bf16[1536,2048]{1,0:T(8,128)(2,1)} fusion(bf16[2048,2048]{0,1:T(8,128)(2,1)} %get-tuple-element.94, bf16[1024,1536]{1,0:T(8,128)(2,1)} %collective-permute-done.36, bf16[1024,1536]{1,0:T(8,128)(2,1)S(1)} %copy-done.29), kind=kOutput, calls=%fused_computation.29 | convolution fusion | flops 12900630528 | bytes 20971520 | tf_op jit(solution)/shard_map/dot_general | solution.py:22
  803.3 17.7 %convolution_convert_fusion.1 = bf16[2048,1536]{1,0:T(8,128)(2,1)} fusion(bf16[2048,2048]{0,1:T(8,128)(2,1)} %get-tuple-element.95, bf16[1024,1536]{1,0:T(8,128)(2,1)} %collective-permute-done.72, bf16[512,1536]{1,0:T(8,128)(2,1)S(1)} %copy-done.45, bf16[512,1536]{1,0:T(8,128)(2,1)S(1)} %copy-done.41), kind=kOutput, calls=%fused_computation.25 | convolution fusion | flops 12906921984 | bytes 20971520 | tf_op jit(solution)/shard_map/dot_general | solution.py:22
  886.5 27.9 %collective-permute-done.105 = bf16[1,4,2,96,2048]{4,3,1,2,0:T(8,128)(2,1)} collective-permute-done((bf16[1,4,2,96,2048]{4,3,1,2,0:T(8,128)(2,1)}, bf16[1,4,2,96,2048]{4,3,1,2,0:T(8,128)(2,1)}, u32[]{:S(2)}, u32[]{:S(2)}) %collective-permute-start.105) | collective-permute-done | bytes 3145760 | tf_op jit(solution)/shard_map/ppermute | solution.py:247
  921.1 60.8 %collective-permute-done.113 = bf16[4,4,2,32,1536]{4,3,0,1,2:T(8,128)(2,1)} collective-permute-done((bf16[4,4,2,32,1536]{4,3,0,1,2:T(8,128)(2,1)}, bf16[4,4,2,32,1536]{4,3,0,1,2:T(8,128)(2,1)}, u32[]{:S(2)}, u32[]{:S(2)}) %collective-permute-start.113) | collective-permute-done | bytes 3145760 | tf_op jit(solution)/shard_map/ppermute | solution.py:247
  988.5 26.2 %collective-permute-done.98 = bf16[1,4,96,2048]{3,2,1,0:T(8,128)(2,1)S(1)} collective-permute-done((bf16[1,4,96,2048]{3,2,1,0:T(8,128)(2,1)S(1)}, bf16[1,4,96,2048]{3,2,1,0:T(8,128)(2,1)S(1)}, u32[]{:S(2)}, u32[]{:S(2)}) %collective-permute-start.98) | collective-permute-done | bytes 1572896 | tf_op jit(solution)/shard_map/ppermute | solution.py:247
  1077.2 109.5 %attend_backward.1 = (bf16[768,2048]{1,0:T(8,128)(2,1)}, bf16[256,2048]{1,0:T(8,128)(2,1)S(1)}, bf16[256,2048]{1,0:T(8,128)(2,1)S(1)}) custom-call(s32[4,4]{1,0:T(4,128)S(1)} %pad_add_fusion.2.ranges, bf16[768,2048]{1,0:T(8,128)(2,1)} %convolution_convert_fusion.8.q_ref, bf16[256,2048]{1,0:T(8,128)(2,1)S(1)} %copy-done.27, bf16[256,2048]{1,0:T(8,128)(2,1)S(1)} %copy-done.25, ...), custom_call_target="tpu_custom_call" | custom-call | flops 64424509440 | bytes 25165824 | tf_op jit(solution)/shard_map/attend_backward/pallas_call | solution.py:202
  1276.4 30.9 %collective-permute-done.80 = bf16[1,4,2,96,1408]{4,3,2,1,0:T(8,128)(2,1)S(1)} collective-permute-done((bf16[1,4,2,96,1408]{4,3,2,1,0:T(8,128)(2,1)S(1)}, bf16[1,4,2,96,1408]{4,3,2,1,0:T(8,128)(2,1)S(1)}, u32[]{:S(2)}, u32[]{:S(2)}) %collective-permute-start.80) | collective-permute-done | bytes 2162720 | tf_op jit(solution)/shard_map/ppermute | solution.py:247
  1310.3 26.5 %collective-permute-done.81 = bf16[1,4,96,1408]{3,2,1,0:T(8,128)(2,1)} collective-permute-done((bf16[1,4,96,1408]{3,2,1,0:T(8,128)(2,1)S(1)}, bf16[1,4,96,1408]{3,2,1,0:T(8,128)(2,1)}, u32[]{:S(2)}, u32[]{:S(2)}) %collective-permute-start.81) | collective-permute-done | bytes 1081376 | tf_op jit(solution)/shard_map/ppermute | solution.py:247
  1384.4 16.5 %collective-permute-done.84 = bf16[1,96,1408]{2,1,0:T(8,128)(2,1)S(1)} collective-permute-done((bf16[1,96,1408]{2,1,0:T(8,128)(2,1)S(1)}, bf16[1,96,1408]{2,1,0:T(8,128)(2,1)S(1)}, u32[]{:S(2)}, u32[]{:S(2)}) %collective-permute-start.84) | collective-permute-done | bytes 270368 | tf_op jit(solution)/shard_map/ppermute | solution.py:426
  1400.8 21.1 %collective-permute-done.87 = bf16[1,96,1408]{2,1,0:T(8,128)(2,1)S(1)} collective-permute-done((bf16[1,96,1408]{2,1,0:T(8,128)(2,1)S(1)}, bf16[1,96,1408]{2,1,0:T(8,128)(2,1)S(1)}, u32[]{:S(2)}, u32[]{:S(2)}) %collective-permute-start.87) | collective-permute-done | bytes 270368 | tf_op jit(solution)/shard_map/ppermute | solution.py:431
  1424.9 34.4 %collective-permute-start.78 = (bf16[512,1536]{1,0:T(8,128)(2,1)S(1)}, bf16[512,1536]{1,0:T(8,128)(2,1)S(1)}, u32[]{:S(2)}, u32[]{:S(2)}) collective-permute-start(bf16[512,1536]{1,0:T(8,128)(2,1)S(1)} %get-tuple-element.106), channel_id=1, source_target_pairs={{2,0},{0,1},{6,2},{4,3},{3,4},{1,5},{7,6},{5,7},{10,8},{8,9},{14,1... | collective-permute-start | bytes 4718600 | tf_op jit(solution)/shard_map/ppermute | solution.py:287
  1464.2 29.6 %collective-permute-done.78 = bf16[512,1536]{1,0:T(8,128)(2,1)S(1)} collective-permute-done((bf16[512,1536]{1,0:T(8,128)(2,1)S(1)}, bf16[512,1536]{1,0:T(8,128)(2,1)S(1)}, u32[]{:S(2)}, u32[]{:S(2)}) %collective-permute-start.78) | collective-permute-done | bytes 1572896 | tf_op jit(solution)/shard_map/ppermute | solution.py:287
  (720 shorter events, 816.6 us)
Async XLA Ops:
  7.2 1488.7 %all-gather.13.cloned.1.call-start = ((), (), s32[]{:S(2)}) async-start(), calls=%async_computation.1 | async-start | bytes 1327104 | tf_op jit(solution)/shard_map/all_gather | solution.py:436
  144.8 110.7 %collective-permute-start = (bf16[512,1536]{1,0:T(8,128)(2,1)}, bf16[512,1536]{1,0:T(8,128)(2,1)}, u32[]{:S(2)}, u32[]{:S(2)}) collective-permute-start(bf16[512,1536]{1,0:T(8,128)(2,1)} %get-tuple-element.122), channel_id=1, source_target_pairs={{0,2},{1,0},{2,6},{3,4},{4,3},{5,1},{6,7},{7,5},{8,10},{9,8},{10,1... | collective-permute-start | bytes 4718600 | tf_op jit(solution)/shard_map/ppermute | solution.py:272
  148.0 108.8 %collective-permute-start.1 = (bf16[512,1536]{1,0:T(8,128)(2,1)}, bf16[512,1536]{1,0:T(8,128)(2,1)}, u32[]{:S(2)}, u32[]{:S(2)}) collective-permute-start(bf16[512,1536]{1,0:T(8,128)(2,1)} %get-tuple-element.123), channel_id=1, source_target_pairs={{0,0},{1,2},{2,4},{3,6},{4,1},{5,3},{6,5},{7,7},{8,8},{9,10},{10,1... | collective-permute-start | bytes 4718600 | tf_op jit(solution)/shard_map/ppermute | solution.py:272
  249.9 136.0 %collective-permute-start.31 = (bf16[1,4,96,768]{3,2,1,0:T(8,128)(2,1)}, bf16[1,4,96,768]{3,2,1,0:T(8,128)(2,1)}, u32[]{:S(2)}, u32[]{:S(2)}) collective-permute-start(bf16[1,4,96,768]{3,2,1,0:T(8,128)(2,1)} %bitcast.21.refs_0_), channel_id=1, source_target_pairs={{0,4},{4,0},{8,12},{12,8},{16,20},{20,16},{24,28},{28,24},{1,5},{5... | collective-permute-start | bytes 1769480 | tf_op jit(solution)/shard_map/ppermute | solution.py:247
  253.3 224.6 %collective-permute-start.70 = (bf16[512,1536]{1,0:T(8,128)(2,1)}, bf16[512,1536]{1,0:T(8,128)(2,1)}, u32[]{:S(2)}, u32[]{:S(2)}) collective-permute-start(bf16[512,1536]{1,0:T(8,128)(2,1)} %get-tuple-element.112), channel_id=1, source_target_pairs={{0,2},{1,0},{2,6},{3,4},{4,3},{5,1},{6,7},{7,5},{8,10},{9,8},{10,1... | collective-permute-start | bytes 4718600 | tf_op jit(solution)/shard_map/ppermute | solution.py:272
  346.2 131.8 %collective-permute-start.71 = (bf16[512,1536]{1,0:T(8,128)(2,1)}, bf16[512,1536]{1,0:T(8,128)(2,1)}, u32[]{:S(2)}, u32[]{:S(2)}) collective-permute-start(bf16[512,1536]{1,0:T(8,128)(2,1)} %get-tuple-element.113), channel_id=1, source_target_pairs={{0,0},{1,2},{2,4},{3,6},{4,1},{5,3},{6,5},{7,7},{8,8},{9,10},{10,1... | collective-permute-start | bytes 4718600 | tf_op jit(solution)/shard_map/ppermute | solution.py:272
  359.5 105.4 %collective-permute-start.28 = (bf16[3,1,96,768]{3,2,1,0:T(8,128)(2,1)S(1)}, bf16[3,1,96,768]{3,2,1,0:T(8,128)(2,1)S(1)}, u32[]{:S(2)}, u32[]{:S(2)}) collective-permute-start(bf16[3,1,96,768]{3,2,1,0:T(8,128)(2,1)S(1)} %copy-done.21), channel_id=1, source_target_pairs={{0,8},{4,12},{8,0},{12,4},{16,24},{20,28},{24,16},{28,20},{1,9},{5... | collective-permute-start | bytes 1327112 | tf_op jit(solution)/shard_map/ppermute | solution.py:247
  364.6 100.3 %collective-permute-start.29 = (bf16[3,1,96,768]{3,2,1,0:T(8,128)(2,1)S(1)}, bf16[3,1,96,768]{3,2,1,0:T(8,128)(2,1)S(1)}, u32[]{:S(2)}, u32[]{:S(2)}) collective-permute-start(bf16[3,1,96,768]{3,2,1,0:T(8,128)(2,1)S(1)} %copy-done.21), channel_id=1, source_target_pairs={{0,16},{4,20},{8,24},{12,28},{16,0},{20,4},{24,8},{28,12},{1,17},{... | collective-permute-start | bytes 1327112 | tf_op jit(solution)/shard_map/ppermute | solution.py:247
  506.6 106.6 %collective-permute-start.72 = (bf16[1024,1536]{1,0:T(8,128)(2,1)}, bf16[1024,1536]{1,0:T(8,128)(2,1)}, u32[]{:S(2)}, u32[]{:S(2)}) collective-permute-start(bf16[1024,1536]{1,0:T(8,128)(2,1)} %pad_maximum_fusion.5), channel_id=1, source_target_pairs={{0,4},{4,0},{8,12},{12,8},{16,20},{20,16},{24,28},{28,24},{1,5},{5... | collective-permute-start | bytes 9437192 | tf_op jit(solution)/shard_map/ppermute | solution.py:247
  588.9 638.7 %collective-permute-start.77 = (bf16[1536,1280]{1,0:T(8,128)(2,1)}, bf16[1536,1280]{1,0:T(8,128)(2,1)}, u32[]{:S(2)}, u32[]{:S(2)}) collective-permute-start(bf16[1536,1280]{1,0:T(8,128)(2,1)} %pad_maximum_fusion.3), channel_id=1, source_target_pairs={{0,4},{4,0},{8,12},{12,8},{16,20},{20,16},{24,28},{28,24},{1,5},{5... | collective-permute-start | bytes 11796488 | tf_op jit(solution)/shard_map/ppermute | solution.py:247
  726.2 117.0 %collective-permute-start.74 = (f32[1024,4]{0,1:T(4,128)}, f32[1024,4]{0,1:T(4,128)}, u32[]{:S(2)}, u32[]{:S(2)}) collective-permute-start(f32[1024,4]{0,1:T(4,128)} %slice.182), channel_id=1, source_target_pairs={{0,4},{4,0},{8,12},{12,8},{16,20},{20,16},{24,28},{28,24},{1,5},{5... | collective-permute-start | bytes 49160 | tf_op jit(solution)/shard_map/ppermute | solution.py:247
  846.6 135.3 %collective-permute-start.113 = (bf16[4,4,2,32,1536]{4,3,0,1,2:T(8,128)(2,1)}, bf16[4,4,2,32,1536]{4,3,0,1,2:T(8,128)(2,1)}, u32[]{:S(2)}, u32[]{:S(2)}) collective-permute-start(bf16[4,4,2,32,1536]{4,3,0,1,2:T(8,128)(2,1)} %bitcast.340), channel_id=1, source_target_pairs={{0,8},{4,12},{8,0},{12,4},{16,24},{20,28},{24,16},{28,20},{1,9},{5... | collective-permute-start | bytes 9437192 | tf_op jit(solution)/shard_map/ppermute | solution.py:247
  881.5 170.0 %collective-permute-start.75 = (bf16[768,1024]{1,0:T(8,128)(2,1)S(1)}, bf16[768,1024]{1,0:T(8,128)(2,1)S(1)}, u32[]{:S(2)}, u32[]{:S(2)}) collective-permute-start(bf16[768,1024]{1,0:T(8,128)(2,1)S(1)} %get-tuple-element.109), channel_id=1, source_target_pairs={{0,4},{4,0},{8,12},{12,8},{16,20},{20,16},{24,28},{28,24},{1,5},{5... | collective-permute-start | bytes 4718600 | tf_op jit(solution)/shard_map/ppermute | solution.py:247
  914.4 100.2 %collective-permute-start.98 = (bf16[1,4,96,2048]{3,2,1,0:T(8,128)(2,1)S(1)}, bf16[1,4,96,2048]{3,2,1,0:T(8,128)(2,1)S(1)}, u32[]{:S(2)}, u32[]{:S(2)}) collective-permute-start(bf16[1,4,96,2048]{3,2,1,0:T(8,128)(2,1)S(1)} %dynamic-slice_bitcast_fusion.3), channel_id=1, source_target_pairs={{0,8},{4,12},{8,0},{12,4},{16,24},{20,28},{24,16},{28,20},{1,9},{5... | collective-permute-start | bytes 4718600 | tf_op jit(solution)/shard_map/ppermute | solution.py:247
  918.6 99.2 %collective-permute-start.106 = (bf16[1,4,96,2048]{3,2,1,0:T(8,128)(2,1)S(1)}, bf16[1,4,96,2048]{3,2,1,0:T(8,128)(2,1)S(1)}, u32[]{:S(2)}, u32[]{:S(2)}) collective-permute-start(bf16[1,4,96,2048]{3,2,1,0:T(8,128)(2,1)S(1)} %dynamic-slice_bitcast_fusion.2), channel_id=1, source_target_pairs={{0,16},{4,20},{8,24},{12,28},{16,0},{20,4},{24,8},{28,12},{1,17},{... | collective-permute-start | bytes 4718600 | tf_op jit(solution)/shard_map/ppermute | solution.py:247
  1039.7 163.9 %collective-permute-start.114 = (bf16[4,4,32,1536]{3,2,0,1:T(8,128)(2,1)}, bf16[4,4,32,1536]{3,2,0,1:T(8,128)(2,1)}, u32[]{:S(2)}, u32[]{:S(2)}) collective-permute-start(bf16[4,4,32,1536]{3,2,0,1:T(8,128)(2,1)} %dynamic-slice_bitcast_fusion.1), channel_id=1, source_target_pairs={{0,16},{4,20},{8,24},{12,28},{16,0},{20,4},{24,8},{28,12},{1,17},{... | collective-permute-start | bytes 4718600 | tf_op jit(solution)/shard_map/ppermute | solution.py:247
  1047.5 145.6 %collective-permute-start.107 = (bf16[1,96,2048]{2,1,0:T(8,128)(2,1)}, bf16[1,96,2048]{2,1,0:T(8,128)(2,1)}, u32[]{:S(2)}, u32[]{:S(2)}) collective-permute-start(bf16[1,96,2048]{2,1,0:T(8,128)(2,1)} %get-tuple-element.136), channel_id=1, source_target_pairs={{0,1},{4,5},{8,9},{12,13},{16,17},{20,21},{24,25},{28,29}} | collective-permute-start | bytes 1179656 | tf_op jit(solution)/shard_map/ppermute | solution.py:426
  1070.0 117.8 %collective-permute-start.101 = (bf16[1,96,2048]{2,1,0:T(8,128)(2,1)}, bf16[1,96,2048]{2,1,0:T(8,128)(2,1)}, u32[]{:S(2)}, u32[]{:S(2)}) collective-permute-start(bf16[1,96,2048]{2,1,0:T(8,128)(2,1)} %get-tuple-element.138), channel_id=1, source_target_pairs={{0,1},{1,2},{2,3},{4,5},{5,6},{6,7},{8,9},{9,10},{10,11},{12,13},{... | collective-permute-start | bytes 1179656 | tf_op jit(solution)/shard_map/ppermute | solution.py:426
  1075.1 112.6 %collective-permute-start.104 = (bf16[1,96,2048]{2,1,0:T(8,128)(2,1)}, bf16[1,96,2048]{2,1,0:T(8,128)(2,1)}, u32[]{:S(2)}, u32[]{:S(2)}) collective-permute-start(bf16[1,96,2048]{2,1,0:T(8,128)(2,1)} %fusion.63), channel_id=1, source_target_pairs={{1,0},{2,1},{3,2},{5,4},{6,5},{7,6},{9,8},{10,9},{11,10},{13,12},{... | collective-permute-start | bytes 1179656 | tf_op jit(solution)/shard_map/ppermute | solution.py:431
  1077.2 423.6 %all-gather.15.cloned.1.call-start = ((), (), s32[]{:S(2)}) async-start(), calls=%async_computation.2 | async-start | bytes 3538944 | tf_op jit(solution)/shard_map/all_gather | solution.py:436
  1189.9 338.6 %all-gather.17.cloned.1.call-start = ((), (), s32[]{:S(2)}) async-start(), calls=%async_computation.3 | async-start | bytes 3538944 | tf_op jit(solution)/shard_map/all_gather | solution.py:436
  1227.3 329.0 %all-gather.19.cloned.1.call-start = ((), (), s32[]{:S(2)}) async-start(), calls=%async_computation.4 | async-start | bytes 3538944 | tf_op jit(solution)/shard_map/all_gather | solution.py:436
  1310.3 252.0 %all-gather.11.cloned.1.call-start = ((), (), s32[]{:S(2)}) async-start(), calls=%async_computation | async-start | bytes 2433024 | tf_op jit(solution)/shard_map/all_gather | solution.py:436
  1357.9 102.1 %collective-permute-start.68 = (bf16[512,1536]{1,0:T(8,128)(2,1)}, bf16[512,1536]{1,0:T(8,128)(2,1)}, u32[]{:S(2)}, u32[]{:S(2)}) collective-permute-start(bf16[512,1536]{1,0:T(8,128)(2,1)} %get-tuple-element.116), channel_id=1, source_target_pairs={{2,0},{0,1},{6,2},{4,3},{3,4},{1,5},{7,6},{5,7},{10,8},{8,9},{14,1... | collective-permute-start | bytes 4718600 | tf_op jit(solution)/shard_map/ppermute | solution.py:287
  (233 other events, 6764.7 us)
Sparse Core Ops, SparseCore 0:
  1077.3 22.6 all-gather.12
  1190.0 29.3 all-gather.14
  1227.4 42.2 all-gather.16
  1310.4 37.9 all-gather.18
  1422.9 58.8 all-gather.10

commit v2 on v1

v2 whole, which is shorter than its diff:
```python
import functools
import math

import jax
import jax.numpy as jnp
from jax import lax
from jax.experimental import pallas as pl
from jax.experimental.pallas import tpu as pltpu
from jax.sharding import PartitionSpec as P

HEAD = 64
EPSILON = 1e-05
NEGATIVE = -1e30
F32 = jnp.float32
BF16 = jnp.bfloat16
LOG2_SCALE = HEAD ** (-0.5) * math.log2(math.e)
SCALE = HEAD ** (-0.5)
PLANE = ("chip", "core")
BOTH = ("chip", "core", "shard")


def together(*arrays):
    return lax.optimization_barrier(arrays)


def dot(left, right, left_dim, right_dim, kind=F32):
    return lax.dot_general(
        left, right, (((left_dim,), (right_dim,)), ((), ())), preferred_element_type=F32
    ).astype(kind)


def forward_blocks(length):
    return min(512, length), min(512, length)


def backward_blocks(length):
    return min(512, length), min(256, length)


def visible_mask(index, width, first_key, first_query, starts):
    rows = first_key + lax.broadcasted_iota(jnp.int32, (width, starts.shape[1]), 0)
    columns = first_query + lax.broadcasted_iota(jnp.int32, (1, starts.shape[1]), 1)
    return (rows >= starts) & (rows <= columns)


def side_by_side(block, group):
    return jnp.concatenate([block[g * HEAD : (g + 1) * HEAD, :] for g in range(group)], axis=1)


def three_loops(ranges, place, step, carry):
    low, full_low, full_high, high = (ranges[place, n] for n in range(4))
    carry = lax.fori_loop(low, full_low, functools.partial(step, True), carry)
    carry = lax.fori_loop(full_low, full_high, functools.partial(step, False), carry)
    return lax.fori_loop(full_high, high, functools.partial(step, True), carry)


def forward_kernel(ranges, q_ref, k_ref, v_ref, starts_ref, o_ref, stat_ref, k_rows, *, group, wide):
    place = pl.program_id(1)
    q_width = q_ref.shape[1]

    @pl.when(place == 0)
    def _():
        k_rows[...] = k_ref[...].T

    queries = side_by_side(q_ref[...], group)
    starts = starts_ref[...]

    def step(masked, index, carry):
        high, total, mixed = carry
        first = pl.multiple_of(index * wide, wide)
        scores = (
            jnp.dot(k_rows[pl.ds(first, wide), :], queries, preferred_element_type=F32)
            * LOG2_SCALE
        )
        if masked:
            seen = visible_mask(index, wide, first, place * q_width, starts)
            scores = jnp.where(jnp.concatenate([seen] * group, axis=1), scores, NEGATIVE)
        new_high = jnp.maximum(high, jnp.max(scores, axis=0, keepdims=True))
        weights = jnp.exp2(scores - new_high)
        fade = jnp.exp2(high - new_high)
        total = total * fade + jnp.sum(weights, axis=0, keepdims=True)
        mixed = mixed * fade + jnp.dot(
            v_ref[:, pl.ds(first, wide)], weights.astype(BF16), preferred_element_type=F32
        )
        return new_high, total, mixed

    columns = group * q_width
    high, total, mixed = three_loops(
        ranges,
        place,
        step,
        (
            jnp.full((1, columns), NEGATIVE, F32),
            jnp.zeros((1, columns), F32),
            jnp.zeros((HEAD, columns), F32),
        ),
    )
    mixed = (mixed / total).astype(BF16)
    stat = high + jnp.log2(total)
    for g in range(group):
        span = slice(g * q_width, (g + 1) * q_width)
        o_ref[g * HEAD : (g + 1) * HEAD, :] = mixed[:, span]
        stat_ref[0, g : g + 1, :] = stat[:, span]


def backward_kernel(
    ranges, q_ref, k_ref, v_ref, o_ref, g_ref, stat_ref, starts_ref,
    dq_ref, dk_ref, dv_ref, k_rows, v_rows, dk_sum, dv_sum, *, group, wide,
):
    place = pl.program_id(1)
    q_width = q_ref.shape[1]

    @pl.when(place == 0)
    def _():
        k_rows[...] = k_ref[...].T
        v_rows[...] = v_ref[...].T
        dk_sum[...] = jnp.zeros_like(dk_sum)
        dv_sum[...] = jnp.zeros_like(dv_sum)

    queries = side_by_side(q_ref[...], group)
    grads = side_by_side(g_ref[...], group)
    outs = side_by_side(o_ref[...], group)
    inner = jnp.sum(grads.astype(F32) * outs.astype(F32), axis=0, keepdims=True)
    stat = jnp.concatenate([stat_ref[0, g : g + 1, :] for g in range(group)], axis=1)
    starts = starts_ref[...]

    def step(masked, index, dq):
        first = pl.multiple_of(index * wide, wide)
        span = pl.ds(first, wide)
        scores = jnp.dot(k_rows[span, :], queries, preferred_element_type=F32) * LOG2_SCALE
        chances = jnp.exp2(scores - stat)
        if masked:
            seen = visible_mask(index, wide, first, place * q_width, starts)
            chances = jnp.where(jnp.concatenate([seen] * group, axis=1), chances, 0.0)
        slopes = jnp.dot(v_rows[span, :], grads, preferred_element_type=F32)
        pull = (chances * (slopes - inner)).astype(BF16)
        dv_sum[:, span] += dot(grads, chances.astype(BF16), 1, 1)
        dk_sum[:, span] += dot(queries, pull, 1, 1)
        return dq + jnp.dot(k_ref[:, span], pull, preferred_element_type=F32)

    dq = three_loops(ranges, place, step, jnp.zeros((HEAD, group * q_width), F32))
    dq = (dq * SCALE).astype(BF16)
    for g in range(group):
        dq_ref[g * HEAD : (g + 1) * HEAD, :] = dq[:, g * q_width : (g + 1) * q_width]

    @pl.when(place == pl.num_programs(1) - 1)
    def _():
        dk_ref[...] = (dk_sum[...] * SCALE).astype(BF16)
        dv_ref[...] = dv_sum[...].astype(BF16)


def block_ranges(starts, q_width, wide):
    length = starts.shape[1]
    count = length // q_width
    first_query = jnp.arange(count, dtype=jnp.int32) * q_width
    low = starts[0, ::q_width] // wide
    full_low = (starts[0, q_width - 1 :: q_width] + wide - 1) // wide
    full_high = (first_query + 1) // wide
    full_high = first_query // wide
    high = (first_query + q_width) // wide
    full_low = jnp.clip(full_low, low, jnp.maximum(full_high, low))
    full_high = jnp.maximum(full_high, full_low)
    return jnp.stack([low, full_low, full_high, high], axis=1)


def attention_specs(head, group, length, q_width):
    per_query = pl.BlockSpec((group * HEAD, q_width), lambda h, i, r: (head, i))
    per_head = pl.BlockSpec((HEAD, length), lambda h, i, r: (head, 0))
    out_query = pl.BlockSpec((group * HEAD, q_width), lambda h, i, r: (0, i))
    out_head = pl.BlockSpec((HEAD, length), lambda h, i, r: (0, 0))
    stat = pl.BlockSpec((1, group, q_width), lambda h, i, r: (0, 0, i))
    starts = pl.BlockSpec((1, q_width), lambda h, i, r: (0, i))
    return per_query, per_head, out_query, out_head, stat, starts


def attend_forward(head, q_t, k_t, v_t, starts):
    length = q_t.shape[1]
    group = q_t.shape[0] // k_t.shape[0]
    q_width, wide = forward_blocks(length)
    per_query, per_head, out_query, _, stat, start_spec = attention_specs(
        head, group, length, q_width
    )
    pairs = group * length * length // 2
    return pl.pallas_call(
        functools.partial(forward_kernel, group=group, wide=wide),
        out_shape=(
            jax.ShapeDtypeStruct((group * HEAD, length), BF16),
            jax.ShapeDtypeStruct((1, group, length), F32),
        ),
        grid_spec=pltpu.PrefetchScalarGridSpec(
            num_scalar_prefetch=1,
            grid=(1, length // q_width),
            in_specs=[per_query, per_head, per_head, start_spec],
            out_specs=(out_query, stat),
            scratch_shapes=[pltpu.VMEM((length, HEAD), BF16)],
        ),
        compiler_params=pltpu.CompilerParams(
            dimension_semantics=("arbitrary", "arbitrary"), vmem_limit_bytes=40 << 20
        ),
        cost_estimate=pl.CostEstimate(
            flops=pairs * HEAD * 4, transcendentals=0, bytes_accessed=group * length * 512
        ),
        name="attend_forward",
    )(block_ranges(starts, q_width, wide), q_t, k_t, v_t, starts)


def attend_backward(head, q_t, k_t, v_t, o_h, g_h, stat_h, starts):
    length = q_t.shape[1]
    group = q_t.shape[0] // k_t.shape[0]
    q_width, wide = backward_blocks(length)
    per_query, per_head, out_query, out_head, stat, start_spec = attention_specs(
        head, group, length, q_width
    )
    pairs = group * length * length // 2
    return pl.pallas_call(
        functools.partial(backward_kernel, group=group, wide=wide),
        out_shape=(
            jax.ShapeDtypeStruct((group * HEAD, length), BF16),
            jax.ShapeDtypeStruct((HEAD, length), BF16),
            jax.ShapeDtypeStruct((HEAD, length), BF16),
        ),
        grid_spec=pltpu.PrefetchScalarGridSpec(
            num_scalar_prefetch=1,
            grid=(1, length // q_width),
            in_specs=[per_query, per_head, per_head, out_query, out_query, stat, start_spec],
            out_specs=(out_query, out_head, out_head),
            scratch_shapes=[
                pltpu.VMEM((length, HEAD), BF16),
                pltpu.VMEM((length, HEAD), BF16),
                pltpu.VMEM((HEAD, length), F32),
                pltpu.VMEM((HEAD, length), F32),
            ],
        ),
        compiler_params=pltpu.CompilerParams(
            dimension_semantics=("arbitrary", "arbitrary"), vmem_limit_bytes=40 << 20
        ),
        cost_estimate=pl.CostEstimate(
            flops=pairs * HEAD * 10, transcendentals=0, bytes_accessed=group * length * 1024
        ),
        name="attend_backward",
    )(block_ranges(starts, q_width, wide), q_t, k_t, v_t, o_h, g_h, stat_h, starts)


class Place:
    def __init__(self):
        self.quarters = lax.axis_size("chip")
        self.reps = 2 * self.quarters
        self.shards = lax.axis_size("shard")
        self.chips = self.shards // 4
        self.core = lax.axis_index("core")
        self.quarter = lax.axis_index("chip")
        self.shard = lax.axis_index("shard")
        self.stream = self.shard // self.chips
        self.batch = self.stream // 2
        self.source = self.quarter * 2 + self.stream % 2
        self.chip = self.shard % self.chips

    def across(self, array, key):
        return lax.ppermute(array, "chip", [(i, i ^ key) for i in range(self.quarters)])

    def swap(self, array):
        return lax.ppermute(array, "core", [(0, 1), (1, 0)])

    def moves(self, turn, home):
        pairs = []
        for quarter in range(self.quarters):
            for core in range(2):
                for shard in range(self.shards):
                    batch = turn ^ (shard & 1)
                    member = shard // 2
                    stream = 2 * batch + core
                    start = (quarter * 2 + core) * self.shards + shard
                    end = (
                        (quarter * 2 + member % 2) * self.shards
                        + stream * self.chips
                        + member // 2
                    )
                    if start != end:
                        pairs.append((end, start) if home else (start, end))
        return pairs

    def stays(self, turn):
        batch = turn ^ (self.shard & 1)
        member = self.shard // 2
        end = (2 * batch + self.core) * self.chips + member // 2
        return (member % 2 == self.core) & (end == self.shard)

    def leaving(self, array):
        odd = self.shard % 2 == 1
        return [jnp.where(odd, array[1 - turn], array[turn]) for turn in range(2)]

    def send_streams(self, array):
        return [
            lax.ppermute(part, BOTH, self.moves(turn, False))
            for turn, part in enumerate(self.leaving(array))
        ]

    def join_streams(self, array, got):
        got = [
            jnp.where(self.stays(turn), part, got[turn])
            for turn, part in enumerate(self.leaving(array))
        ]
        swapped = self.batch == 1
        return jnp.concatenate(
            [jnp.where(swapped, got[1], got[0]), jnp.where(swapped, got[0], got[1])], axis=0
        )

    def to_streams(self, array):
        return self.join_streams(array, self.send_streams(array))

    def to_homes(self, array):
        half = array.shape[0] // 2
        swapped = self.batch == 1
        parts = [array[:half], array[half:]]
        got = [
            jnp.where(swapped, parts[1 - turn], parts[turn]) for turn in range(2)
        ]
        got = [
            jnp.where(
                self.stays(turn), part, lax.ppermute(part, BOTH, self.moves(turn, True))
            )
            for turn, part in enumerate(got)
        ]
        odd = self.shard % 2 == 1
        return jnp.stack([jnp.where(odd, got[1], got[0]), jnp.where(odd, got[0], got[1])])

    def ordered(self, mine, other, axis):
        return jnp.where(
            self.core == 0,
            jnp.concatenate([mine, other], axis=axis),
            jnp.concatenate([other, mine], axis=axis),
        )

    def halves(self, array, axis):
        size = array.shape[axis] // 2
        mine = lax.dynamic_slice_in_dim(array, self.core * size, size, axis)
        other = lax.dynamic_slice_in_dim(array, (1 - self.core) * size, size, axis)
        return mine, other

    def head_order(self, pieces, heads):
        if self.chips == 1:
            return jnp.concatenate(pieces, axis=0)
        stacked = jnp.stack([p.reshape(self.chips, -1, p.shape[1]) for p in pieces], axis=1)
        return stacked.reshape(-1, pieces[0].shape[1])

    def chip_exchange(self, array, split, join):
        if self.chips == 1:
            return array
        size = array.shape[split] // self.chips
        width = array.shape[join]
        shape = list(array.shape)
        shape[split] = size
        shape[join] = width * self.chips
        result = jnp.zeros(shape, array.dtype)
        for step in range(self.chips):
            other = self.chip ^ step
            piece = lax.dynamic_slice_in_dim(array, other * size, size, split)
            if step:
                piece = lax.ppermute(
                    piece, "shard", [(i, i ^ step) for i in range(self.shards)]
                )
            result = lax.dynamic_update_slice_in_dim(result, piece, other * width, join)
        return result

    def along(self, array, step):
        return lax.ppermute(
            array, "shard", [(i, (i + step) % self.shards) for i in range(self.shards)]
        )

    def fetch_along(self, own):
        piece = lax.dynamic_index_in_dim(own, self.quarter, 1, keepdims=False)
        return [self.along(piece, step) for step in range(1, self.shards)]

    def fetch_across(self, got):
        got = jnp.stack(got)
        return [got] + [self.across(got, key) for key in range(1, self.quarters)]

    def assemble(self, own, found, widths):
        parts, quarters, rows, _ = own.shape
        shards = self.shards
        places = jnp.stack([self.shard, self.quarter]).astype(jnp.int32)
        edges = [sum(widths[:n]) for n in range(len(widths) + 1)]

        def kernel(places_ref, own_ref, *refs):
            found_refs, out_refs, sem = refs[:quarters], refs[quarters:-1], refs[-1]
            shard, quarter = places_ref[0], places_ref[1]
            copies = []
            for n, out_ref in enumerate(out_refs):
                span = pl.ds(edges[n], widths[n])
                for part in range(parts):
                    copies.append((own_ref.at[part, :, :, span], out_ref.at[part, shard]))
                    for key in range(quarters):
                        for step in range(1, shards):
                            where = (shard - step + shards) % shards
                            copies.append(
                                (
                                    found_refs[key].at[step - 1, part, :, span],
                                    out_ref.at[part, where, quarter ^ key],
                                )
                            )
            copies = [
                pltpu.make_async_copy(source, end, sem.at[n])
                for n, (source, end) in enumerate(copies)
            ]
            for copy in copies:
                copy.start()
            for copy in copies:
                copy.wait()

        whole = pl.pallas_call(
            kernel,
            out_shape=tuple(
                jax.ShapeDtypeStruct((parts, shards, quarters, rows, width), own.dtype)
                for width in widths
            ),
            in_specs=[pl.BlockSpec(memory_space=pltpu.SMEM)]
            + [pl.BlockSpec(memory_space=pl.ANY)] * (quarters + 1),
            out_specs=tuple(pl.BlockSpec(memory_space=pltpu.VMEM) for _ in widths),
            scratch_shapes=[
                pltpu.SemaphoreType.DMA((len(widths) * parts * (1 + quarters * (shards - 1)),))
            ],
            compiler_params=pltpu.CompilerParams(vmem_limit_bytes=24 << 20),
            cost_estimate=pl.CostEstimate(
                flops=0, transcendentals=0, bytes_accessed=own.size * shards * 4
            ),
            name="assemble",
        )(places, own, *found)
        return [part.reshape(parts * shards * quarters * rows, -1) for part in whole]

    def gather_experts(self, w_gate, w_up):
        which = self.quarter * 2 + self.core

        def part(weight):
            size = weight.shape[1] // self.reps
            piece = lax.dynamic_slice_in_dim(weight, which * size, size, 1)
            return piece.reshape(-1, weight.shape[2])

        piece = jnp.concatenate([part(w_gate), part(w_up)], axis=0)
        return lax.all_gather(piece, ("shard", "chip", "core"), axis=0, tiled=False)

    def reduce_across(self, grad):
        got = lax.all_to_all(grad, "chip", 0, 0, tiled=True)
        return jnp.sum(got.astype(F32), axis=0).astype(BF16)

    def by_shard(self, held):
        return jnp.transpose(held.reshape(held.shape[0], self.shards, -1), (1, 0, 2))

    def reduce_along(self, held):
        total = lax.dynamic_index_in_dim(held, self.shard, 0, keepdims=False).astype(F32)
        for step in range(1, self.shards):
            give = lax.dynamic_index_in_dim(
                held, (self.shard + step) % self.shards, 0, keepdims=False
            )
            total = total + self.along(give, step).astype(F32)
        return total.astype(BF16)

    def scatter(self, held):
        return lax.psum_scatter(held, "shard", scatter_dimension=0, tiled=False)

    def gather(self, total):
        whole = lax.all_gather(total, PLANE, axis=0, tiled=False)
        return whole.reshape(self.quarters, 2, *total.shape)


def core_columns(packed, which, core, shards, experts):
    pieces, _, hidden = packed.shape
    rows = packed.shape[1] // 2
    part = hidden // shards // 2
    small = rows // experts
    if part % 128 or small % 16:
        parts = packed[:, which * rows : (which + 1) * rows]
        parts = parts.reshape(pieces, experts, small, shards, 2, part)
        parts = lax.dynamic_index_in_dim(parts, core, 4, keepdims=False)
        return jnp.transpose(parts, (0, 2, 1, 3, 4)).reshape(pieces * small, -1)
    group = 4

    def kernel(core_ref, *refs):
        out_ref = refs[-1]
        for shard in range(shards):
            for piece in range(group):
                for expert in range(experts):
                    column = (expert * shards + shard) * part
                    out_ref[piece * small : (piece + 1) * small, column : column + part] = refs[
                        shard
                    ][piece, expert * small : (expert + 1) * small, :]

    def columns(shard):
        return pl.BlockSpec((group, rows, part), lambda i, c: (i, which, 2 * shard + c[0]))

    return pl.pallas_call(
        kernel,
        out_shape=jax.ShapeDtypeStruct((pieces * small, experts * hidden // 2), packed.dtype),
        grid_spec=pltpu.PrefetchScalarGridSpec(
            num_scalar_prefetch=1,
            grid=(pieces // group,),
            in_specs=[columns(shard) for shard in range(shards)],
            out_specs=pl.BlockSpec(
                (group * small, experts * hidden // 2), lambda i, c: (i, 0)
            ),
        ),
        cost_estimate=pl.CostEstimate(
            flops=0, transcendentals=0, bytes_accessed=packed.size
        ),
        name="core_columns",
    )(core.astype(jnp.int32)[None], *([packed] * shards))


def spread_experts(summed, which, experts, shards):
    quarters, _, _, columns, rows = summed.shape
    hidden = 2 * columns * quarters // experts
    part = hidden // shards // 2
    if part % 128 or quarters != experts:
        piece = jnp.transpose(summed[:, :, which].astype(F32), (1, 0, 2, 3))
        piece = piece.reshape(2, experts, shards, part, rows)
        return jnp.transpose(piece, (1, 4, 2, 0, 3)).reshape(experts, rows, hidden)

    def kernel(in_ref, out_ref):
        for core in range(2):
            turned = in_ref[0, core, 0].astype(F32).T
            for shard in range(shards):
                first = (2 * shard + core) * part
                out_ref[0, :, first : first + part] = turned[:, shard * part : (shard + 1) * part]

    return pl.pallas_call(
        kernel,
        out_shape=jax.ShapeDtypeStruct((experts, rows, hidden), F32),
        grid=(experts,),
        in_specs=[pl.BlockSpec((1, 2, 1, columns, rows), lambda e: (e, 0, which, 0, 0))],
        out_specs=pl.BlockSpec((1, rows, hidden), lambda e: (e, 0, 0)),
        cost_estimate=pl.CostEstimate(
            flops=0, transcendentals=0, bytes_accessed=summed.size * 3
        ),
        name="spread_experts",
    )(summed)


def spread_rows(mine, other, quarter, core, widths):
    quarters, columns, rows = mine.shape
    rest = quarters * columns - sum(widths)
    places = jnp.stack([quarter, core]).astype(jnp.int32)

    def kernel(places_ref, mine_ref, other_ref, *out_refs):
        quarter, core = places_ref[0], places_ref[1]
        for side, ref in enumerate((mine_ref, other_ref)):
            at = core if side == 0 else 1 - core
            whole = jnp.concatenate(
                [ref[n ^ quarter].astype(F32) for n in range(quarters)], axis=0
            )
            first = 0
            for width, out_ref in zip(widths, out_refs):
                span = pl.ds(pl.multiple_of(at * width, 128), width)
                out_ref[:, span] = whole[first : first + width].T
                first += width
            if rest and side == 0:
                out_refs[-1][...] = whole[first:]
            elif rest:
                out_refs[-1][...] += whole[first:]

    shapes = [jax.ShapeDtypeStruct((rows, 2 * width), F32) for width in widths]
    if rest:
        shapes.append(jax.ShapeDtypeStruct((rest, rows), F32))
    return pl.pallas_call(
        kernel,
        out_shape=tuple(shapes),
        in_specs=[
            pl.BlockSpec(memory_space=pltpu.SMEM),
            pl.BlockSpec(memory_space=pltpu.VMEM),
            pl.BlockSpec(memory_space=pltpu.VMEM),
        ],
        out_specs=tuple(pl.BlockSpec(memory_space=pltpu.VMEM) for _ in shapes),
        compiler_params=pltpu.CompilerParams(vmem_limit_bytes=40 << 20),
        cost_estimate=pl.CostEstimate(
            flops=0, transcendentals=0, bytes_accessed=mine.size * 12
        ),
        name="spread_rows",
    )(places, mine, other)


def rms_scale(rows_in):
    return lax.rsqrt(jnp.mean(rows_in * rows_in, axis=-1, keepdims=True) + EPSILON)


def norm_back(rows_in, row_scale, gain_row, grad_normed):
    grad_gain = jnp.sum(grad_normed * rows_in * row_scale, axis=0)
    scaled = grad_normed * gain_row
    scale_cubed = row_scale * row_scale * row_scale
    grad_rows = row_scale * scaled - rows_in * scale_cubed * jnp.mean(
        scaled * rows_in, axis=-1, keepdims=True
    )
    return (grad_rows, grad_gain)


def local(
    tokens,
    cotangent,
    routes,
    lengths,
    attn_gain,
    w_query,
    w_key,
    w_value,
    w_out,
    moe_gain,
    w_router,
    w_gate,
    w_up,
    w_down,
):
    here = Place()
    core, shards, quarters = here.core, here.shards, here.quarters
    experts = w_gate.shape[0]
    features = tokens.shape[3]
    hidden_all = w_gate.shape[2]
    width_q = w_query.shape[1] // 2
    width_k = w_key.shape[1] // 2
    shard_rows = w_query.shape[0]
    rows_q = shard_rows // quarters
    hidden_part = hidden_all // shards // 2
    hidden_core = hidden_all // 2

    def columns_of(weight, width):
        return lax.dynamic_slice_in_dim(weight, core * width, width, 1)

    small = jnp.concatenate([attn_gain[:, None], moe_gain[:, None], w_router], axis=1)
    small = jnp.pad(small, ((0, 0), (0, 128 - small.shape[1])))
    own = jnp.concatenate(
        [
            columns_of(w_query, width_q),
            columns_of(w_key, width_k),
            columns_of(w_value, width_k),
            small,
            columns_of(w_out, features // 2),
        ],
        axis=1,
    ).reshape(1, quarters, rows_q, -1)
    got = here.fetch_along(own)

    tokens, own = together(tokens, own)
    x_own = here.to_streams(tokens[:, 0])
    rows = x_own.shape[0]
    w_gate, *got = together(w_gate, *got)
    packed = here.gather_experts(w_gate, w_up)
    own_down = lax.dynamic_slice_in_dim(w_down, core * hidden_part, hidden_part, 1).reshape(
        experts, quarters, hidden_part // quarters, features
    )
    found = here.fetch_across(got)
    routes, x_own = together(routes, x_own)
    route_own = here.to_streams(routes[:, 0])
    own_down, route_own = together(own_down, route_own)
    got_down = here.fetch_along(own_down)
    qkv_w, small_w, out_w = here.assemble(
        own, found, [width_q + 2 * width_k, 128, features // 2]
    )
    out_w = here.ordered(out_w, here.swap(out_w), 1)
    smalls = small_w[:, : 2 + experts].astype(F32)
    gain_one = smalls[:, 0][None, :]
    gain_two = smalls[:, 1][None, :]
    router_w = small_w[:, 2 : 2 + experts]

    x_wide = x_own.astype(F32)
    scale_one = rms_scale(x_wide)
    normed_own = (x_wide * scale_one * gain_one).astype(BF16)
    normed = here.ordered(normed_own, here.swap(normed_own), 0)
    route_all = jnp.concatenate([route_own, here.swap(route_own)], axis=0)
    qkv_t = dot(qkv_w, normed, 0, 1, BF16)
    q_t, k_t, v_t = qkv_t[:width_q], qkv_t[width_q : width_q + width_k], qkv_t[width_q + width_k :]
    q_t, k_t, v_t = (here.chip_exchange(part, 0, 1) for part in (q_t, k_t, v_t))
    length = q_t.shape[1]

    my_lengths = lax.dynamic_index_in_dim(
        lax.dynamic_index_in_dim(lengths, here.batch, 0, keepdims=False),
        here.source,
        0,
        keepdims=False,
    )
    ends = jnp.cumsum(my_lengths)[:-1]
    positions = jnp.arange(length, dtype=jnp.int32)
    starts = jnp.max(
        jnp.where(ends[:, None] <= positions[None, :], ends[:, None], 0), axis=0, keepdims=True
    ).astype(jnp.int32)
    heads = k_t.shape[0] // HEAD
    o_heads, stats, o_mine, o_got = [], [], [], []
    for head in range(heads):
        source = k_t
        if head == 0:
            source, route_all = together(k_t, route_all)
        else:
            source, stats[-1] = together(k_t, stats[-1])
        o_h, stat = attend_forward(head, q_t, source, v_t, starts)
        o_heads.append(o_h)
        stats.append(stat)
        if head == 1:
            *got_down, stats[-1] = together(*got_down, stats[-1])
            found_down = here.fetch_across(got_down)
        mine, other = here.halves(here.chip_exchange(o_h, 1, 0), 1)
        o_mine.append(mine)
        o_got.append(here.swap(other))
    o_own = here.ordered(
        here.head_order(o_mine, heads), here.head_order(o_got, heads), 0
    )
    gate_w = core_columns(packed, 0, core, shards, experts)
    up_w = core_columns(packed, 1, core, shards, experts)
    h_own = x_wide + dot(o_own, out_w, 0, 0)

    scale_two = rms_scale(h_own)
    b_own = (h_own * scale_two * gain_two).astype(BF16)
    b_all = jnp.concatenate([b_own, here.swap(b_own)], axis=0)
    cotangent, gate_w = together(cotangent, gate_w)
    dy_blocks = here.send_streams(cotangent[:, 0])

    logits = dot(b_all, router_w, 1, 0)
    route_hot = (
        route_all[:, :, None] == jnp.arange(experts, dtype=jnp.int32)[None, None, :]
    ).astype(F32)
    chosen = jnp.sum(logits[:, None, :] * route_hot, axis=2)
    gate_share = jax.nn.softmax(chosen, axis=1)
    shares = jnp.sum(gate_share[:, :, None] * route_hot, axis=1)
    share_wide = jnp.repeat(shares, hidden_core, axis=1)

    gate_v = dot(b_all, gate_w, 1, 0, BF16)
    *found_down, gate_v = together(*found_down, gate_v)
    down_w = here.assemble(own_down, found_down, [features])[0]
    up_v = dot(b_all, up_w, 1, 0, BF16)
    *dy_blocks, up_v = together(*dy_blocks, up_v)
    dy_own = here.join_streams(cotangent[:, 0], dy_blocks)
    dy_all = jnp.concatenate([dy_own, here.swap(dy_own)], axis=0)
    gate_f, up_f = gate_v.astype(F32), up_v.astype(F32)
    squashed = jax.nn.sigmoid(gate_f)
    mid = (gate_f * squashed * up_f * share_wide).astype(BF16)
    y_other = dot(mid[rows:], down_w, 1, 0, BF16)
    y_got = here.swap(y_other)
    y_own = dot(mid[:rows], down_w, 1, 0)
    block_own = (h_own + y_own + y_got.astype(F32)).astype(BF16)
    block_out = here.to_homes(block_own)

    slope = dot(dy_all, down_w, 1, 1)
    grad_down = dot(mid, dy_all, 0, 0, BF16)
    if quarters == experts:
        grad_down = grad_down.reshape(quarters, shards, hidden_part, features)
    else:
        grad_down = jnp.transpose(
            grad_down.reshape(experts, shards, hidden_part, quarters, features // quarters),
            (3, 1, 0, 2, 4),
        )
    held_down = here.reduce_across(grad_down)
    active = gate_f * squashed
    grad_share = jnp.sum((slope * active * up_f).reshape(2 * rows, experts, hidden_core), axis=2)
    scaled = slope * share_wide
    grad_gate_v = (scaled * up_f * squashed * (1.0 + gate_f * (1.0 - squashed))).astype(BF16)
    grad_up_v = (scaled * active).astype(BF16)
    share_got = here.swap(grad_share[rows:])
    grad_share = grad_share[:rows] + share_got

    def expert_grad(back):
        return dot(back, b_all, 0, 0, BF16).reshape(quarters, -1, features)

    grad_gate = expert_grad(grad_gate_v)
    grad_up = expert_grad(grad_up_v)
    grad_gate_v, grad_up_v, grad_gate, grad_up = together(
        grad_gate_v, grad_up_v, grad_gate, grad_up
    )
    db_other = (
        dot(grad_gate_v[rows:], gate_w, 1, 1) + dot(grad_up_v[rows:], up_w, 1, 1)
    ).astype(BF16)
    db_got = here.swap(db_other)
    db_got, held_down = together(db_got, held_down)
    db_own = dot(grad_gate_v[:rows], gate_w, 1, 1) + dot(grad_up_v[:rows], up_w, 1, 1)

    hot_own, share_own = route_hot[:rows], gate_share[:rows]
    grad_gates = jnp.sum(grad_share[:, None, :] * hot_own, axis=2)
    grad_chosen = share_own * (
        grad_gates - jnp.sum(share_own * grad_gates, axis=1, keepdims=True)
    )
    grad_logits = jnp.sum(grad_chosen[:, :, None] * hot_own, axis=1).astype(BF16)
    grad_router = dot(grad_logits, b_own, 0, 0)
    db = db_own + db_got.astype(F32) + dot(grad_logits, router_w, 1, 1)
    dh, grad_gain_two = norm_back(h_own, scale_two, gain_two, db)
    dh = dh + dy_own.astype(F32)
    dattn = dh.astype(BF16)

    dattn, grad_gate = together(dattn, grad_gate)
    held_gate = here.by_shard(here.reduce_across(grad_gate))
    do_t = dot(out_w, dattn, 1, 1, BF16)
    do_mine, do_other = here.halves(do_t, 0)
    do_t = here.ordered(do_mine, here.swap(do_other), 1)
    do_t = here.chip_exchange(do_t, 0, 1)
    grad_out = dot(dattn, o_own, 0, 1, BF16)
    out_mine, out_other = here.halves(grad_out, 0)
    grad_out = (out_mine.astype(F32) + here.swap(out_other).astype(F32)).astype(BF16)
    back_heads, back_rows, back_got = [], [], []
    for head in range(heads):
        g_h = do_t[head * o_heads[0].shape[0] : (head + 1) * o_heads[0].shape[0]]
        if head == 1:
            g_h, block_out, held_gate, grad_up, grad_out, back_heads[0] = together(
                g_h, block_out, held_gate, grad_up, grad_out, back_heads[0]
            )
            cut = grad_up.shape[1]
            held_both = here.reduce_across(
                jnp.concatenate([grad_up, grad_out.reshape(quarters, -1, features)], axis=1)
            )
        elif head:
            g_h, back_heads[-1] = together(g_h, back_heads[-1])
        parts = attend_backward(head, q_t, k_t, v_t, o_heads[head], g_h, stats[head], starts)
        parts = [here.chip_exchange(part, 1, 0) for part in parts]
        back_heads.append(parts)
        back_h = jnp.concatenate(parts, axis=0)
        mine, other = here.halves(back_h, 1)
        back_rows.append(mine)
        back_got.append(here.swap(other))

    def all_heads(which):
        return here.head_order([parts[which] for parts in back_heads], heads)

    back_t = jnp.concatenate([all_heads(0), all_heads(1), all_heads(2)], axis=0)
    qkv_w_got = here.swap(qkv_w)
    sizes = [parts.shape[0] for parts in back_heads[0]]

    def regroup(pieces):
        edges = [0, sizes[0], sizes[0] + sizes[1], sum(sizes)]
        return jnp.concatenate(
            [
                here.head_order([piece[edges[n] : edges[n + 1]] for piece in pieces], heads)
                for n in range(3)
            ],
            axis=0,
        )

    da = dot(regroup(back_rows), qkv_w, 0, 1) + dot(regroup(back_got), qkv_w_got, 0, 1)
    grad_qkv = dot(back_t, normed, 1, 0, BF16)
    dx, grad_gain_one = norm_back(x_wide, scale_one, gain_one, da)
    input_grad = here.to_homes((dx + dh).astype(BF16))

    grad_small = jnp.concatenate([grad_gain_one[None], grad_gain_two[None], grad_router], axis=0)
    grad_small = jnp.pad(grad_small, ((0, 64 - grad_small.shape[0]), (0, 0))).astype(BF16)
    grad_qkv = jnp.concatenate([grad_qkv, grad_small], axis=0).reshape(quarters, -1, features)
    grad_qkv, held_both = together(grad_qkv, held_both)
    held_up = here.by_shard(held_both[:cut])
    held_out = here.by_shard(held_both[cut:])
    held_qkv = here.by_shard(here.reduce_across(grad_qkv))
    sum_down = here.gather(here.scatter(held_down))
    sum_gate_up = here.gather(jnp.stack([here.scatter(held_gate), here.scatter(held_up)]))
    sum_out = here.gather(here.scatter(held_out))
    total = here.reduce_along(held_qkv)
    mine = jnp.stack([total] + [here.across(total, key) for key in range(1, quarters)])
    out_query, out_key, out_value, small_sum = spread_rows(
        mine, here.swap(mine), here.quarter, core, [width_q, width_k, width_k]
    )
    out_out = jnp.transpose(sum_out.astype(F32), (3, 1, 0, 2)).reshape(shard_rows, features)
    if quarters == experts:
        out_down = sum_down.astype(F32).reshape(experts, 2 * hidden_part, features)
    else:
        out_down = jnp.transpose(sum_down.astype(F32), (2, 1, 3, 0, 4)).reshape(
            experts, 2 * hidden_part, features
        )
    return (
        block_out[:, None],
        input_grad[:, None],
        small_sum[0],
        out_query,
        out_key,
        out_value,
        out_out,
        small_sum[1],
        small_sum[2 : 2 + experts].T,
        spread_experts(sum_gate_up, 0, experts, shards),
        spread_experts(sum_gate_up, 1, experts, shards),
        out_down,
    )


def solution(mesh):
    chips = mesh.shape["rep"] // 2
    mesh = jax.sharding.Mesh(
        mesh.devices.reshape(chips, 2, mesh.shape["shard"]), ("chip", "core", "shard")
    )
    in_specs = (
        P(None, PLANE, "shard", None),
        P(None, PLANE, "shard", None),
        P(None, PLANE, "shard", None),
        P(),
        P("shard"),
        P("shard", None),
        P("shard", None),
        P("shard", None),
        P("shard", None),
        P("shard"),
        P("shard", None),
        P(None, "shard", None),
        P(None, "shard", None),
        P(None, "shard", None),
    )
    out_specs = (
        P(None, PLANE, "shard", None),
        P(None, PLANE, "shard", None),
        P("shard"),
        P("shard", None),
        P("shard", None),
        P("shard", None),
        P("shard", None),
        P("shard"),
        P("shard", None),
        P(None, "shard", None),
        P(None, "shard", None),
        P(None, "shard", None),
    )
    return jax.shard_map(local, mesh=mesh, in_specs=in_specs, out_specs=out_specs, check_vma=False)
```

time: 1610 us -> 1250 us (0.78); the launches traced: 1580 us -> 1250 us
  waiting for transfers between devices: 509 us -> 300 us
  starting transfers between devices: 276 us -> 190 us
  local copies, waits for them, and re-layouts: 174 us -> 139 us
    ppermute x121 -> x48, waiting for transfers between devices: 508 us -> 134 us  [the longest x6 59.1 us: send_streams(): lax.ppermute(part, BOTH, self.moves(turn, False))]
    ppermute x121 -> x48, starting transfers between devices: 276 us -> 168 us  [the longest x20 106 us: swap(): return lax.ppermute(array, 'core', [(0, 1), (1, 0)])]
    reduce_scatter x0 -> x4, waiting for transfers between devices: none -> 89.5 us  [scatter(): return lax.psum_scatter(held, 'shard', scatter_dimension=0, tiled=False)]
    all_to_all x0 -> x4, waiting for transfers between devices: none -> 63.2 us  [reduce_across(): got = lax.all_to_all(grad, 'chip', 0, 0, tiled=True)]
    reshape x13 -> x4, local copies, waits for them, and re-layouts: 75.7 us -> 24.6 us  [the longest x1 20.4 us: local(): (slope * active * up_f).reshape(2 * rows, experts, hidden_core)]
    unnamed x271 -> x258, local copies, waits for them, and re-layouts: 25.9 us -> 63.3 us
    dynamic_slice x14 -> x2, local copies, waits for them, and re-layouts: 37.8 us -> 2.04 us  [part(): piece = lax.dynamic_slice_in_dim(weight, which * size, size, 1)]
    all_to_all x0 -> x4, starting transfers between devices: none -> 21.5 us  [reduce_across(): got = lax.all_to_all(grad, 'chip', 0, 0, tiled=True)]
  transfers between devices with their start and end apart: 126 -> 60, of which waited for: 37 -> 18; matrix products, arithmetic and copies ran while one was open for 34% -> 39% of each run, Pallas kernels for 13% -> 16%
where the time goes in v2:
time: 1250 us
  waiting for transfers between devices  300 us (24%)
  matrix products  281 us (22%)
  Pallas kernels  212 us (17%)
  starting transfers between devices  190 us (15%)
  local copies, waits for them, and re-layouts  139 us (11%)
  other arithmetic  107 us (9%)
  between operations  16.3 us (1%)
    dot_general x22, matrix products, dot(): lax.dot_general(left, right, (((left_dim,), (right_dim,)), ((), ())), pre...  281 us
    pallas_call x4, Pallas kernels, attend_backward(): pl.pallas_call(functools.partial(backward_kernel, group=group, wide=wide)...  109 us
    ppermute x20, starting transfers between devices, swap(): return lax.ppermute(array, 'core', [(0, 1), (1, 0)])  106 us
    reduce_scatter x4, waiting for transfers between devices, scatter(): return lax.psum_scatter(held, 'shard', scatter_dimension=0, tiled=False)  89.5 us
    pallas_call x4, Pallas kernels, attend_forward(): pl.pallas_call(functools.partial(forward_kernel, group=group, wide=wide),...  66.5 us
    unnamed x258, local copies, waits for them, and re-layouts  63.3 us
    all_to_all x4, waiting for transfers between devices, reduce_across(): got = lax.all_to_all(grad, 'chip', 0, 0, tiled=True)  63.2 us
    ppermute x6, waiting for transfers between devices, send_streams(): lax.ppermute(part, BOTH, self.moves(turn, False))  59.1 us
  transfers between devices with their start and end apart: 60, of which 18 were waited for; matrix products, arithmetic and copies ran while one was open for 39% of the time, Pallas kernels for 16%

profile of v2, /device:TPU:0, one launch (start us, length us, event | category | flops | bytes accessed | tf_op | source)
XLA Modules:
  0.0 1245.2 jit_solution(14999488783921726675)
XLA Ops:
  35.2 17.1 %collective-permute-done.1 = bf16[1,96,2176]{2,1,0:T(8,128)(2,1)} collective-permute-done((bf16[1,96,2176]{2,1,0:T(8,128)(2,1)}, bf16[1,96,2176]{2,1,0:T(8,128)(2,1)}, u32[]{:S(2)}, u32[]{:S(2)}) %collective-permute-start.1) | collective-permute-done | bytes 417824 | tf_op jit(solution)/shard_map/ppermute | solution.py:366
  73.4 42.4 %collective-permute-done.7 = bf16[512,1536]{1,0:T(8,128)(2,1)} collective-permute-done((bf16[512,1536]{1,0:T(8,128)(2,1)}, bf16[512,1536]{1,0:T(8,128)(2,1)}, u32[]{:S(2)}, u32[]{:S(2)}) %collective-permute-start.7) | collective-permute-done | bytes 1572896 | tf_op jit(solution)/shard_map/ppermute | solution.py:294
  144.2 60.6 %collective-permute-start.9 = (bf16[1024,1536]{1,0:T(8,128)(2,1)}, bf16[1024,1536]{1,0:T(8,128)(2,1)}, u32[]{:S(2)}, u32[]{:S(2)}) collective-permute-start(bf16[1024,1536]{1,0:T(8,128)(2,1)} %fusion.11), channel_id=1, source_target_pairs={{0,4},{4,0},{1,5},{5,1},{2,6},{6,2},{3,7},{7,3},{8,12},{12,8},{9,1... | collective-permute-start | bytes 9437192 | tf_op jit(solution)/shard_map/ppermute | solution.py:262
  228.7 16.7 %convolution_convert_fusion.3 = bf16[1280,2048]{1,0:T(8,128)(2,1)} fusion(bf16[1536,1280]{1,0:T(8,128)(2,1)} %bitcast.148, bf16[1024,1536]{1,0:T(8,128)(2,1)} %collective-permute-done.9, bf16[1024,1536]{1,0:T(8,128)(2,1)} %fusion.11, pred[]{:T(512)S(6)} %eq.41), kind=kOutput, calls=%fused_computation.26 | convolution fusion | flops 8083996672 | bytes 15466497 | tf_op jit(solution)/shard_map/dot_general | solution.py:27
  250.1 16.6 %attend_forward.4 = (bf16[192,2048]{1,0:T(8,128)(2,1)S(1)}, f32[1,3,2048]{2,1,0:T(4,128)S(1)}) custom-call(s32[4,4]{1,0:T(4,128)S(1)} %pad_add_fusion.2.ranges, bf16[768,2048]{1,0:T(8,128)(2,1)S(1)} %slice.294.q_ref, bf16[256,2048]{1,0:T(8,128)(2,1)S(1)} %get-tuple-element.119.k_ref, bf16[256,2048]{1,0:T(8,128)(2,1)S(1)} %get-tuple-element.282.v_ref, ...), custom_call_target="tpu_custom_call" | custom-call | flops 1610612736 | bytes 3145728 | tf_op jit(solution)/shard_map/attend_forward/pallas_call | solution.py:184
  283.9 16.9 %attend_forward.6 = (bf16[192,2048]{1,0:T(8,128)(2,1)S(1)}, f32[1,3,2048]{2,1,0:T(4,128)S(1)}) custom-call(s32[4,4]{1,0:T(4,128)S(1)} %pad_add_fusion.2.ranges, bf16[768,2048]{1,0:T(8,128)(2,1)S(1)} %slice.294.q_ref, bf16[256,2048]{1,0:T(8,128)(2,1)S(1)} %get-tuple-element.119.k_ref, bf16[256,2048]{1,0:T(8,128)(2,1)S(1)} %get-tuple-element.282.v_ref, ...), custom_call_target="tpu_custom_call" | custom-call | flops 1610612736 | bytes 3145728 | tf_op jit(solution)/shard_map/attend_forward/pallas_call | solution.py:184
  304.3 16.6 %attend_forward.7 = (bf16[192,2048]{1,0:T(8,128)(2,1)S(1)}, f32[1,3,2048]{2,1,0:T(4,128)S(1)}) custom-call(s32[4,4]{1,0:T(4,128)S(1)} %pad_add_fusion.2.ranges, bf16[768,2048]{1,0:T(8,128)(2,1)S(1)} %slice.294.q_ref, bf16[256,2048]{1,0:T(8,128)(2,1)S(1)} %get-tuple-element.119.k_ref, bf16[256,2048]{1,0:T(8,128)(2,1)S(1)} %get-tuple-element.282.v_ref, ...), custom_call_target="tpu_custom_call" | custom-call | flops 1610612736 | bytes 3145728 | tf_op jit(solution)/shard_map/attend_forward/pallas_call | solution.py:184
  388.7 18.4 %convolution_convert_fusion.2 = bf16[2048,2048]{1,0:T(8,128)(2,1)} fusion(bf16[1536,2048]{1,0:T(8,128)(2,1)S(1)} %copy-done.57, bf16[1024,1536]{1,0:T(8,128)(2,1)} %collective-permute-done.22, bf16[1024,1536]{1,0:T(8,128)(2,1)} %multiply_convert_fusion.1), kind=kOutput, calls=%fused_computation.25 | convolution fusion | flops 12901679104 | bytes 20971520 | tf_op jit(solution)/shard_map/dot_general | solution.py:27
  426.6 35.6 %collective-permute-start.23 = (bf16[1024,1536]{1,0:T(8,128)(2,1)}, bf16[1024,1536]{1,0:T(8,128)(2,1)}, u32[]{:S(2)}, u32[]{:S(2)}) collective-permute-start(bf16[1024,1536]{1,0:T(8,128)(2,1)} %pad_maximum_fusion.5), channel_id=1, source_target_pairs={{0,4},{4,0},{1,5},{5,1},{2,6},{6,2},{3,7},{7,3},{8,12},{12,8},{9,1... | collective-permute-start | bytes 9437192 | tf_op jit(solution)/shard_map/ppermute | solution.py:262
  476.7 18.2 %convolution_convert_fusion.1 = bf16[2048,2048]{1,0:T(8,128)(2,1)} fusion(bf16[1536,2048]{1,0:T(8,128)(2,1)S(1)} %bitcast.170, bf16[1024,1536]{1,0:T(8,128)(2,1)} %collective-permute-done.22, bf16[1024,1536]{1,0:T(8,128)(2,1)} %multiply_convert_fusion.1), kind=kOutput, calls=%fused_computation.24 | convolution fusion | flops 12901679104 | bytes 20971520 | tf_op jit(solution)/shard_map/dot_general | solution.py:27
  502.3 36.9 %multiply_convert_fusion = (bf16[2048,2048]{1,0:T(8,128)(2,1)}, bf16[2048,2048]{1,0:T(8,128)(2,1)}, f32[2048,2048]{1,0:T(8,128)}, bf16[2048,2048]{1,0:T(8,128)(2,1)}) fusion(f32[2048,2048]{1,0:T(8,128)} %bitcast.165, bf16[2048,2048]{1,0:T(8,128)(2,1)} %convolution_convert_fusion.1, bf16[2048,2048]{1,0:T(8,128)(2,1)} %convolution_convert_fusion.2, ...), kind=kOutput, calls=%fused_computation.15 | convolution fusion | flops 12991856640 | bytes 88080384 | tf_op jit(solution)/shard_map/dot_general | solution.py:27
  539.2 19.3 %convolution_convert_fusion.6 = bf16[2048,1536]{1,0:T(8,128)(2,1)} fusion(bf16[2048,2048]{1,0:T(8,128)(2,1)} %get-tuple-element.137, bf16[1024,1536]{1,0:T(8,128)(2,1)} %collective-permute-done.22, bf16[1024,1536]{1,0:T(8,128)(2,1)} %multiply_convert_fusion.1), kind=kOutput, calls=%fused_computation.29 | convolution fusion | flops 12900630528 | bytes 20971520 | tf_op jit(solution)/shard_map/dot_general | solution.py:27
  558.6 19.5 %convolution_convert_fusion.7 = bf16[2048,1536]{1,0:T(8,128)(2,1)} fusion(bf16[2048,2048]{1,0:T(8,128)(2,1)} %get-tuple-element.136, bf16[1024,1536]{1,0:T(8,128)(2,1)} %collective-permute-done.22, bf16[1024,1536]{1,0:T(8,128)(2,1)} %multiply_convert_fusion.1), kind=kOutput, calls=%fused_computation.30 | convolution fusion | flops 12900630528 | bytes 20971520 | tf_op jit(solution)/shard_map/dot_general | solution.py:27
  596.5 17.0 %convolution_convert_fusion.5 = bf16[2048,1536]{1,0:T(8,128)(2,1)} fusion(bf16[2048,2048]{1,0:T(8,128)(2,1)S(1)} %bitcast.199, bf16[1024,1536]{1,0:T(8,128)(2,1)} %collective-permute-done.23, bf16[512,1536]{1,0:T(8,128)(2,1)S(1)} %copy-done.55, bf16[512,1536]{1,0:T(8,128)(2,1)S(1)} %copy-done.52), kind=kOutput, calls=%fused_computation.28 | convolution fusion | flops 12906921984 | bytes 20971520 | tf_op jit(solution)/shard_map/dot_general | solution.py:27
  640.3 20.4 %reshape.708 = f32[2048,4,512]{2,1,0:T(4,128)} reshape(f32[2048,2048]{1,0:T(8,128)} %get-tuple-element.272) | data formatting | bytes 33554432 | tf_op jit(solution)/shard_map/reshape | solution.py:747
  759.0 27.1 %attend_backward.4 = (bf16[192,2048]{1,0:T(8,128)(2,1)S(1)}, bf16[64,2048]{1,0:T(8,128)(2,1)S(1)}, bf16[64,2048]{1,0:T(8,128)(2,1)S(1)}) custom-call(s32[4,4]{1,0:T(4,128)S(1)} %pad_add_fusion.3.ranges, bf16[768,2048]{1,0:T(8,128)(2,1)S(1)} %copy-done.6, bf16[256,2048]{1,0:T(8,128)(2,1)S(1)} %copy-done.17, bf16[256,2048]{1,0:T(8,128)(2,1)S(1)} %copy-done.14, ...), custom_call_target="tpu_custom_call" | custom-call | flops 4026531840 | bytes 6291456 | tf_op jit(solution)/shard_map/attend_backward/pallas_call | solution.py:215
  838.4 27.3 %attend_backward.5 = (bf16[192,2048]{1,0:T(8,128)(2,1)S(1)}, bf16[64,2048]{1,0:T(8,128)(2,1)S(1)}, bf16[64,2048]{1,0:T(8,128)(2,1)S(1)}) custom-call(s32[4,4]{1,0:T(4,128)S(1)} %pad_add_fusion.3.ranges, bf16[768,2048]{1,0:T(8,128)(2,1)S(1)} %copy-done.6, bf16[256,2048]{1,0:T(8,128)(2,1)S(1)} %copy-done.18, bf16[256,2048]{1,0:T(8,128)(2,1)S(1)} %copy-done.15, ...), custom_call_target="tpu_custom_call" | custom-call | flops 4026531840 | bytes 6291456 | tf_op jit(solution)/shard_map/attend_backward/pallas_call | solution.py:215
  865.9 27.1 %attend_backward.6 = (bf16[192,2048]{1,0:T(8,128)(2,1)S(1)}, bf16[64,2048]{1,0:T(8,128)(2,1)S(1)}, bf16[64,2048]{1,0:T(8,128)(2,1)S(1)}) custom-call(s32[4,4]{1,0:T(4,128)S(1)} %pad_add_fusion.3.ranges, bf16[768,2048]{1,0:T(8,128)(2,1)S(1)} %copy-done.6, bf16[256,2048]{1,0:T(8,128)(2,1)S(1)} %copy-done.18, bf16[256,2048]{1,0:T(8,128)(2,1)S(1)} %copy-done.15, ...), custom_call_target="tpu_custom_call" | custom-call | flops 4026531840 | bytes 6291456 | tf_op jit(solution)/shard_map/attend_backward/pallas_call | solution.py:215
  894.4 27.5 %attend_backward.7 = (bf16[192,2048]{1,0:T(8,128)(2,1)S(1)}, bf16[64,2048]{1,0:T(8,128)(2,1)S(1)}, bf16[64,2048]{1,0:T(8,128)(2,1)S(1)}) custom-call(s32[4,4]{1,0:T(4,128)S(1)} %pad_add_fusion.3.ranges, bf16[768,2048]{1,0:T(8,128)(2,1)S(1)} %copy-done.6, bf16[256,2048]{1,0:T(8,128)(2,1)S(1)} %copy-done.18, bf16[256,2048]{1,0:T(8,128)(2,1)S(1)} %copy-done.15, ...), custom_call_target="tpu_custom_call" | custom-call | flops 4026531840 | bytes 6291456 | tf_op jit(solution)/shard_map/attend_backward/pallas_call | solution.py:215
  987.4 16.7 %reduce-scatter.5.cloned.1.call-done = bf16[1,192,384]{2,1,0:T(8,128)(2,1)} async-done(((bf16[4,192,384]{2,1,0:T(8,128)(2,1)}), bf16[1,192,384]{2,1,0:T(8,128)(2,1)}) %reduce-scatter.5.cloned.1.call-update) | async-done | bytes 147472 | tf_op jit(solution)/shard_map/reduce_scatter | solution.py:458
  1004.2 35.8 %reduce-scatter.7.cloned.1.call-done = bf16[1,512,384]{1,2,0:T(8,128)(2,1)} async-done(((bf16[4,512,384]{1,2,0:T(8,128)(2,1)}), bf16[1,512,384]{1,2,0:T(8,128)(2,1)}) %reduce-scatter.7.cloned.1.call-update) | async-done | bytes 393232 | tf_op jit(solution)/shard_map/reduce_scatter | solution.py:458
  1040.0 37.0 %reduce-scatter.9.cloned.1.call-done = bf16[1,512,384]{1,2,0:T(8,128)(2,1)} async-done(((bf16[4,512,384]{1,2,0:T(8,128)(2,1)}), bf16[1,512,384]{1,2,0:T(8,128)(2,1)}) %reduce-scatter.9.cloned.1.call-update) | async-done | bytes 393232 | tf_op jit(solution)/shard_map/reduce_scatter | solution.py:458
  1096.3 48.8 %all-to-all-done.3 = bf16[4,336,1536]{2,1,0:T(8,128)(2,1)} async-done(((bf16[4,336,1536]{2,1,0:T(8,128)(2,1)}), bf16[4,336,1536]{2,1,0:T(8,128)(2,1)}, u32[]{:S(2)}, u32[]{:S(2)}) %all-to-all-start.3) | async-done | bytes 4128800 | tf_op jit(solution)/shard_map/all_to_all | solution.py:442
  1162.0 23.4 %collective-permute-done.42 = bf16[336,384]{1,0:T(8,128)(2,1)S(1)} collective-permute-done((bf16[336,384]{1,0:T(8,128)(2,1)S(1)}, bf16[336,384]{1,0:T(8,128)(2,1)S(1)}, u32[]{:S(2)}, u32[]{:S(2)}) %collective-permute-start.42) | collective-permute-done | bytes 258080 | tf_op jit(solution)/shard_map/ppermute | solution.py:366
  (526 shorter events, 585.9 us)
Async XLA Ops:
  7.2 348.4 %all-gather.11.cloned.1.call-start = ((), (), s32[]{:S(2)}) async-start(), calls=%async_computation.14 | async-start | bytes 25952256 | tf_op jit(solution)/shard_map/all_gather | solution.py:439
  72.9 60.3 %collective-permute-start.5 = (bf16[3,1,96,2176]{3,2,1,0:T(8,128)(2,1)S(1)}, bf16[3,1,96,2176]{3,2,1,0:T(8,128)(2,1)S(1)}, u32[]{:S(2)}, u32[]{:S(2)}) collective-permute-start(bf16[3,1,96,2176]{3,2,1,0:T(8,128)(2,1)S(1)} %pad_maximum_fusion.9.refs_0_), channel_id=1, source_target_pairs={{0,24},{8,16},{16,8},{24,0},{1,25},{9,17},{17,9},{25,1},{2,26},{10... | collective-permute-start | bytes 3760136 | tf_op jit(solution)/shard_map/ppermute | solution.py:259
  144.2 84.6 %collective-permute-start.9 = (bf16[1024,1536]{1,0:T(8,128)(2,1)}, bf16[1024,1536]{1,0:T(8,128)(2,1)}, u32[]{:S(2)}, u32[]{:S(2)}) collective-permute-start(bf16[1024,1536]{1,0:T(8,128)(2,1)} %fusion.11), channel_id=1, source_target_pairs={{0,4},{4,0},{1,5},{5,1},{2,6},{6,2},{3,7},{7,3},{8,12},{12,8},{9,1... | collective-permute-start | bytes 9437192 | tf_op jit(solution)/shard_map/ppermute | solution.py:262
  224.7 59.2 %collective-permute-start.13 = (bf16[4,32,1536]{2,1,0:T(8,128)(2,1)S(1)}, bf16[4,32,1536]{2,1,0:T(8,128)(2,1)S(1)}, u32[]{:S(2)}, u32[]{:S(2)}) collective-permute-start(bf16[4,32,1536]{2,1,0:T(8,128)(2,1)S(1)} %dynamic-slice_bitcast_fusion.1), channel_id=1, source_target_pairs={{0,1},{1,2},{2,3},{3,0},{4,5},{5,6},{6,7},{7,4},{8,9},{9,10},{10,1... | collective-permute-start | bytes 1179656 | tf_op jit(solution)/shard_map/ppermute | solution.py:366
  228.7 101.9 %collective-permute-start.6 = (bf16[1536,768]{1,0:T(8,128)(2,1)}, bf16[1536,768]{1,0:T(8,128)(2,1)}, u32[]{:S(2)}, u32[]{:S(2)}) collective-permute-start(bf16[1536,768]{1,0:T(8,128)(2,1)} %bitcast.151), channel_id=1, source_target_pairs={{0,4},{4,0},{1,5},{5,1},{2,6},{6,2},{3,7},{7,3},{8,12},{12,8},{9,1... | collective-permute-start | bytes 7077896 | tf_op jit(solution)/shard_map/ppermute | solution.py:262
  346.0 601.4 %collective-permute-start.38 = (bf16[1536,1280]{1,0:T(8,128)(2,1)}, bf16[1536,1280]{1,0:T(8,128)(2,1)}, u32[]{:S(2)}, u32[]{:S(2)}) collective-permute-start(bf16[1536,1280]{1,0:T(8,128)(2,1)} %bitcast.149), channel_id=1, source_target_pairs={{0,4},{4,0},{1,5},{5,1},{2,6},{6,2},{3,7},{7,3},{8,12},{12,8},{9,1... | collective-permute-start | bytes 11796488 | tf_op jit(solution)/shard_map/ppermute | solution.py:262
  346.3 148.7 %collective-permute-start.24 = (bf16[3,4,32,1536]{3,2,1,0:T(8,128)(2,1)S(1)}, bf16[3,4,32,1536]{3,2,1,0:T(8,128)(2,1)}, u32[]{:S(2)}, u32[]{:S(2)}) collective-permute-start(bf16[3,4,32,1536]{3,2,1,0:T(8,128)(2,1)S(1)} %pad_maximum_fusion.10.refs_0_), channel_id=1, source_target_pairs={{0,8},{8,0},{16,24},{24,16},{1,9},{9,1},{17,25},{25,17},{2,10},{10... | collective-permute-start | bytes 3538952 | tf_op jit(solution)/shard_map/ppermute | solution.py:259
  346.4 148.6 %collective-permute-start.25 = (bf16[3,4,32,1536]{3,2,1,0:T(8,128)(2,1)S(1)}, bf16[3,4,32,1536]{3,2,1,0:T(8,128)(2,1)}, u32[]{:S(2)}, u32[]{:S(2)}) collective-permute-start(bf16[3,4,32,1536]{3,2,1,0:T(8,128)(2,1)S(1)} %pad_maximum_fusion.10.refs_0_), channel_id=1, source_target_pairs={{0,16},{8,24},{16,0},{24,8},{1,17},{9,25},{17,1},{25,9},{2,18},{10... | collective-permute-start | bytes 3538952 | tf_op jit(solution)/shard_map/ppermute | solution.py:259
  407.1 87.9 %collective-permute-start.26 = (bf16[3,4,32,1536]{3,2,1,0:T(8,128)(2,1)S(1)}, bf16[3,4,32,1536]{3,2,1,0:T(8,128)(2,1)}, u32[]{:S(2)}, u32[]{:S(2)}) collective-permute-start(bf16[3,4,32,1536]{3,2,1,0:T(8,128)(2,1)S(1)} %pad_maximum_fusion.10.refs_0_), channel_id=1, source_target_pairs={{0,24},{8,16},{16,8},{24,0},{1,25},{9,17},{17,9},{25,1},{2,26},{10... | collective-permute-start | bytes 3538952 | tf_op jit(solution)/shard_map/ppermute | solution.py:259
  426.6 75.8 %collective-permute-start.23 = (bf16[1024,1536]{1,0:T(8,128)(2,1)}, bf16[1024,1536]{1,0:T(8,128)(2,1)}, u32[]{:S(2)}, u32[]{:S(2)}) collective-permute-start(bf16[1024,1536]{1,0:T(8,128)(2,1)} %pad_maximum_fusion.5), channel_id=1, source_target_pairs={{0,4},{4,0},{1,5},{5,1},{2,6},{6,2},{3,7},{7,3},{8,12},{12,8},{9,1... | collective-permute-start | bytes 9437192 | tf_op jit(solution)/shard_map/ppermute | solution.py:262
  613.4 90.1 %all-to-all-start = ((bf16[4,4,128,1536]{3,2,1,0:T(8,128)(2,1)}), bf16[4,4,128,1536]{3,2,1,0:T(8,128)(2,1)}, u32[]{:S(2)}, u32[]{:S(2)}) async-start(bf16[4,4,128,1536]{3,2,1,0:T(8,128)(2,1)} %bitcast.175), calls=%async_computation | async-start | bytes 12582912 | tf_op jit(solution)/shard_map/all_to_all | solution.py:442
  700.3 86.6 %collective-permute-start.31 = (bf16[512,1536]{1,0:T(8,128)(2,1)}, bf16[512,1536]{1,0:T(8,128)(2,1)}, u32[]{:S(2)}, u32[]{:S(2)}) collective-permute-start(bf16[512,1536]{1,0:T(8,128)(2,1)} %get-tuple-element.291), channel_id=1, source_target_pairs={{2,0},{0,1},{6,2},{4,3},{3,4},{1,5},{7,6},{5,7},{10,8},{8,9},{14,1... | collective-permute-start | bytes 4718600 | tf_op jit(solution)/shard_map/ppermute | solution.py:320
  701.5 85.4 %collective-permute-start.32 = (bf16[512,1536]{1,0:T(8,128)(2,1)}, bf16[512,1536]{1,0:T(8,128)(2,1)}, u32[]{:S(2)}, u32[]{:S(2)}) collective-permute-start(bf16[512,1536]{1,0:T(8,128)(2,1)} %get-tuple-element.290), channel_id=1, source_target_pairs={{2,1},{4,2},{6,3},{1,4},{3,5},{5,6},{10,9},{12,10},{14,11},{9,12},... | collective-permute-start | bytes 4718600 | tf_op jit(solution)/shard_map/ppermute | solution.py:320
  737.1 75.6 %all-to-all-start.1 = ((bf16[4,512,1536]{2,1,0:T(8,128)(2,1)}), bf16[4,512,1536]{2,1,0:T(8,128)(2,1)}, u32[]{:S(2)}, u32[]{:S(2)}) async-start(bf16[4,512,1536]{2,1,0:T(8,128)(2,1)} %bitcast.174), calls=%async_computation.1 | async-start | bytes 12582912 | tf_op jit(solution)/shard_map/all_to_all | solution.py:442
  742.3 244.5 %reduce-scatter.11.cloned.1.call-start = ((), (), s32[]{:S(2)}) async-start(), calls=%async_computation.12 | async-start | bytes 1966080 | tf_op jit(solution)/shard_map/reduce_scatter | solution.py:458
  827.8 140.1 %all-to-all-start.2 = ((bf16[4,704,1536]{2,1,0:T(8,128)(2,1)}), bf16[4,704,1536]{2,1,0:T(8,128)(2,1)}, u32[]{:S(2)}, u32[]{:S(2)}) async-start(bf16[4,704,1536]{2,1,0:T(8,128)(2,1)} %pad_maximum_fusion), calls=%async_computation.2 | async-start | bytes 17301504 | tf_op jit(solution)/shard_map/all_to_all | solution.py:442
  833.7 170.5 %reduce-scatter.5.cloned.1.call-start = ((), (), s32[]{:S(2)}) async-start(), calls=%async_computation.8 | async-start | bytes 737280 | tf_op jit(solution)/shard_map/reduce_scatter | solution.py:458
  981.5 95.5 %reduce-scatter.9.cloned.1.call-start = ((), (), s32[]{:S(2)}) async-start(), calls=%async_computation.11 | async-start | bytes 1966080 | tf_op jit(solution)/shard_map/reduce_scatter | solution.py:458
  986.8 212.2 %all-gather.9.cloned.1.call-start = ((), (), s32[]{:S(2)}) async-start(), calls=%async_computation.13 | async-start | bytes 3538944 | tf_op jit(solution)/shard_map/all_gather | solution.py:461
  987.4 217.1 %all-gather.7.cloned.1.call-start = ((), (), s32[]{:S(2)}) async-start(), calls=%async_computation.9 | async-start | bytes 1327104 | tf_op jit(solution)/shard_map/all_gather | solution.py:461
  1004.2 223.1 %all-gather.13.cloned.1.call-start = ((), (), s32[]{:S(2)}) async-start(), calls=%async_computation.15 | async-start | bytes 7077888 | tf_op jit(solution)/shard_map/all_gather | solution.py:461
  1081.4 63.7 %all-to-all-start.3 = ((bf16[4,336,1536]{2,1,0:T(8,128)(2,1)}), bf16[4,336,1536]{2,1,0:T(8,128)(2,1)}, u32[]{:S(2)}, u32[]{:S(2)}) async-start(bf16[4,336,1536]{2,1,0:T(8,128)(2,1)} %bitcast.166), calls=%async_computation.3 | async-start | bytes 8257536 | tf_op jit(solution)/shard_map/all_to_all | solution.py:442
  1093.9 62.5 %collective-permute-start.39 = (bf16[512,1536]{1,0:T(8,128)(2,1)}, bf16[512,1536]{1,0:T(8,128)(2,1)}, u32[]{:S(2)}, u32[]{:S(2)}) collective-permute-start(bf16[512,1536]{1,0:T(8,128)(2,1)} %get-tuple-element.285), channel_id=1, source_target_pairs={{2,0},{0,1},{6,2},{4,3},{3,4},{1,5},{7,6},{5,7},{10,8},{8,9},{14,1... | collective-permute-start | bytes 4718600 | tf_op jit(solution)/shard_map/ppermute | solution.py:320
  1094.3 62.0 %collective-permute-start.40 = (bf16[512,1536]{1,0:T(8,128)(2,1)}, bf16[512,1536]{1,0:T(8,128)(2,1)}, u32[]{:S(2)}, u32[]{:S(2)}) collective-permute-start(bf16[512,1536]{1,0:T(8,128)(2,1)} %get-tuple-element.284), channel_id=1, source_target_pairs={{2,1},{4,2},{6,3},{1,4},{3,5},{5,6},{10,9},{12,10},{14,11},{9,12},... | collective-permute-start | bytes 4718600 | tf_op jit(solution)/shard_map/ppermute | solution.py:320
  (135 other events, 2729.5 us)
Sparse Core Ops, SparseCore 0:
  54.4 246.5 all-gather.10
  754.2 38.8 reduce-scatter.10
  981.0 23.0 reduce-scatter.4
  1006.3 33.6 reduce-scatter.6
  1042.7 34.2 reduce-scatter.8
  1078.7 65.1 all-gather.8
  1145.8 25.7 all-gather.6
  1173.5 53.7 all-gather.12

commit v3 on v2

--- a/solution.py
+++ b/solution.py
@@ -19,6 +19,9 @@
 BOTH = ("chip", "core", "shard")
 
 
+SHORT = pl.CostEstimate(flops=1 << 20, transcendentals=0, bytes_accessed=1 << 20)
+
+
 def together(*arrays):
     return lax.optimization_barrier(arrays)
 
@@ -54,15 +57,16 @@
     return lax.fori_loop(full_high, high, functools.partial(step, True), carry)
 
 
-def forward_kernel(ranges, q_ref, k_ref, v_ref, starts_ref, o_ref, stat_ref, k_rows, *, group, wide):
+def forward_kernel(ranges, *refs, group, wide):
+    q_refs, (k_ref, v_ref, starts_ref, o_ref, stat_ref, k_rows) = refs[:group], refs[group:]
     place = pl.program_id(1)
-    q_width = q_ref.shape[1]
+    q_width = q_refs[0].shape[1]
 
     @pl.when(place == 0)
     def _():
         k_rows[...] = k_ref[...].T
 
-    queries = side_by_side(q_ref[...], group)
+    queries = jnp.concatenate([ref[...] for ref in q_refs], axis=1)
     starts = starts_ref[...]
 
     def step(masked, index, carry):
@@ -103,12 +107,12 @@
         stat_ref[0, g : g + 1, :] = stat[:, span]
 
 
-def backward_kernel(
-    ranges, q_ref, k_ref, v_ref, o_ref, g_ref, stat_ref, starts_ref,
-    dq_ref, dk_ref, dv_ref, k_rows, v_rows, dk_sum, dv_sum, *, group, wide,
-):
+def backward_kernel(ranges, *refs, group, wide):
+    q_refs, (k_ref, v_ref, o_ref, g_ref, stat_ref, starts_ref), (
+        back_ref, k_rows, v_rows, dk_sum, dv_sum,
+    ) = refs[:group], refs[group : group + 6], refs[group + 6 :]
     place = pl.program_id(1)
-    q_width = q_ref.shape[1]
+    q_width = q_refs[0].shape[1]
 
     @pl.when(place == 0)
     def _():
@@ -117,7 +121,7 @@
         dk_sum[...] = jnp.zeros_like(dk_sum)
         dv_sum[...] = jnp.zeros_like(dv_sum)
 
-    queries = side_by_side(q_ref[...], group)
+    queries = jnp.concatenate([ref[...] for ref in q_refs], axis=1)
     grads = side_by_side(g_ref[...], group)
     outs = side_by_side(o_ref[...], group)
     inner = jnp.sum(grads.astype(F32) * outs.astype(F32), axis=0, keepdims=True)
@@ -140,13 +144,14 @@
 
     dq = three_loops(ranges, place, step, jnp.zeros((HEAD, group * q_width), F32))
     dq = (dq * SCALE).astype(BF16)
+    here = pl.ds(pl.multiple_of(place * q_width, q_width), q_width)
     for g in range(group):
-        dq_ref[g * HEAD : (g + 1) * HEAD, :] = dq[:, g * q_width : (g + 1) * q_width]
+        back_ref[g * HEAD : (g + 1) * HEAD, here] = dq[:, g * q_width : (g + 1) * q_width]
 
     @pl.when(place == pl.num_programs(1) - 1)
     def _():
-        dk_ref[...] = (dk_sum[...] * SCALE).astype(BF16)
-        dv_ref[...] = dv_sum[...].astype(BF16)
+        back_ref[group * HEAD : (group + 1) * HEAD, :] = (dk_sum[...] * SCALE).astype(BF16)
+        back_ref[(group + 1) * HEAD :, :] = dv_sum[...].astype(BF16)
 
 
 def block_ranges(starts, q_width, wide):
@@ -164,23 +169,22 @@
 
 
 def attention_specs(head, group, length, q_width):
-    per_query = pl.BlockSpec((group * HEAD, q_width), lambda h, i, r: (head, i))
-    per_head = pl.BlockSpec((HEAD, length), lambda h, i, r: (head, 0))
-    out_query = pl.BlockSpec((group * HEAD, q_width), lambda h, i, r: (0, i))
-    out_head = pl.BlockSpec((HEAD, length), lambda h, i, r: (0, 0))
+    first = head * (group + 2)
+    queries = [
+        pl.BlockSpec((HEAD, q_width), lambda h, i, r, g=g: (first + g, i)) for g in range(group)
+    ]
+    keys = pl.BlockSpec((HEAD, length), lambda h, i, r: (first + group, 0))
+    values = pl.BlockSpec((HEAD, length), lambda h, i, r: (first + group + 1, 0))
+    per_query = pl.BlockSpec((group * HEAD, q_width), lambda h, i, r: (0, i))
     stat = pl.BlockSpec((1, group, q_width), lambda h, i, r: (0, 0, i))
     starts = pl.BlockSpec((1, q_width), lambda h, i, r: (0, i))
-    return per_query, per_head, out_query, out_head, stat, starts
-
-
-def attend_forward(head, q_t, k_t, v_t, starts):
-    length = q_t.shape[1]
-    group = q_t.shape[0] // k_t.shape[0]
+    return [*queries, keys, values], per_query, stat, starts
+
+
+def attend_forward(head, group, qkv_t, starts, ranges):
+    length = qkv_t.shape[1]
     q_width, wide = forward_blocks(length)
-    per_query, per_head, out_query, _, stat, start_spec = attention_specs(
-        head, group, length, q_width
-    )
-    pairs = group * length * length // 2
+    rows, per_query, stat, start_spec = attention_specs(head, group, length, q_width)
     return pl.pallas_call(
         functools.partial(forward_kernel, group=group, wide=wide),
         out_shape=(
@@ -190,40 +194,31 @@
         grid_spec=pltpu.PrefetchScalarGridSpec(
             num_scalar_prefetch=1,
             grid=(1, length // q_width),
-            in_specs=[per_query, per_head, per_head, start_spec],
-            out_specs=(out_query, stat),
+            in_specs=[*rows, start_spec],
+            out_specs=(per_query, stat),
             scratch_shapes=[pltpu.VMEM((length, HEAD), BF16)],
         ),
         compiler_params=pltpu.CompilerParams(
             dimension_semantics=("arbitrary", "arbitrary"), vmem_limit_bytes=40 << 20
         ),
-        cost_estimate=pl.CostEstimate(
-            flops=pairs * HEAD * 4, transcendentals=0, bytes_accessed=group * length * 512
-        ),
+        cost_estimate=SHORT,
         name="attend_forward",
-    )(block_ranges(starts, q_width, wide), q_t, k_t, v_t, starts)
-
-
-def attend_backward(head, q_t, k_t, v_t, o_h, g_h, stat_h, starts):
-    length = q_t.shape[1]
-    group = q_t.shape[0] // k_t.shape[0]
+    )(ranges, *[qkv_t] * (group + 2), starts)
+
+
+def attend_backward(head, group, qkv_t, o_h, g_h, stat_h, starts, ranges):
+    length = qkv_t.shape[1]
     q_width, wide = backward_blocks(length)
-    per_query, per_head, out_query, out_head, stat, start_spec = attention_specs(
-        head, group, length, q_width
-    )
-    pairs = group * length * length // 2
+    rows, per_query, stat, start_spec = attention_specs(head, group, length, q_width)
+    count = (group + 2) * HEAD
     return pl.pallas_call(
         functools.partial(backward_kernel, group=group, wide=wide),
-        out_shape=(
-            jax.ShapeDtypeStruct((group * HEAD, length), BF16),
-            jax.ShapeDtypeStruct((HEAD, length), BF16),
-            jax.ShapeDtypeStruct((HEAD, length), BF16),
-        ),
+        out_shape=jax.ShapeDtypeStruct((count, length), BF16),
         grid_spec=pltpu.PrefetchScalarGridSpec(
             num_scalar_prefetch=1,
             grid=(1, length // q_width),
-            in_specs=[per_query, per_head, per_head, out_query, out_query, stat, start_spec],
-            out_specs=(out_query, out_head, out_head),
+            in_specs=[*rows, per_query, per_query, stat, start_spec],
+            out_specs=pl.BlockSpec((count, length), lambda h, i, r: (0, 0)),
             scratch_shapes=[
                 pltpu.VMEM((length, HEAD), BF16),
                 pltpu.VMEM((length, HEAD), BF16),
@@ -234,11 +229,9 @@
         compiler_params=pltpu.CompilerParams(
             dimension_semantics=("arbitrary", "arbitrary"), vmem_limit_bytes=40 << 20
         ),
-        cost_estimate=pl.CostEstimate(
-            flops=pairs * HEAD * 10, transcendentals=0, bytes_accessed=group * length * 1024
-        ),
+        cost_estimate=SHORT,
         name="attend_backward",
-    )(block_ranges(starts, q_width, wide), q_t, k_t, v_t, o_h, g_h, stat_h, starts)
+    )(ranges, *[qkv_t] * (group + 2), o_h, g_h, stat_h, starts)
 
 
 class Place:
@@ -308,19 +301,16 @@
     def to_streams(self, array):
         return self.join_streams(array, self.send_streams(array))
 
-    def to_homes(self, array):
+    def send_homes(self, array):
         half = array.shape[0] // 2
         swapped = self.batch == 1
         parts = [array[:half], array[half:]]
-        got = [
-            jnp.where(swapped, parts[1 - turn], parts[turn]) for turn in range(2)
-        ]
-        got = [
-            jnp.where(
-                self.stays(turn), part, lax.ppermute(part, BOTH, self.moves(turn, True))
-            )
-            for turn, part in enumerate(got)
-        ]
+        parts = [jnp.where(swapped, parts[1 - turn], parts[turn]) for turn in range(2)]
+        got = [lax.ppermute(part, BOTH, self.moves(turn, True)) for turn, part in enumerate(parts)]
+        return parts, got
+
+    def join_homes(self, parts, got):
+        got = [jnp.where(self.stays(turn), parts[turn], got[turn]) for turn in range(2)]
         odd = self.shard % 2 == 1
         return jnp.stack([jnp.where(odd, got[1], got[0]), jnp.where(odd, got[0], got[1])])
 
@@ -420,9 +410,7 @@
                 pltpu.SemaphoreType.DMA((len(widths) * parts * (1 + quarters * (shards - 1)),))
             ],
             compiler_params=pltpu.CompilerParams(vmem_limit_bytes=24 << 20),
-            cost_estimate=pl.CostEstimate(
-                flops=0, transcendentals=0, bytes_accessed=own.size * shards * 4
-            ),
+            cost_estimate=SHORT,
             name="assemble",
         )(places, own, *found)
         return [part.reshape(parts * shards * quarters * rows, -1) for part in whole]
@@ -438,12 +426,8 @@
         piece = jnp.concatenate([part(w_gate), part(w_up)], axis=0)
         return lax.all_gather(piece, ("shard", "chip", "core"), axis=0, tiled=False)
 
-    def reduce_across(self, grad):
-        got = lax.all_to_all(grad, "chip", 0, 0, tiled=True)
-        return jnp.sum(got.astype(F32), axis=0).astype(BF16)
-
-    def by_shard(self, held):
-        return jnp.transpose(held.reshape(held.shape[0], self.shards, -1), (1, 0, 2))
+    def exchange(self, grad):
+        return lax.all_to_all(grad, "chip", 0, 0, tiled=True)
 
     def reduce_along(self, held):
         total = lax.dynamic_index_in_dim(held, self.shard, 0, keepdims=False).astype(F32)
@@ -498,25 +482,23 @@
                 (group * small, experts * hidden // 2), lambda i, c: (i, 0)
             ),
         ),
-        cost_estimate=pl.CostEstimate(
-            flops=0, transcendentals=0, bytes_accessed=packed.size
-        ),
+        cost_estimate=SHORT,
         name="core_columns",
     )(core.astype(jnp.int32)[None], *([packed] * shards))
 
 
-def spread_experts(summed, which, experts, shards):
-    quarters, _, _, columns, rows = summed.shape
-    hidden = 2 * columns * quarters // experts
+def spread_experts(summed, experts, shards, hidden):
+    quarters, _, _, rows = summed.shape
+    columns = experts * hidden // 2 // quarters
     part = hidden // shards // 2
     if part % 128 or quarters != experts:
-        piece = jnp.transpose(summed[:, :, which].astype(F32), (1, 0, 2, 3))
+        piece = jnp.transpose(summed[:, :, :columns].astype(F32), (1, 0, 2, 3))
         piece = piece.reshape(2, experts, shards, part, rows)
         return jnp.transpose(piece, (1, 4, 2, 0, 3)).reshape(experts, rows, hidden)
 
     def kernel(in_ref, out_ref):
         for core in range(2):
-            turned = in_ref[0, core, 0].astype(F32).T
+            turned = in_ref[0, core].astype(F32).T
             for shard in range(shards):
                 first = (2 * shard + core) * part
                 out_ref[0, :, first : first + part] = turned[:, shard * part : (shard + 1) * part]
@@ -525,40 +507,75 @@
         kernel,
         out_shape=jax.ShapeDtypeStruct((experts, rows, hidden), F32),
         grid=(experts,),
-        in_specs=[pl.BlockSpec((1, 2, 1, columns, rows), lambda e: (e, 0, which, 0, 0))],
+        in_specs=[pl.BlockSpec((1, 2, columns, rows), lambda e: (e, 0, 0, 0))],
         out_specs=pl.BlockSpec((1, rows, hidden), lambda e: (e, 0, 0)),
-        cost_estimate=pl.CostEstimate(
-            flops=0, transcendentals=0, bytes_accessed=summed.size * 3
-        ),
+        cost_estimate=SHORT,
         name="spread_experts",
     )(summed)
 
 
-def spread_rows(mine, other, quarter, core, widths):
+def attention_columns(core, w_query, w_key, w_value, small, w_out):
+    rows = w_query.shape[0]
+    width_q, width_k, width_out = (w.shape[1] // 2 for w in (w_query, w_key, w_out))
+    heads = width_k // HEAD
+    part = width_q // heads
+    total = width_q + 2 * width_k + small.shape[1] + width_out
+
+    def kernel(core_ref, q_ref, k_ref, v_ref, small_ref, o_ref, out_ref):
+        def half(ref, width):
+            return ref[:, pl.ds(pl.multiple_of(core_ref[0] * width, 128), width)]
+
+        query, key, value = half(q_ref, width_q), half(k_ref, width_k), half(v_ref, width_k)
+        pieces = []
+        for head in range(heads):
+            span = slice(head * HEAD, (head + 1) * HEAD)
+            pieces += [query[:, head * part : (head + 1) * part], key[:, span], value[:, span]]
+        first = width_q + 2 * width_k
+        out_ref[:, :first] = jnp.concatenate(pieces, axis=1)
+        out_ref[:, first : first + small.shape[1]] = small_ref[...]
+        out_ref[:, first + small.shape[1] :] = half(o_ref, width_out)
+
+    return pl.pallas_call(
+        kernel,
+        out_shape=jax.ShapeDtypeStruct((rows, total), w_query.dtype),
+        in_specs=[pl.BlockSpec(memory_space=pltpu.SMEM)]
+        + [pl.BlockSpec(memory_space=pltpu.VMEM)] * 5,
+        out_specs=pl.BlockSpec(memory_space=pltpu.VMEM),
+        cost_estimate=SHORT,
+        name="attention_columns",
+    )(core.astype(jnp.int32)[None], w_query, w_key, w_value, small, w_out)
+
+
+def spread_rows(mine, other, quarter, core, heads, group):
     quarters, columns, rows = mine.shape
-    rest = quarters * columns - sum(widths)
+    each = (group + 2) * HEAD
+    own = heads * each // quarters
+    rest = columns - own
+    widths = [heads * group * HEAD, heads * HEAD, heads * HEAD]
+    edges = [0, group * HEAD, (group + 1) * HEAD, each]
     places = jnp.stack([quarter, core]).astype(jnp.int32)
 
     def kernel(places_ref, mine_ref, other_ref, *out_refs):
         quarter, core = places_ref[0], places_ref[1]
+        smalls = jnp.zeros((rest, rows), F32)
         for side, ref in enumerate((mine_ref, other_ref)):
             at = core if side == 0 else 1 - core
             whole = jnp.concatenate(
-                [ref[n ^ quarter].astype(F32) for n in range(quarters)], axis=0
+                [ref[n ^ quarter, :own].astype(F32) for n in range(quarters)], axis=0
             )
-            first = 0
-            for width, out_ref in zip(widths, out_refs):
+            for n in range(quarters):
+                smalls = smalls + ref[n, own:].astype(F32)
+            for n, (width, out_ref) in enumerate(zip(widths, out_refs)):
                 span = pl.ds(pl.multiple_of(at * width, 128), width)
-                out_ref[:, span] = whole[first : first + width].T
-                first += width
-            if rest and side == 0:
-                out_refs[-1][...] = whole[first:]
-            elif rest:
-                out_refs[-1][...] += whole[first:]
+                picked = [
+                    whole[head * each + edges[n] : head * each + edges[n + 1]]
+                    for head in range(heads)
+                ]
+                out_ref[:, span] = jnp.concatenate(picked, axis=0).T
+        out_refs[-1][...] = smalls
 
     shapes = [jax.ShapeDtypeStruct((rows, 2 * width), F32) for width in widths]
-    if rest:
-        shapes.append(jax.ShapeDtypeStruct((rest, rows), F32))
+    shapes.append(jax.ShapeDtypeStruct((rest, rows), F32))
     return pl.pallas_call(
         kernel,
         out_shape=tuple(shapes),
@@ -569,11 +586,149 @@
         ],
         out_specs=tuple(pl.BlockSpec(memory_space=pltpu.VMEM) for _ in shapes),
         compiler_params=pltpu.CompilerParams(vmem_limit_bytes=40 << 20),
-        cost_estimate=pl.CostEstimate(
-            flops=0, transcendentals=0, bytes_accessed=mine.size * 12
-        ),
+        cost_estimate=SHORT,
         name="spread_rows",
     )(places, mine, other)
+
+
+def spread_out(summed, first):
+    quarters, _, columns, rows = summed.shape
+    width = quarters * (columns - first)
+
+    def kernel(in_ref, out_ref):
+        for core in range(2):
+            whole = jnp.concatenate(
+                [in_ref[n, core, first:].astype(F32) for n in range(quarters)], axis=0
+            )
+            out_ref[:, core * width : (core + 1) * width] = whole.T
+
+    return pl.pallas_call(
+        kernel,
+        out_shape=jax.ShapeDtypeStruct((rows, 2 * width), F32),
+        in_specs=[pl.BlockSpec(memory_space=pltpu.VMEM)],
+        out_specs=pl.BlockSpec(memory_space=pltpu.VMEM),
+        compiler_params=pltpu.CompilerParams(vmem_limit_bytes=40 << 20),
+        cost_estimate=SHORT,
+        name="spread_out",
+    )(summed)
+
+
+def full_block(array):
+    return pl.BlockSpec(array.shape, lambda i: (0, 0), pipeline_mode=pl.Buffered(1))
+
+
+def row_block(rows, columns):
+    return pl.BlockSpec((rows, columns), lambda i: (i, 0))
+
+
+def experts_forward(b_all, gate_w, up_w, shares):
+    count, features = b_all.shape
+    columns = gate_w.shape[1]
+    experts = shares.shape[1]
+    width = columns // experts
+    tile = min(256, count)
+
+    def kernel(b_ref, gate_w_ref, up_w_ref, share_ref, gate_ref, up_ref, mid_ref):
+        rows = b_ref[...]
+        for expert in range(experts):
+            span = slice(expert * width, (expert + 1) * width)
+            gate = jnp.dot(rows, gate_w_ref[:, span], preferred_element_type=F32).astype(BF16)
+            up = jnp.dot(rows, up_w_ref[:, span], preferred_element_type=F32).astype(BF16)
+            gate_ref[:, span] = gate
+            up_ref[:, span] = up
+            gate, up = gate.astype(F32), up.astype(F32)
+            share = share_ref[:, expert : expert + 1]
+            mid_ref[:, span] = (gate * jax.nn.sigmoid(gate) * up * share).astype(BF16)
+
+    return pl.pallas_call(
+        kernel,
+        out_shape=(jax.ShapeDtypeStruct((count, columns), BF16),) * 3,
+        grid=(count // tile,),
+        in_specs=[
+            row_block(tile, features),
+            full_block(gate_w),
+            full_block(up_w),
+            row_block(tile, experts),
+        ],
+        out_specs=(row_block(tile, columns),) * 3,
+        compiler_params=pltpu.CompilerParams(vmem_limit_bytes=48 << 20),
+        cost_estimate=SHORT,
+        name="experts_forward",
+    )(b_all, gate_w, up_w, shares)
+
+
+def experts_backward(dy_all, down_w, gate_v, up_v, shares):
+    count, features = dy_all.shape
+    columns = gate_v.shape[1]
+    experts = shares.shape[1]
+    width = columns // experts
+    tile = min(256, count)
+
+    def kernel(dy_ref, down_ref, gate_ref, up_ref, share_ref, dgate_ref, dup_ref, dshare_ref):
+        rows = dy_ref[...]
+        sums = []
+        for expert in range(experts):
+            span = slice(expert * width, (expert + 1) * width)
+            slope = dot(rows, down_ref[span, :], 1, 1)
+            gate, up = gate_ref[:, span].astype(F32), up_ref[:, span].astype(F32)
+            squashed = jax.nn.sigmoid(gate)
+            active = gate * squashed
+            sums.append(jnp.sum(slope * active * up, axis=1, keepdims=True))
+            scaled = slope * share_ref[:, expert : expert + 1]
+            dgate_ref[:, span] = (
+                scaled * up * squashed * (1.0 + gate * (1.0 - squashed))
+            ).astype(BF16)
+            dup_ref[:, span] = (scaled * active).astype(BF16)
+        dshare_ref[...] = jnp.concatenate(sums, axis=1)
+
+    return pl.pallas_call(
+        kernel,
+        out_shape=(
+            jax.ShapeDtypeStruct((count, columns), BF16),
+            jax.ShapeDtypeStruct((count, columns), BF16),
+            jax.ShapeDtypeStruct((count, experts), F32),
+        ),
+        grid=(count // tile,),
+        in_specs=[
+            row_block(tile, features),
+            full_block(down_w),
+            row_block(tile, columns),
+            row_block(tile, columns),
+            row_block(tile, experts),
+        ],
+        out_specs=(
+            row_block(tile, columns),
+            row_block(tile, columns),
+            row_block(tile, experts),
+        ),
+        compiler_params=pltpu.CompilerParams(vmem_limit_bytes=48 << 20),
+        cost_estimate=SHORT,
+        name="experts_backward",
+    )(dy_all, down_w, gate_v, up_v, shares)
+
+
+def sum_parts(parts, shards):
+    count, rows, features = parts.shape
+    width = features // shards
+    if width % 128:
+        held = jnp.sum(parts.astype(F32), axis=0).astype(BF16)
+        return jnp.transpose(held.reshape(rows, shards, width), (1, 0, 2))
+
+    def kernel(in_ref, out_ref):
+        total = in_ref[0].astype(F32)
+        for n in range(1, count):
+            total = total + in_ref[n].astype(F32)
+        out_ref[0] = total.astype(BF16)
+
+    return pl.pallas_call(
+        kernel,
+        out_shape=jax.ShapeDtypeStruct((shards, rows, width), BF16),
+        grid=(shards,),
+        in_specs=[pl.BlockSpec((count, rows, width), lambda i: (0, 0, i))],
+        out_specs=pl.BlockSpec((1, rows, width), lambda i: (i, 0, 0)),
+        cost_estimate=SHORT,
+        name="sum_parts",
+    )(parts)
 
 
 def rms_scale(rows_in):
@@ -618,33 +773,39 @@
     hidden_part = hidden_all // shards // 2
     hidden_core = hidden_all // 2
 
-    def columns_of(weight, width):
-        return lax.dynamic_slice_in_dim(weight, core * width, width, 1)
-
     small = jnp.concatenate([attn_gain[:, None], moe_gain[:, None], w_router], axis=1)
     small = jnp.pad(small, ((0, 0), (0, 128 - small.shape[1])))
-    own = jnp.concatenate(
-        [
-            columns_of(w_query, width_q),
-            columns_of(w_key, width_k),
-            columns_of(w_value, width_k),
-            small,
-            columns_of(w_out, features // 2),
-        ],
-        axis=1,
-    ).reshape(1, quarters, rows_q, -1)
+    own = attention_columns(core, w_query, w_key, w_value, small, w_out)
+    own = own.reshape(1, quarters, rows_q, -1)
     got = here.fetch_along(own)
 
-    tokens, own = together(tokens, own)
-    x_own = here.to_streams(tokens[:, 0])
+    length = tokens.shape[2] * shards
+    my_lengths = lax.dynamic_index_in_dim(
+        lax.dynamic_index_in_dim(lengths, here.batch, 0, keepdims=False),
+        here.source,
+        0,
+        keepdims=False,
+    )
+    ends = jnp.cumsum(my_lengths)[:-1]
+    positions = jnp.arange(length, dtype=jnp.int32)
+    starts = jnp.max(
+        jnp.where(ends[:, None] <= positions[None, :], ends[:, None], 0), axis=0, keepdims=True
+    ).astype(jnp.int32)
+    forward_ranges = block_ranges(starts, *forward_blocks(length))
+    backward_ranges = block_ranges(starts, *backward_blocks(length))
+    x_blocks = here.send_streams(tokens[:, 0])
+    found = here.fetch_across(got)
+    starts, forward_ranges, backward_ranges, *held = together(
+        starts, forward_ranges, backward_ranges, *x_blocks, *found
+    )
+    x_blocks, found = held[:2], held[2:]
+    x_own = here.join_streams(tokens[:, 0], x_blocks)
     rows = x_own.shape[0]
-    w_gate, *got = together(w_gate, *got)
+    w_gate, routes, x_own = together(w_gate, routes, x_own)
     packed = here.gather_experts(w_gate, w_up)
     own_down = lax.dynamic_slice_in_dim(w_down, core * hidden_part, hidden_part, 1).reshape(
         experts, quarters, hidden_part // quarters, features
     )
-    found = here.fetch_across(got)
-    routes, x_own = together(routes, x_own)
     route_own = here.to_streams(routes[:, 0])
     own_down, route_own = together(own_down, route_own)
     got_down = here.fetch_along(own_down)
@@ -663,30 +824,17 @@
     normed = here.ordered(normed_own, here.swap(normed_own), 0)
     route_all = jnp.concatenate([route_own, here.swap(route_own)], axis=0)
     qkv_t = dot(qkv_w, normed, 0, 1, BF16)
-    q_t, k_t, v_t = qkv_t[:width_q], qkv_t[width_q : width_q + width_k], qkv_t[width_q + width_k :]
-    q_t, k_t, v_t = (here.chip_exchange(part, 0, 1) for part in (q_t, k_t, v_t))
-    length = q_t.shape[1]
-
-    my_lengths = lax.dynamic_index_in_dim(
-        lax.dynamic_index_in_dim(lengths, here.batch, 0, keepdims=False),
-        here.source,
-        0,
-        keepdims=False,
-    )
-    ends = jnp.cumsum(my_lengths)[:-1]
-    positions = jnp.arange(length, dtype=jnp.int32)
-    starts = jnp.max(
-        jnp.where(ends[:, None] <= positions[None, :], ends[:, None], 0), axis=0, keepdims=True
-    ).astype(jnp.int32)
-    heads = k_t.shape[0] // HEAD
+    qkv_t = here.chip_exchange(qkv_t, 0, 1)
+    group = width_q // width_k
+    heads = width_k // HEAD // here.chips
     o_heads, stats, o_mine, o_got = [], [], [], []
     for head in range(heads):
-        source = k_t
+        source = qkv_t
         if head == 0:
-            source, route_all = together(k_t, route_all)
+            source, route_all = together(qkv_t, route_all)
         else:
-            source, stats[-1] = together(k_t, stats[-1])
-        o_h, stat = attend_forward(head, q_t, source, v_t, starts)
+            source, stats[-1] = together(qkv_t, stats[-1])
+        o_h, stat = attend_forward(head, group, source, starts, forward_ranges)
         o_heads.append(o_h)
         stats.append(stat)
         if head == 1:
@@ -698,6 +846,8 @@
     o_own = here.ordered(
         here.head_order(o_mine, heads), here.head_order(o_got, heads), 0
     )
+    cotangent, packed = together(cotangent, packed)
+    dy_blocks = here.send_streams(cotangent[:, 0])
     gate_w = core_columns(packed, 0, core, shards, experts)
     up_w = core_columns(packed, 1, core, shards, experts)
     h_own = x_wide + dot(o_own, out_w, 0, 0)
@@ -705,8 +855,6 @@
     scale_two = rms_scale(h_own)
     b_own = (h_own * scale_two * gain_two).astype(BF16)
     b_all = jnp.concatenate([b_own, here.swap(b_own)], axis=0)
-    cotangent, gate_w = together(cotangent, gate_w)
-    dy_blocks = here.send_streams(cotangent[:, 0])
 
     logits = dot(b_all, router_w, 1, 0)
     route_hot = (
@@ -715,25 +863,19 @@
     chosen = jnp.sum(logits[:, None, :] * route_hot, axis=2)
     gate_share = jax.nn.softmax(chosen, axis=1)
     shares = jnp.sum(gate_share[:, :, None] * route_hot, axis=1)
-    share_wide = jnp.repeat(shares, hidden_core, axis=1)
-
-    gate_v = dot(b_all, gate_w, 1, 0, BF16)
-    *found_down, gate_v = together(*found_down, gate_v)
-    down_w = here.assemble(own_down, found_down, [features])[0]
-    up_v = dot(b_all, up_w, 1, 0, BF16)
-    *dy_blocks, up_v = together(*dy_blocks, up_v)
+
+    gate_v, up_v, mid = experts_forward(b_all, gate_w, up_w, shares)
+    *found_down, mid = together(*found_down, mid)
+    *dy_blocks, mid = together(*dy_blocks, mid)
     dy_own = here.join_streams(cotangent[:, 0], dy_blocks)
     dy_all = jnp.concatenate([dy_own, here.swap(dy_own)], axis=0)
-    gate_f, up_f = gate_v.astype(F32), up_v.astype(F32)
-    squashed = jax.nn.sigmoid(gate_f)
-    mid = (gate_f * squashed * up_f * share_wide).astype(BF16)
+    down_w = here.assemble(own_down, found_down, [features])[0]
     y_other = dot(mid[rows:], down_w, 1, 0, BF16)
     y_got = here.swap(y_other)
     y_own = dot(mid[:rows], down_w, 1, 0)
     block_own = (h_own + y_own + y_got.astype(F32)).astype(BF16)
-    block_out = here.to_homes(block_own)
-
-    slope = dot(dy_all, down_w, 1, 1)
+    block_out = here.join_homes(*here.send_homes(block_own))
+
     grad_down = dot(mid, dy_all, 0, 0, BF16)
     if quarters == experts:
         grad_down = grad_down.reshape(quarters, shards, hidden_part, features)
@@ -742,12 +884,9 @@
             grad_down.reshape(experts, shards, hidden_part, quarters, features // quarters),
             (3, 1, 0, 2, 4),
         )
-    held_down = here.reduce_across(grad_down)
-    active = gate_f * squashed
-    grad_share = jnp.sum((slope * active * up_f).reshape(2 * rows, experts, hidden_core), axis=2)
-    scaled = slope * share_wide
-    grad_gate_v = (scaled * up_f * squashed * (1.0 + gate_f * (1.0 - squashed))).astype(BF16)
-    grad_up_v = (scaled * active).astype(BF16)
+    dy_all, down_w, grad_down = together(dy_all, down_w, grad_down)
+    got_grad_down = here.exchange(grad_down)
+    grad_gate_v, grad_up_v, grad_share = experts_backward(dy_all, down_w, gate_v, up_v, shares)
     share_got = here.swap(grad_share[rows:])
     grad_share = grad_share[:rows] + share_got
 
@@ -756,14 +895,15 @@
 
     grad_gate = expert_grad(grad_gate_v)
     grad_up = expert_grad(grad_up_v)
-    grad_gate_v, grad_up_v, grad_gate, grad_up = together(
-        grad_gate_v, grad_up_v, grad_gate, grad_up
-    )
+    grad_gate_v, grad_up_v, grad_gate, grad_up, got_grad_down = together(
+        grad_gate_v, grad_up_v, grad_gate, grad_up, got_grad_down
+    )
+    held_down = jnp.sum(got_grad_down.astype(F32), axis=0).astype(BF16)
     db_other = (
         dot(grad_gate_v[rows:], gate_w, 1, 1) + dot(grad_up_v[rows:], up_w, 1, 1)
     ).astype(BF16)
     db_got = here.swap(db_other)
-    db_got, held_down = together(db_got, held_down)
+    got_grad_gate = here.exchange(grad_gate)
     db_own = dot(grad_gate_v[:rows], gate_w, 1, 1) + dot(grad_up_v[:rows], up_w, 1, 1)
 
     hot_own, share_own = route_hot[:rows], gate_share[:rows]
@@ -778,8 +918,7 @@
     dh = dh + dy_own.astype(F32)
     dattn = dh.astype(BF16)
 
-    dattn, grad_gate = together(dattn, grad_gate)
-    held_gate = here.by_shard(here.reduce_across(grad_gate))
+    qkv_w_got = here.swap(qkv_w)
     do_t = dot(out_w, dattn, 1, 1, BF16)
     do_mine, do_other = here.halves(do_t, 0)
     do_t = here.ordered(do_mine, here.swap(do_other), 1)
@@ -790,62 +929,68 @@
     back_heads, back_rows, back_got = [], [], []
     for head in range(heads):
         g_h = do_t[head * o_heads[0].shape[0] : (head + 1) * o_heads[0].shape[0]]
-        if head == 1:
-            g_h, block_out, held_gate, grad_up, grad_out, back_heads[0] = together(
-                g_h, block_out, held_gate, grad_up, grad_out, back_heads[0]
+        if head == 0:
+            g_h, grad_out, qkv_w_got = together(g_h, grad_out, qkv_w_got)
+        elif head == 1:
+            g_h, block_out, got_grad_gate, grad_out, back_heads[0] = together(
+                g_h, block_out, got_grad_gate, grad_out, back_heads[0]
             )
-            cut = grad_up.shape[1]
-            held_both = here.reduce_across(
-                jnp.concatenate([grad_up, grad_out.reshape(quarters, -1, features)], axis=1)
-            )
-        elif head:
+            got_grad_out = here.exchange(grad_out.reshape(quarters, -1, features))
+            total_gate = here.scatter(sum_parts(got_grad_gate, shards))
+        else:
             g_h, back_heads[-1] = together(g_h, back_heads[-1])
-        parts = attend_backward(head, q_t, k_t, v_t, o_heads[head], g_h, stats[head], starts)
-        parts = [here.chip_exchange(part, 1, 0) for part in parts]
-        back_heads.append(parts)
-        back_h = jnp.concatenate(parts, axis=0)
+        if head == heads // 2:
+            g_h, got_grad_out, grad_up = together(g_h, got_grad_out, grad_up)
+            got_grad_up = here.exchange(grad_up)
+            total_out = here.scatter(sum_parts(got_grad_out, shards))
+        back_h = attend_backward(
+            head, group, qkv_t, o_heads[head], g_h, stats[head], starts, backward_ranges
+        )
+        back_h = here.chip_exchange(back_h, 1, 0)
+        back_heads.append(back_h)
         mine, other = here.halves(back_h, 1)
         back_rows.append(mine)
         back_got.append(here.swap(other))
 
-    def all_heads(which):
-        return here.head_order([parts[which] for parts in back_heads], heads)
-
-    back_t = jnp.concatenate([all_heads(0), all_heads(1), all_heads(2)], axis=0)
-    qkv_w_got = here.swap(qkv_w)
-    sizes = [parts.shape[0] for parts in back_heads[0]]
-
-    def regroup(pieces):
-        edges = [0, sizes[0], sizes[0] + sizes[1], sum(sizes)]
-        return jnp.concatenate(
-            [
-                here.head_order([piece[edges[n] : edges[n + 1]] for piece in pieces], heads)
-                for n in range(3)
-            ],
-            axis=0,
-        )
-
-    da = dot(regroup(back_rows), qkv_w, 0, 1) + dot(regroup(back_got), qkv_w_got, 0, 1)
-    grad_qkv = dot(back_t, normed, 1, 0, BF16)
+    grad_qkv = jnp.stack(
+        [
+            dot(back_h, normed, 1, 0, BF16).reshape(here.chips, -1, features)
+            for back_h in back_heads
+        ],
+        axis=1,
+    ).reshape(quarters, -1, features)
+    grad_qkv, got_grad_up = together(grad_qkv, got_grad_up)
+    total_up = here.scatter(sum_parts(got_grad_up, shards))
+    got_grad_qkv = here.exchange(grad_qkv)
+    da = dot(here.head_order(back_rows, heads), qkv_w, 0, 1) + dot(
+        here.head_order(back_got, heads), qkv_w_got, 0, 1
+    )
+    da, got_grad_qkv = together(da, got_grad_qkv)
     dx, grad_gain_one = norm_back(x_wide, scale_one, gain_one, da)
-    input_grad = here.to_homes((dx + dh).astype(BF16))
+    dx_rows = (dx + dh).astype(BF16)
 
     grad_small = jnp.concatenate([grad_gain_one[None], grad_gain_two[None], grad_router], axis=0)
-    grad_small = jnp.pad(grad_small, ((0, 64 - grad_small.shape[0]), (0, 0))).astype(BF16)
-    grad_qkv = jnp.concatenate([grad_qkv, grad_small], axis=0).reshape(quarters, -1, features)
-    grad_qkv, held_both = together(grad_qkv, held_both)
-    held_up = here.by_shard(held_both[:cut])
-    held_out = here.by_shard(held_both[cut:])
-    held_qkv = here.by_shard(here.reduce_across(grad_qkv))
+    grad_small = jnp.pad(grad_small, ((0, 16 - grad_small.shape[0]), (0, 0))).astype(BF16)
+    grad_small = jnp.transpose(grad_small.reshape(16, shards, shard_rows), (1, 0, 2))
+    held_qkv = sum_parts(got_grad_qkv, shards)
+    held_qkv, total_up, total_out = together(held_qkv, total_up, total_out)
+    held_qkv = jnp.concatenate([held_qkv, grad_small], axis=1)
+    total = here.reduce_along(held_qkv)
+    total, dx_rows = together(total, dx_rows)
+    input_grad = here.join_homes(*here.send_homes(dx_rows))
     sum_down = here.gather(here.scatter(held_down))
-    sum_gate_up = here.gather(jnp.stack([here.scatter(held_gate), here.scatter(held_up)]))
-    sum_out = here.gather(here.scatter(held_out))
-    total = here.reduce_along(held_qkv)
+    sum_gate = here.gather(total_gate)
+    sum_up_out = here.gather(jnp.concatenate([total_up, total_out], axis=0))
+    cut = total_up.shape[0]
     mine = jnp.stack([total] + [here.across(total, key) for key in range(1, quarters)])
     out_query, out_key, out_value, small_sum = spread_rows(
-        mine, here.swap(mine), here.quarter, core, [width_q, width_k, width_k]
-    )
-    out_out = jnp.transpose(sum_out.astype(F32), (3, 1, 0, 2)).reshape(shard_rows, features)
+        mine, here.swap(mine), here.quarter, core, width_k // HEAD, group
+    )
+    if (features // 2) % 128 or (features // 2 // quarters) % 16:
+        out_out = sum_up_out[:, :, cut:].astype(F32)
+        out_out = jnp.transpose(out_out, (3, 1, 0, 2)).reshape(shard_rows, features)
+    else:
+        out_out = spread_out(sum_up_out, cut)
     if quarters == experts:
         out_down = sum_down.astype(F32).reshape(experts, 2 * hidden_part, features)
     else:
@@ -862,8 +1007,8 @@
         out_out,
         small_sum[1],
         small_sum[2 : 2 + experts].T,
-        spread_experts(sum_gate_up, 0, experts, shards),
-        spread_experts(sum_gate_up, 1, experts, shards),
+        spread_experts(sum_gate, experts, shards, hidden_all),
+        spread_experts(sum_up_out, experts, shards, hidden_all),
         out_down,
     )
 

time: 1250 us -> 1020 us (0.82)
  Pallas kernels: 212 us -> 298 us
  local copies, waits for them, and re-layouts: 139 us -> 56.6 us
  starting transfers between devices: 190 us -> 110 us
  waiting for transfers between devices: 300 us -> 226 us
  matrix products: 281 us -> 213 us
  other arithmetic: 107 us -> 90.1 us
    ppermute x20, starting transfers between devices: 106 us -> 8.07 us  [swap(): return lax.ppermute(array, 'core', [(0, 1), (1, 0)])]
    reduce_scatter x4, waiting for transfers between devices: 89.5 us -> 0.04 us  [scatter(): return lax.psum_scatter(held, 'shard', scatter_dimension=0, tiled=False)]
    pallas_call x0 -> x8, Pallas kernels: none -> 84.6 us  [the longest x1 34.7 us: experts_forward(): pl.pallas_call(kernel, out_shape=(jax.ShapeDtypeStruct((count, columns),...]
    dot_general x22, matrix products: 281 us -> 213 us  [dot(): lax.dot_general(left, right, (((left_dim,), (right_dim,)), ((), ())), pre...]
    ppermute x6, waiting for transfers between devices: 59.1 us -> 6.55 us  [send_streams(): lax.ppermute(part, BOTH, self.moves(turn, False))]
    ppermute x4, waiting for transfers between devices: 0.01 us -> 45.6 us  [send_homes(): lax.ppermute(part, BOTH, self.moves(turn, True))]
    unnamed x258 -> x217, local copies, waits for them, and re-layouts: 63.3 us -> 33.7 us
    ppermute x9, waiting for transfers between devices: 21.3 us -> 49.8 us  [across(): lax.ppermute(array, 'chip', [(i, i ^ key) for i in range(self.quarters)])]
  transfers between devices with their start and end apart: 60 -> 61, of which waited for: 18 -> 17; matrix products, arithmetic and copies ran while one was open for 39% -> 31% of each run, Pallas kernels for 16% -> 28%
where the time goes in v3:
time: 1020 us; the launch traced here: 1010 us
  Pallas kernels  298 us (29%)
  waiting for transfers between devices  226 us (22%)
  matrix products  213 us (21%)
  starting transfers between devices  110 us (11%)
  other arithmetic  90.1 us (9%)
  local copies, waits for them, and re-layouts  56.6 us (6%)
  between operations  16.2 us (2%)
    dot_general x22, matrix products, dot(): lax.dot_general(left, right, (((left_dim,), (right_dim,)), ((), ())), pre...  213 us
    pallas_call x4, Pallas kernels, attend_backward(): pl.pallas_call(functools.partial(backward_kernel, group=group, wide=wide)...  108 us
    pallas_call x4, Pallas kernels, attend_forward(): pl.pallas_call(functools.partial(forward_kernel, group=group, wide=wide),...  66.6 us
    ppermute x9, waiting for transfers between devices, along(): lax.ppermute(array, 'shard', [(i, (i + step) % self.shards) for i in rang...  56.6 us
    ppermute x9, waiting for transfers between devices, across(): lax.ppermute(array, 'chip', [(i, i ^ key) for i in range(self.quarters)])  49.8 us
    ppermute x4, waiting for transfers between devices, send_homes(): lax.ppermute(part, BOTH, self.moves(turn, True))  45.6 us
    all_to_all x5, waiting for transfers between devices, exchange(): return lax.all_to_all(grad, 'chip', 0, 0, tiled=True)  41.5 us
    ppermute x6, starting transfers between devices, send_streams(): lax.ppermute(part, BOTH, self.moves(turn, False))  40.5 us
  transfers between devices with their start and end apart: 61, of which 17 were waited for; matrix products, arithmetic and copies ran while one was open for 31% of the time, Pallas kernels for 28%

profile of v3, /device:TPU:0, one launch (start us, length us, event | category | flops | bytes accessed | tf_op | source)
XLA Modules:
  0.0 1009.0 jit_solution(6706294077608005149)
XLA Ops:
  30.9 36.9 %collective-permute-done.3 = bf16[1,96,2176]{2,1,0:T(8,128)(2,1)} collective-permute-done((bf16[1,96,2176]{2,1,0:T(8,128)(2,1)}, bf16[1,96,2176]{2,1,0:T(8,128)(2,1)}, u32[]{:S(2)}, u32[]{:S(2)}) %collective-permute-start.3) | collective-permute-done | bytes 417824 | tf_op jit(solution)/shard_map/ppermute | solution.py:356
  82.5 19.4 %collective-permute-done.7.refs_3_ = bf16[3,1,96,2176]{3,2,1,0:T(8,128)(2,1)} collective-permute-done((bf16[3,1,96,2176]{3,2,1,0:T(8,128)(2,1)}, bf16[3,1,96,2176]{3,2,1,0:T(8,128)(2,1)}, u32[]{:S(2)}, u32[]{:S(2)}) %collective-permute-start.7) | collective-permute-done | bytes 1253408 | tf_op jit(solution)/shard_map/ppermute | solution.py:252
  102.0 21.4 %collective-permute-done.6.refs_2_ = bf16[3,1,96,2176]{3,2,1,0:T(8,128)(2,1)} collective-permute-done((bf16[3,1,96,2176]{3,2,1,0:T(8,128)(2,1)}, bf16[3,1,96,2176]{3,2,1,0:T(8,128)(2,1)}, u32[]{:S(2)}, u32[]{:S(2)}) %collective-permute-start.6) | collective-permute-done | bytes 1253408 | tf_op jit(solution)/shard_map/ppermute | solution.py:252
  162.7 17.1 %convolution_convert_fusion.1.refs_0_.refs_1_.refs_2_.refs_3_.refs_4_ = bf16[1280,2048]{1,0:T(8,128)(2,1)} fusion(bf16[1536,1280]{1,0:T(8,128)(2,1)} %bitcast.150, bf16[1024,1536]{1,0:T(8,128)(2,1)} %collective-permute-done.9, bf16[1024,1536]{1,0:T(8,128)(2,1)} %fusion.2, pred[]{:T(512)S(6)} %eq.41), kind=kOutput, calls=%fused_computation.7 | convolution fusion | flops 8083996672 | bytes 15466497 | tf_op jit(solution)/shard_map/dot_general | solution.py:30
  182.3 16.7 %attend_forward.4 = (bf16[192,2048]{1,0:T(8,128)(2,1)S(1)}, f32[1,3,2048]{2,1,0:T(4,128)S(1)}) custom-call(s32[4,4]{1,0:T(4,128)S(1)} %pad_add_fusion.2.ranges, bf16[1280,2048]{1,0:T(8,128)(2,1)S(1)} %copy-done.2, bf16[1280,2048]{1,0:T(8,128)(2,1)S(1)} %copy-done.2, bf16[1280,2048]{1,0:T(8,128)(2,1)S(1)} %copy-done.2, bf16[1280,2048]{1,0:T(8,128)(2,1)S(1)} %copy-done.2, ...), custom_call_target="tpu_custom_call" | custom-call | flops 1048576 | bytes 1048576 | tf_op jit(solution)/shard_map/attend_forward/pallas_call | solution.py:188
  200.6 16.4 %attend_forward.5 = (bf16[192,2048]{1,0:T(8,128)(2,1)S(1)}, f32[1,3,2048]{2,1,0:T(4,128)S(1)}) custom-call(s32[4,4]{1,0:T(4,128)S(1)} %pad_add_fusion.2.ranges, bf16[1280,2048]{1,0:T(8,128)(2,1)S(1)} %copy-done.2, bf16[1280,2048]{1,0:T(8,128)(2,1)S(1)} %copy-done.2, bf16[1280,2048]{1,0:T(8,128)(2,1)S(1)} %copy-done.2, bf16[1280,2048]{1,0:T(8,128)(2,1)S(1)} %copy-done.2, ...), custom_call_target="tpu_custom_call" | custom-call | flops 1048576 | bytes 1048576 | tf_op jit(solution)/shard_map/attend_forward/pallas_call | solution.py:188
  223.4 16.9 %attend_forward.6 = (bf16[192,2048]{1,0:T(8,128)(2,1)S(1)}, f32[1,3,2048]{2,1,0:T(4,128)S(1)}) custom-call(s32[4,4]{1,0:T(4,128)S(1)} %pad_add_fusion.2.ranges, bf16[1280,2048]{1,0:T(8,128)(2,1)S(1)} %copy-done.2, bf16[1280,2048]{1,0:T(8,128)(2,1)S(1)} %copy-done.2, bf16[1280,2048]{1,0:T(8,128)(2,1)S(1)} %copy-done.2, bf16[1280,2048]{1,0:T(8,128)(2,1)S(1)} %copy-done.2, ...), custom_call_target="tpu_custom_call" | custom-call | flops 1048576 | bytes 1048576 | tf_op jit(solution)/shard_map/attend_forward/pallas_call | solution.py:188
  242.3 16.6 %attend_forward.7 = (bf16[192,2048]{1,0:T(8,128)(2,1)S(1)}, f32[1,3,2048]{2,1,0:T(4,128)S(1)}) custom-call(s32[4,4]{1,0:T(4,128)S(1)} %pad_add_fusion.2.ranges, bf16[1280,2048]{1,0:T(8,128)(2,1)S(1)} %copy-done.2, bf16[1280,2048]{1,0:T(8,128)(2,1)S(1)} %copy-done.2, bf16[1280,2048]{1,0:T(8,128)(2,1)S(1)} %copy-done.2, bf16[1280,2048]{1,0:T(8,128)(2,1)S(1)} %copy-done.2, ...), custom_call_target="tpu_custom_call" | custom-call | flops 1048576 | bytes 1048576 | tf_op jit(solution)/shard_map/attend_forward/pallas_call | solution.py:188
  290.1 21.7 %all-gather.11.cloned.1.call-done = bf16[12288,1024]{1,0:T(8,128)(2,1)} async-done(((bf16[384,1024]{1,0:T(8,128)(2,1)}), bf16[12288,1024]{1,0:T(8,128)(2,1)}) %all-gather.11.cloned.1.call-update) | async-done | bytes 25165840 | tf_op jit(solution)/shard_map/all_gather | solution.py:427
  317.4 29.9 %collective-permute-start.21 = (bf16[512,1536]{1,0:T(8,128)(2,1)}, bf16[512,1536]{1,0:T(8,128)(2,1)}, u32[]{:S(2)}, u32[]{:S(2)}) collective-permute-start(bf16[512,1536]{1,0:T(8,128)(2,1)} %get-tuple-element.271), channel_id=1, source_target_pairs={{0,2},{1,0},{2,6},{3,4},{4,3},{5,1},{6,7},{7,5},{8,10},{9,8},{10,1... | collective-permute-start | bytes 4718600 | tf_op jit(solution)/shard_map/ppermute | solution.py:287
  375.0 34.7 %experts_forward.1 = (bf16[2048,2048]{1,0:T(8,128)(2,1)}, bf16[2048,2048]{1,0:T(8,128)(2,1)}, bf16[2048,2048]{1,0:T(8,128)(2,1)}) custom-call(bf16[2048,1536]{1,0:T(8,128)(2,1)} %pad_maximum_fusion.b_ref, bf16[1536,2048]{1,0:T(8,128)(2,1)} %core_columns.2.gate_w_ref, bf16[1536,2048]{1,0:T(8,128)(2,1)} %core_columns.3.up_w_ref, f32[2048,4]{1,0:T(8,128)S(1)} %copy.100.share_ref), custom_call_target="tpu_custom_call" | custom-call | flops 1048576 | bytes 1048576 | tf_op jit(solution)/shard_map/experts_forward/pallas_call | solution.py:643
  430.4 10.2 %add_convert_fusion = bf16[1024,1536]{1,0:T(8,128)(2,1)S(1)} fusion(bf16[1024,1536]{1,0:T(8,128)(2,1)} %collective-permute-done.30, f32[1024,1536]{1,0:T(8,128)} %copy-done.52, bf16[2048,1536]{1,0:T(8,128)(2,1)S(1)} %bitcast.130, bf16[2048,2048]{1,0:T(8,128)(2,1)} %get-tuple-element.143), kind=kOutput, calls=%fused_computation.25 | convolution fusion | flops 6448742400 | bytes 23068672 | tf_op jit(solution)/shard_map/dot_general | solution.py:30
  446.6 17.7 %convolution_convert_fusion.4 = bf16[2048,1536]{1,0:T(8,128)(2,1)} fusion(bf16[2048,2048]{1,0:T(8,128)(2,1)} %get-tuple-element.143, bf16[1024,1536]{1,0:T(8,128)(2,1)S(1)} %collective-permute-done.26, bf16[512,1536]{1,0:T(8,128)(2,1)S(1)} %get-tuple-element.257, bf16[512,1536]{1,0:T(8,128)(2,1)S(1)} %get-tuple-element.256), kind=kOutput, calls=%fused_computation.10 | convolution fusion | flops 12906921984 | bytes 20971520 | tf_op jit(solution)/shard_map/dot_general | solution.py:30
  473.2 26.4 %experts_backward.1 = (bf16[2048,2048]{1,0:T(8,128)(2,1)}, bf16[2048,2048]{1,0:T(8,128)(2,1)}, f32[2048,4]{1,0:T(8,128)S(1)}) custom-call(bf16[2048,1536]{1,0:T(8,128)(2,1)} %pad_maximum_fusion.1.dy_ref, bf16[2048,1536]{1,0:T(8,128)(2,1)} %bitcast.129, bf16[2048,2048]{1,0:T(8,128)(2,1)} %get-tuple-element.146.gate_ref, ...), custom_call_target="tpu_custom_call" | custom-call | flops 1048576 | bytes 1048576 | tf_op jit(solution)/shard_map/experts_backward/pallas_call | solution.py:684
  500.2 18.7 %convolution_convert_fusion.3 = bf16[2048,1536]{1,0:T(8,128)(2,1)} fusion(bf16[2048,2048]{1,0:T(8,128)(2,1)} %get-tuple-element.151, bf16[1024,1536]{1,0:T(8,128)(2,1)} %collective-permute-done.25, bf16[1024,1536]{1,0:T(8,128)(2,1)S(1)} %copy-done.51), kind=kOutput, calls=%fused_computation.9 | convolution fusion | flops 12900630528 | bytes 20971520 | tf_op jit(solution)/shard_map/dot_general | solution.py:30
  518.9 16.6 %convolution_convert_fusion.2 = bf16[2048,1536]{1,0:T(8,128)(2,1)} fusion(bf16[2048,2048]{1,0:T(8,128)(2,1)S(1)} %bitcast.192, bf16[1024,1536]{1,0:T(8,128)(2,1)} %collective-permute-done.25, bf16[1024,1536]{1,0:T(8,128)(2,1)S(1)} %copy-done.51), kind=kOutput, calls=%fused_computation.8 | convolution fusion | flops 12900630528 | bytes 20971520 | tf_op jit(solution)/shard_map/dot_general | solution.py:30
  574.0 12.1 %fusion.17 = f32[1024,1536]{1,0:T(8,128)} fusion(bf16[1536,2048]{1,0:T(8,128)(2,1)} %core_columns.2.gate_w_ref, bf16[2048,2048]{1,0:T(8,128)(2,1)} %get-tuple-element.151), kind=kOutput, calls=%fused_computation.42 | convolution fusion | flops 6442450944 | bytes 16777216 | tf_op jit(solution)/shard_map/dot_general | solution.py:30
  586.1 18.1 %multiply_reduce_fusion = (bf16[1536]{0:T(1024)(128)(2,1)}, f32[1024]{0:T(1024)S(1)}, f32[1024,1536]{1,0:T(8,128)}) fusion(f32[1024,1536]{1,0:T(8,128)} %copy-done.52, f32[1024]{0:T(1024)S(1)} %copy-done.86, f32[1536]{0:T(1024)S(1)} %copy-done.78, f32[1024,1536]{1,0:T(8,128)} %fusion.46, bf16[1024,1536]{1,0:T(8,128)(2,1)} %collective-permute-done.27, ...), kind=kOutput, calls=%fused_computation.24 | convolution fusion | flops 6458177024 | bytes 38814720 | tf_op jit(solution)/shard_map/dot_general | solution.py:30
  647.6 27.1 %attend_backward.4 = bf16[320,2048]{1,0:T(8,128)(2,1)S(1)} custom-call(s32[4,4]{1,0:T(4,128)S(1)} %pad_add_fusion.3.ranges, bf16[1280,2048]{1,0:T(8,128)(2,1)S(1)} %bitcast.125, bf16[1280,2048]{1,0:T(8,128)(2,1)S(1)} %bitcast.125, bf16[1280,2048]{1,0:T(8,128)(2,1)S(1)} %bitcast.125, bf16[1280,2048]{1,0:T(8,128)(2,1)S(1)} %bitcast.125, ...), custom_call_target="tpu_custom_call" | custom-call | flops 1048576 | bytes 1048576 | tf_op jit(solution)/shard_map/attend_backward/pallas_call | solution.py:214
  687.0 27.1 %attend_backward.5 = bf16[320,2048]{1,0:T(8,128)(2,1)S(1)} custom-call(s32[4,4]{1,0:T(4,128)S(1)} %pad_add_fusion.3.ranges, bf16[1280,2048]{1,0:T(8,128)(2,1)S(1)} %copy-done.3, bf16[1280,2048]{1,0:T(8,128)(2,1)S(1)} %copy-done.3, bf16[1280,2048]{1,0:T(8,128)(2,1)S(1)} %copy-done.3, bf16[1280,2048]{1,0:T(8,128)(2,1)S(1)} %copy-done.3, ...), custom_call_target="tpu_custom_call" | custom-call | flops 1048576 | bytes 1048576 | tf_op jit(solution)/shard_map/attend_backward/pallas_call | solution.py:214
  734.8 27.0 %attend_backward.6 = bf16[320,2048]{1,0:T(8,128)(2,1)S(1)} custom-call(s32[4,4]{1,0:T(4,128)S(1)} %pad_add_fusion.3.ranges, bf16[1280,2048]{1,0:T(8,128)(2,1)S(1)} %bitcast.127, bf16[1280,2048]{1,0:T(8,128)(2,1)S(1)} %bitcast.127, bf16[1280,2048]{1,0:T(8,128)(2,1)S(1)} %bitcast.127, bf16[1280,2048]{1,0:T(8,128)(2,1)S(1)} %bitcast.127, ...), custom_call_target="tpu_custom_call" | custom-call | flops 1048576 | bytes 1048576 | tf_op jit(solution)/shard_map/attend_backward/pallas_call | solution.py:214
  768.6 27.3 %attend_backward.7 = bf16[320,2048]{1,0:T(8,128)(2,1)S(1)} custom-call(s32[4,4]{1,0:T(4,128)S(1)} %pad_add_fusion.3.ranges, bf16[1280,2048]{1,0:T(8,128)(2,1)S(1)} %copy-done.4, bf16[1280,2048]{1,0:T(8,128)(2,1)S(1)} %copy-done.4, bf16[1280,2048]{1,0:T(8,128)(2,1)S(1)} %copy-done.4, bf16[1280,2048]{1,0:T(8,128)(2,1)S(1)} %copy-done.4, ...), custom_call_target="tpu_custom_call" | custom-call | flops 1048576 | bytes 1048576 | tf_op jit(solution)/shard_map/attend_backward/pallas_call | solution.py:214
  838.6 33.0 %all-to-all-done.4.in_ref = bf16[4,320,1536]{2,1,0:T(8,128)(2,1)} async-done(((bf16[4,320,1536]{2,1,0:T(8,128)(2,1)}), bf16[4,320,1536]{2,1,0:T(8,128)(2,1)}, u32[]{:S(2)}, u32[]{:S(2)}) %all-to-all-start.4) | async-done | bytes 3932192 | tf_op jit(solution)/shard_map/all_to_all | solution.py:430
  942.5 45.6 %collective-permute-done.42 = bf16[512,1536]{1,0:T(8,128)(2,1)} collective-permute-done((bf16[512,1536]{1,0:T(8,128)(2,1)}, bf16[512,1536]{1,0:T(8,128)(2,1)}, u32[]{:S(2)}, u32[]{:S(2)}) %collective-permute-start.42) | collective-permute-done | bytes 1572896 | tf_op jit(solution)/shard_map/ppermute | solution.py:309
  (474 shorter events, 438.1 us)
Async XLA Ops:
  7.2 304.6 %all-gather.11.cloned.1.call-start = ((), (), s32[]{:S(2)}) async-start(), calls=%async_computation.15 | async-start | bytes 25952256 | tf_op jit(solution)/shard_map/all_gather | solution.py:427
  153.7 116.7 %collective-permute-start.8 = (bf16[1536,768]{1,0:T(8,128)(2,1)}, bf16[1536,768]{1,0:T(8,128)(2,1)}, u32[]{:S(2)}, u32[]{:S(2)}) collective-permute-start(bf16[1536,768]{1,0:T(8,128)(2,1)} %bitcast.153), channel_id=1, source_target_pairs={{0,4},{4,0},{1,5},{5,1},{2,6},{6,2},{3,7},{7,3},{8,12},{12,8},{9,1... | collective-permute-start | bytes 7077896 | tf_op jit(solution)/shard_map/ppermute | solution.py:255
  161.2 61.3 %collective-permute-start.14 = (bf16[4,32,1536]{2,1,0:T(8,128)(2,1)S(1)}, bf16[4,32,1536]{2,1,0:T(8,128)(2,1)S(1)}, u32[]{:S(2)}, u32[]{:S(2)}) collective-permute-start(bf16[4,32,1536]{2,1,0:T(8,128)(2,1)S(1)} %dynamic-slice_bitcast_fusion.1), channel_id=1, source_target_pairs={{0,2},{1,3},{2,0},{3,1},{4,6},{5,7},{6,4},{7,5},{8,10},{9,11},{10,... | collective-permute-start | bytes 1179656 | tf_op jit(solution)/shard_map/ppermute | solution.py:356
  161.2 61.3 %collective-permute-start.13 = (bf16[4,32,1536]{2,1,0:T(8,128)(2,1)S(1)}, bf16[4,32,1536]{2,1,0:T(8,128)(2,1)S(1)}, u32[]{:S(2)}, u32[]{:S(2)}) collective-permute-start(bf16[4,32,1536]{2,1,0:T(8,128)(2,1)S(1)} %dynamic-slice_bitcast_fusion.1), channel_id=1, source_target_pairs={{0,1},{1,2},{2,3},{3,0},{4,5},{5,6},{6,7},{7,4},{8,9},{9,10},{10,1... | collective-permute-start | bytes 1179656 | tf_op jit(solution)/shard_map/ppermute | solution.py:356
  286.6 123.1 %collective-permute-start.24 = (bf16[3,4,32,1536]{3,2,1,0:T(8,128)(2,1)}, bf16[3,4,32,1536]{3,2,1,0:T(8,128)(2,1)}, u32[]{:S(2)}, u32[]{:S(2)}) collective-permute-start(bf16[3,4,32,1536]{3,2,1,0:T(8,128)(2,1)} %pad_maximum_fusion.6.refs_0_), channel_id=1, source_target_pairs={{0,24},{8,16},{16,8},{24,0},{1,25},{9,17},{17,9},{25,1},{2,26},{10... | collective-permute-start | bytes 3538952 | tf_op jit(solution)/shard_map/ppermute | solution.py:252
  286.6 123.1 %collective-permute-start.23 = (bf16[3,4,32,1536]{3,2,1,0:T(8,128)(2,1)}, bf16[3,4,32,1536]{3,2,1,0:T(8,128)(2,1)}, u32[]{:S(2)}, u32[]{:S(2)}) collective-permute-start(bf16[3,4,32,1536]{3,2,1,0:T(8,128)(2,1)} %pad_maximum_fusion.6.refs_0_), channel_id=1, source_target_pairs={{0,16},{8,24},{16,0},{24,8},{1,17},{9,25},{17,1},{25,9},{2,18},{10... | collective-permute-start | bytes 3538952 | tf_op jit(solution)/shard_map/ppermute | solution.py:252
  286.7 123.1 %collective-permute-start.22 = (bf16[3,4,32,1536]{3,2,1,0:T(8,128)(2,1)}, bf16[3,4,32,1536]{3,2,1,0:T(8,128)(2,1)}, u32[]{:S(2)}, u32[]{:S(2)}) collective-permute-start(bf16[3,4,32,1536]{3,2,1,0:T(8,128)(2,1)} %pad_maximum_fusion.6.refs_0_), channel_id=1, source_target_pairs={{0,8},{8,0},{16,24},{24,16},{1,9},{9,1},{17,25},{25,17},{2,10},{10... | collective-permute-start | bytes 3538952 | tf_op jit(solution)/shard_map/ppermute | solution.py:252
  315.6 98.2 %collective-permute-start.20 = (bf16[512,1536]{1,0:T(8,128)(2,1)}, bf16[512,1536]{1,0:T(8,128)(2,1)}, u32[]{:S(2)}, u32[]{:S(2)}) collective-permute-start(bf16[512,1536]{1,0:T(8,128)(2,1)} %get-tuple-element.270), channel_id=1, source_target_pairs={{1,2},{2,4},{3,6},{4,1},{5,3},{6,5},{9,10},{10,12},{11,14},{12,9},... | collective-permute-start | bytes 4718600 | tf_op jit(solution)/shard_map/ppermute | solution.py:287
  317.4 96.4 %collective-permute-start.21 = (bf16[512,1536]{1,0:T(8,128)(2,1)}, bf16[512,1536]{1,0:T(8,128)(2,1)}, u32[]{:S(2)}, u32[]{:S(2)}) collective-permute-start(bf16[512,1536]{1,0:T(8,128)(2,1)} %get-tuple-element.271), channel_id=1, source_target_pairs={{0,2},{1,0},{2,6},{3,4},{4,3},{5,1},{6,7},{7,5},{8,10},{9,8},{10,1... | collective-permute-start | bytes 4718600 | tf_op jit(solution)/shard_map/ppermute | solution.py:287
  424.2 223.4 %collective-permute-start.34 = (bf16[1536,1280]{1,0:T(8,128)(2,1)}, bf16[1536,1280]{1,0:T(8,128)(2,1)}, u32[]{:S(2)}, u32[]{:S(2)}) collective-permute-start(bf16[1536,1280]{1,0:T(8,128)(2,1)} %bitcast.151), channel_id=1, source_target_pairs={{0,4},{4,0},{1,5},{5,1},{2,6},{6,2},{3,7},{7,3},{8,12},{12,8},{9,1... | collective-permute-start | bytes 11796488 | tf_op jit(solution)/shard_map/ppermute | solution.py:255
  442.5 192.0 %collective-permute-start.32 = (bf16[512,1536]{1,0:T(8,128)(2,1)}, bf16[512,1536]{1,0:T(8,128)(2,1)}, u32[]{:S(2)}, u32[]{:S(2)}) collective-permute-start(bf16[512,1536]{1,0:T(8,128)(2,1)} %get-tuple-element.266), channel_id=1, source_target_pairs={{2,1},{4,2},{6,3},{1,4},{3,5},{5,6},{10,9},{12,10},{14,11},{9,12},... | collective-permute-start | bytes 4718600 | tf_op jit(solution)/shard_map/ppermute | solution.py:309
  444.4 190.1 %collective-permute-start.31 = (bf16[512,1536]{1,0:T(8,128)(2,1)}, bf16[512,1536]{1,0:T(8,128)(2,1)}, u32[]{:S(2)}, u32[]{:S(2)}) collective-permute-start(bf16[512,1536]{1,0:T(8,128)(2,1)} %get-tuple-element.267), channel_id=1, source_target_pairs={{2,0},{0,1},{6,2},{4,3},{3,4},{1,5},{7,6},{5,7},{10,8},{8,9},{14,1... | collective-permute-start | bytes 4718600 | tf_op jit(solution)/shard_map/ppermute | solution.py:309
  467.5 76.5 %all-to-all-start = ((bf16[4,4,128,1536]{3,2,1,0:T(8,128)(2,1)}), bf16[4,4,128,1536]{3,2,1,0:T(8,128)(2,1)}, u32[]{:S(2)}, u32[]{:S(2)}) async-start(bf16[4,4,128,1536]{3,2,1,0:T(8,128)(2,1)} %bitcast.169), calls=%async_computation | async-start | bytes 12582912 | tf_op jit(solution)/shard_map/all_to_all | solution.py:430
  499.7 64.7 %collective-permute-start.28 = (f32[1024,4]{1,0:T(8,128)S(1)}, f32[1024,4]{1,0:T(8,128)S(1)}, u32[]{:S(2)}, u32[]{:S(2)}) collective-permute-start(f32[1024,4]{1,0:T(8,128)S(1)} %slice.150), channel_id=1, source_target_pairs={{0,4},{4,0},{1,5},{5,1},{2,6},{6,2},{3,7},{7,3},{8,12},{12,8},{9,1... | collective-permute-start | bytes 49160 | tf_op jit(solution)/shard_map/ppermute | solution.py:255
  568.7 106.1 %all-to-all-start.1 = ((bf16[4,512,1536]{2,1,0:T(8,128)(2,1)}), bf16[4,512,1536]{2,1,0:T(8,128)(2,1)}, u32[]{:S(2)}, u32[]{:S(2)}) async-start(bf16[4,512,1536]{2,1,0:T(8,128)(2,1)} %bitcast.168), calls=%async_computation.1 | async-start | bytes 12582912 | tf_op jit(solution)/shard_map/all_to_all | solution.py:430
  573.9 241.7 %reduce-scatter.11.cloned.1.call-start = ((), (), s32[]{:S(2)}) async-start(), calls=%async_computation.13 | async-start | bytes 1966080 | tf_op jit(solution)/shard_map/reduce_scatter | solution.py:442
  679.3 136.9 %reduce-scatter.9.cloned.1.call-start = ((), (), s32[]{:S(2)}) async-start(), calls=%async_computation.11 | async-start | bytes 1966080 | tf_op jit(solution)/shard_map/reduce_scatter | solution.py:442
  715.2 95.5 %all-to-all-start.3 = ((bf16[4,512,1536]{2,1,0:T(8,128)(2,1)}), bf16[4,512,1536]{2,1,0:T(8,128)(2,1)}, u32[]{:S(2)}, u32[]{:S(2)}) async-start(bf16[4,512,1536]{2,1,0:T(8,128)(2,1)} %bitcast.167), calls=%async_computation.3 | async-start | bytes 12582912 | tf_op jit(solution)/shard_map/all_to_all | solution.py:430
  720.5 155.4 %reduce-scatter.7.cloned.1.call-start = ((), (), s32[]{:S(2)}) async-start(), calls=%async_computation.10 | async-start | bytes 737280 | tf_op jit(solution)/shard_map/reduce_scatter | solution.py:442
  766.0 109.8 %reduce-scatter.5.cloned.1.call-start = ((), (), s32[]{:S(2)}) async-start(), calls=%async_computation.9 | async-start | bytes 1966080 | tf_op jit(solution)/shard_map/reduce_scatter | solution.py:442
  815.5 112.0 %all-gather.9.cloned.1.call-start = ((), (), s32[]{:S(2)}) async-start(), calls=%async_computation.14 | async-start | bytes 3538944 | tf_op jit(solution)/shard_map/all_gather | solution.py:445
  816.1 116.9 %all-gather.7.cloned.1.call-start = ((), (), s32[]{:S(2)}) async-start(), calls=%async_computation.12 | async-start | bytes 3538944 | tf_op jit(solution)/shard_map/all_gather | solution.py:445
  821.8 170.5 %all-gather.13.cloned.1.call-start = ((), (), s32[]{:S(2)}) async-start(), calls=%async_computation.16 | async-start | bytes 4866048 | tf_op jit(solution)/shard_map/all_gather | solution.py:445
  913.1 75.0 %collective-permute-start.42 = (bf16[512,1536]{1,0:T(8,128)(2,1)}, bf16[512,1536]{1,0:T(8,128)(2,1)}, u32[]{:S(2)}, u32[]{:S(2)}) collective-permute-start(bf16[512,1536]{1,0:T(8,128)(2,1)} %get-tuple-element.261), channel_id=1, source_target_pairs={{2,0},{0,1},{6,2},{4,3},{3,4},{1,5},{7,6},{5,7},{10,8},{8,9},{14,1... | collective-permute-start | bytes 4718600 | tf_op jit(solution)/shard_map/ppermute | solution.py:309
  (140 other events, 2480.2 us)
Sparse Core Ops, SparseCore 0:
  129.6 182.1 all-gather.10
  634.6 33.8 reduce-scatter.10
  684.6 33.8 reduce-scatter.8
  766.2 20.5 reduce-scatter.6
  815.6 34.2 reduce-scatter.4
  851.7 34.9 all-gather.8
  888.6 40.2 all-gather.6
  930.8 40.3 all-gather.12

commit v4 on v3

--- a/solution.py
+++ b/solution.py
@@ -37,7 +37,7 @@
 
 
 def backward_blocks(length):
-    return min(512, length), min(256, length)
+    return min(256, length), min(256, length)
 
 
 def visible_mask(index, width, first_key, first_query, starts):
@@ -800,6 +800,7 @@
     )
     x_blocks, found = held[:2], held[2:]
     x_own = here.join_streams(tokens[:, 0], x_blocks)
+    x_other = here.swap(x_own)
     rows = x_own.shape[0]
     w_gate, routes, x_own = together(w_gate, routes, x_own)
     packed = here.gather_experts(w_gate, w_up)
@@ -820,8 +821,8 @@
 
     x_wide = x_own.astype(F32)
     scale_one = rms_scale(x_wide)
-    normed_own = (x_wide * scale_one * gain_one).astype(BF16)
-    normed = here.ordered(normed_own, here.swap(normed_own), 0)
+    x_all = here.ordered(x_own, x_other, 0).astype(F32)
+    normed = (x_all * rms_scale(x_all) * gain_one).astype(BF16)
     route_all = jnp.concatenate([route_own, here.swap(route_own)], axis=0)
     qkv_t = dot(qkv_w, normed, 0, 1, BF16)
     qkv_t = here.chip_exchange(qkv_t, 0, 1)
@@ -846,10 +847,6 @@
     o_own = here.ordered(
         here.head_order(o_mine, heads), here.head_order(o_got, heads), 0
     )
-    cotangent, packed = together(cotangent, packed)
-    dy_blocks = here.send_streams(cotangent[:, 0])
-    gate_w = core_columns(packed, 0, core, shards, experts)
-    up_w = core_columns(packed, 1, core, shards, experts)
     h_own = x_wide + dot(o_own, out_w, 0, 0)
 
     scale_two = rms_scale(h_own)
@@ -863,6 +860,11 @@
     chosen = jnp.sum(logits[:, None, :] * route_hot, axis=2)
     gate_share = jax.nn.softmax(chosen, axis=1)
     shares = jnp.sum(gate_share[:, :, None] * route_hot, axis=1)
+    packed, b_all, shares = together(packed, b_all, shares)
+    cotangent, packed = together(cotangent, packed)
+    dy_blocks = here.send_streams(cotangent[:, 0])
+    gate_w = core_columns(packed, 0, core, shards, experts)
+    up_w = core_columns(packed, 1, core, shards, experts)
 
     gate_v, up_v, mid = experts_forward(b_all, gate_w, up_w, shares)
     *found_down, mid = together(*found_down, mid)
@@ -926,6 +928,7 @@
     grad_out = dot(dattn, o_own, 0, 1, BF16)
     out_mine, out_other = here.halves(grad_out, 0)
     grad_out = (out_mine.astype(F32) + here.swap(out_other).astype(F32)).astype(BF16)
+    sum_down = here.gather(here.scatter(held_down))
     back_heads, back_rows, back_got = [], [], []
     for head in range(heads):
         g_h = do_t[head * o_heads[0].shape[0] : (head + 1) * o_heads[0].shape[0]]
@@ -940,7 +943,10 @@
         else:
             g_h, back_heads[-1] = together(g_h, back_heads[-1])
         if head == heads // 2:
-            g_h, got_grad_out, grad_up = together(g_h, got_grad_out, grad_up)
+            g_h, got_grad_out, grad_up, total_gate = together(
+                g_h, got_grad_out, grad_up, total_gate
+            )
+            sum_gate = here.gather(total_gate)
             got_grad_up = here.exchange(grad_up)
             total_out = here.scatter(sum_parts(got_grad_out, shards))
         back_h = attend_backward(
@@ -965,9 +971,9 @@
     da = dot(here.head_order(back_rows, heads), qkv_w, 0, 1) + dot(
         here.head_order(back_got, heads), qkv_w_got, 0, 1
     )
-    da, got_grad_qkv = together(da, got_grad_qkv)
     dx, grad_gain_one = norm_back(x_wide, scale_one, gain_one, da)
-    dx_rows = (dx + dh).astype(BF16)
+    dx_parts, dx_blocks = here.send_homes((dx + dh).astype(BF16))
+    got_grad_qkv, dx_blocks[0] = together(got_grad_qkv, dx_blocks[0])
 
     grad_small = jnp.concatenate([grad_gain_one[None], grad_gain_two[None], grad_router], axis=0)
     grad_small = jnp.pad(grad_small, ((0, 16 - grad_small.shape[0]), (0, 0))).astype(BF16)
@@ -976,10 +982,8 @@
     held_qkv, total_up, total_out = together(held_qkv, total_up, total_out)
     held_qkv = jnp.concatenate([held_qkv, grad_small], axis=1)
     total = here.reduce_along(held_qkv)
-    total, dx_rows = together(total, dx_rows)
-    input_grad = here.join_homes(*here.send_homes(dx_rows))
-    sum_down = here.gather(here.scatter(held_down))
-    sum_gate = here.gather(total_gate)
+    total, dx_blocks[1] = together(total, dx_blocks[1])
+    input_grad = here.join_homes(dx_parts, dx_blocks)
     sum_up_out = here.gather(jnp.concatenate([total_up, total_out], axis=0))
     cut = total_up.shape[0]
     mine = jnp.stack([total] + [here.across(total, key) for key in range(1, quarters)])

time: 1020 us -> 974 us (0.955)
  starting transfers between devices: 110 us -> 82.9 us
  matrix products: 213 us -> 201 us
    ppermute x4, waiting for transfers between devices: 45.6 us -> 0.01 us  [send_homes(): lax.ppermute(part, BOTH, self.moves(turn, True))]
    ppermute x9, waiting for transfers between devices: 56.6 us -> 90.8 us  [along(): lax.ppermute(array, 'shard', [(i, (i + step) % self.shards) for i in rang...]
    ppermute x6, starting transfers between devices: 40.5 us -> 13.6 us  [send_streams(): lax.ppermute(part, BOTH, self.moves(turn, False))]
    all_to_all x5, waiting for transfers between devices: 41.5 us -> 56.8 us  [exchange(): return lax.all_to_all(grad, 'chip', 0, 0, tiled=True)]
    dot_general x22, matrix products: 213 us -> 201 us  [dot(): lax.dot_general(left, right, (((left_dim,), (right_dim,)), ((), ())), pre...]
    unnamed x217 -> x209, local copies, waits for them, and re-layouts: 33.7 us -> 28.8 us
  transfers between devices with their start and end apart: 61 -> 61, of which waited for: 17 -> 18; matrix products, arithmetic and copies ran while one was open for 31% -> 31% of each run, Pallas kernels for 28% -> 29%
where the time goes in v4:
time: 974 us; the launch traced here: 968 us
  Pallas kernels  293 us (30%)
  waiting for transfers between devices  232 us (24%)
  matrix products  201 us (21%)
  other arithmetic  91.1 us (9%)
  starting transfers between devices  82.9 us (9%)
  local copies, waits for them, and re-layouts  51.8 us (5%)
  between operations  16 us (2%)
    dot_general x22, matrix products, dot(): lax.dot_general(left, right, (((left_dim,), (right_dim,)), ((), ())), pre...  201 us
    pallas_call x4, Pallas kernels, attend_backward(): pl.pallas_call(functools.partial(backward_kernel, group=group, wide=wide)...  102 us
    ppermute x9, waiting for transfers between devices, along(): lax.ppermute(array, 'shard', [(i, (i + step) % self.shards) for i in rang...  90.8 us
    pallas_call x4, Pallas kernels, attend_forward(): pl.pallas_call(functools.partial(forward_kernel, group=group, wide=wide),...  66.4 us
    all_to_all x5, waiting for transfers between devices, exchange(): return lax.all_to_all(grad, 'chip', 0, 0, tiled=True)  56.8 us
    ppermute x9, waiting for transfers between devices, across(): lax.ppermute(array, 'chip', [(i, i ^ key) for i in range(self.quarters)])  44.6 us
    pallas_call x1, Pallas kernels, experts_forward(): pl.pallas_call(kernel, out_shape=(jax.ShapeDtypeStruct((count, columns),...  34.7 us
    unnamed x209, local copies, waits for them, and re-layouts  28.8 us
  transfers between devices with their start and end apart: 61, of which 18 were waited for; matrix products, arithmetic and copies ran while one was open for 31% of the time, Pallas kernels for 29%

profile of v4, /device:TPU:0, one launch (start us, length us, event | category | flops | bytes accessed | tf_op | source)
XLA Modules:
  0.0 968.0 jit_solution(2495928836172650035)
XLA Ops:
  30.9 36.9 %collective-permute-done.3 = bf16[1,96,2176]{2,1,0:T(8,128)(2,1)} collective-permute-done((bf16[1,96,2176]{2,1,0:T(8,128)(2,1)}, bf16[1,96,2176]{2,1,0:T(8,128)(2,1)}, u32[]{:S(2)}, u32[]{:S(2)}) %collective-permute-start.3) | collective-permute-done | bytes 417824 | tf_op jit(solution)/shard_map/ppermute | solution.py:356
  82.5 19.4 %collective-permute-done.7.refs_3_ = bf16[3,1,96,2176]{3,2,1,0:T(8,128)(2,1)} collective-permute-done((bf16[3,1,96,2176]{3,2,1,0:T(8,128)(2,1)}, bf16[3,1,96,2176]{3,2,1,0:T(8,128)(2,1)}, u32[]{:S(2)}, u32[]{:S(2)}) %collective-permute-start.7) | collective-permute-done | bytes 1253408 | tf_op jit(solution)/shard_map/ppermute | solution.py:252
  102.0 21.4 %collective-permute-done.6.refs_2_ = bf16[3,1,96,2176]{3,2,1,0:T(8,128)(2,1)} collective-permute-done((bf16[3,1,96,2176]{3,2,1,0:T(8,128)(2,1)}, bf16[3,1,96,2176]{3,2,1,0:T(8,128)(2,1)}, u32[]{:S(2)}, u32[]{:S(2)}) %collective-permute-start.6) | collective-permute-done | bytes 1253408 | tf_op jit(solution)/shard_map/ppermute | solution.py:252
  173.0 16.4 %attend_forward.4 = (bf16[192,2048]{1,0:T(8,128)(2,1)S(1)}, f32[1,3,2048]{2,1,0:T(4,128)S(1)}) custom-call(s32[4,4]{1,0:T(4,128)S(1)} %pad_add_fusion.3.ranges, bf16[1280,2048]{1,0:T(8,128)(2,1)S(1)} %convolution_convert_fusion.1.refs_0_.refs_1_.refs_2_.refs_3_.refs_4_, ...), custom_call_target="tpu_custom_call" | custom-call | flops 1048576 | bytes 1048576 | tf_op jit(solution)/shard_map/attend_forward/pallas_call | solution.py:188
  191.4 16.7 %attend_forward.5 = (bf16[192,2048]{1,0:T(8,128)(2,1)S(1)}, f32[1,3,2048]{2,1,0:T(4,128)S(1)}) custom-call(s32[4,4]{1,0:T(4,128)S(1)} %pad_add_fusion.3.ranges, bf16[1280,2048]{1,0:T(8,128)(2,1)S(1)} %convolution_convert_fusion.1.refs_0_.refs_1_.refs_2_.refs_3_.refs_4_, ...), custom_call_target="tpu_custom_call" | custom-call | flops 1048576 | bytes 1048576 | tf_op jit(solution)/shard_map/attend_forward/pallas_call | solution.py:188
  212.2 16.4 %attend_forward.6 = (bf16[192,2048]{1,0:T(8,128)(2,1)S(1)}, f32[1,3,2048]{2,1,0:T(4,128)S(1)}) custom-call(s32[4,4]{1,0:T(4,128)S(1)} %pad_add_fusion.3.ranges, bf16[1280,2048]{1,0:T(8,128)(2,1)S(1)} %convolution_convert_fusion.1.refs_0_.refs_1_.refs_2_.refs_3_.refs_4_, ...), custom_call_target="tpu_custom_call" | custom-call | flops 1048576 | bytes 1048576 | tf_op jit(solution)/shard_map/attend_forward/pallas_call | solution.py:188
  230.6 16.9 %attend_forward.7 = (bf16[192,2048]{1,0:T(8,128)(2,1)S(1)}, f32[1,3,2048]{2,1,0:T(4,128)S(1)}) custom-call(s32[4,4]{1,0:T(4,128)S(1)} %pad_add_fusion.3.ranges, bf16[1280,2048]{1,0:T(8,128)(2,1)S(1)} %convolution_convert_fusion.1.refs_0_.refs_1_.refs_2_.refs_3_.refs_4_, ...), custom_call_target="tpu_custom_call" | custom-call | flops 1048576 | bytes 1048576 | tf_op jit(solution)/shard_map/attend_forward/pallas_call | solution.py:188
  286.9 22.3 %all-gather.10.cloned.1.call-done = bf16[12288,1024]{1,0:T(8,128)(2,1)} async-done(((bf16[384,1024]{1,0:T(8,128)(2,1)}), bf16[12288,1024]{1,0:T(8,128)(2,1)}) %all-gather.10.cloned.1.call-update) | async-done | bytes 25165840 | tf_op jit(solution)/shard_map/all_gather | solution.py:427
  339.8 34.7 %experts_forward.1 = (bf16[2048,2048]{1,0:T(8,128)(2,1)}, bf16[2048,2048]{1,0:T(8,128)(2,1)}, bf16[2048,2048]{1,0:T(8,128)(2,1)}) custom-call(bf16[2048,1536]{1,0:T(8,128)(2,1)} %pad_maximum_fusion.b_ref, bf16[1536,2048]{1,0:T(8,128)(2,1)} %core_columns.2.gate_w_ref, bf16[1536,2048]{1,0:T(8,128)(2,1)} %core_columns.3.up_w_ref, f32[2048,4]{1,0:T(8,128)S(1)} %copy.116.share_ref), custom_call_target="tpu_custom_call" | custom-call | flops 1048576 | bytes 1048576 | tf_op jit(solution)/shard_map/experts_forward/pallas_call | solution.py:643
  399.4 10.2 %add_convert_fusion = bf16[1024,1536]{1,0:T(8,128)(2,1)S(1)} fusion(bf16[1024,1536]{1,0:T(8,128)(2,1)} %collective-permute-done.30, f32[1024,1536]{1,0:T(8,128)} %copy-done.50, bf16[2048,1536]{1,0:T(8,128)(2,1)S(1)} %bitcast.139, bf16[2048,2048]{1,0:T(8,128)(2,1)} %get-tuple-element.150), kind=kOutput, calls=%fused_computation.27 | convolution fusion | flops 6448742400 | bytes 23068672 | tf_op jit(solution)/shard_map/dot_general | solution.py:30
  415.7 17.4 %convolution_convert_fusion.4 = bf16[2048,1536]{1,0:T(8,128)(2,1)} fusion(bf16[2048,2048]{1,0:T(8,128)(2,1)} %get-tuple-element.150, bf16[1024,1536]{1,0:T(8,128)(2,1)S(1)} %collective-permute-done.26, bf16[512,1536]{1,0:T(8,128)(2,1)S(1)} %get-tuple-element.264, bf16[512,1536]{1,0:T(8,128)(2,1)S(1)} %get-tuple-element.263), kind=kOutput, calls=%fused_computation.14 | convolution fusion | flops 12906921984 | bytes 20971520 | tf_op jit(solution)/shard_map/dot_general | solution.py:30
  441.7 26.4 %experts_backward.1 = (bf16[2048,2048]{1,0:T(8,128)(2,1)}, bf16[2048,2048]{1,0:T(8,128)(2,1)}, f32[2048,4]{1,0:T(8,128)S(1)}) custom-call(bf16[2048,1536]{1,0:T(8,128)(2,1)} %pad_maximum_fusion.1.dy_ref, bf16[2048,1536]{1,0:T(8,128)(2,1)} %bitcast.138, bf16[2048,2048]{1,0:T(8,128)(2,1)} %get-tuple-element.153.gate_ref, ...), custom_call_target="tpu_custom_call" | custom-call | flops 1048576 | bytes 1048576 | tf_op jit(solution)/shard_map/experts_backward/pallas_call | solution.py:684
  468.8 19.5 %convolution_convert_fusion.3 = bf16[2048,1536]{1,0:T(8,128)(2,1)} fusion(bf16[2048,2048]{1,0:T(8,128)(2,1)} %get-tuple-element.158, bf16[2048,1536]{1,0:T(8,128)(2,1)} %pad_maximum_fusion.b_ref), kind=kOutput, calls=%fused_computation.13 | convolution fusion | flops 12888047616 | bytes 20971520 | tf_op jit(solution)/shard_map/dot_general | solution.py:30
  488.4 15.1 %convolution_convert_fusion.2 = bf16[2048,1536]{1,0:T(8,128)(2,1)} fusion(bf16[2048,2048]{1,0:T(8,128)(2,1)S(1)} %bitcast.200, bf16[2048,1536]{1,0:T(8,128)(2,1)S(1)} %bitcast.173), kind=kOutput, calls=%fused_computation.12 | convolution fusion | flops 12888047616 | bytes 20971520 | tf_op jit(solution)/shard_map/dot_general | solution.py:30
  512.7 10.6 %fusion.15 = f32[1024,1536]{1,0:T(8,128)S(1)} fusion(bf16[1536,2048]{1,0:T(8,128)(2,1)} %core_columns.2.gate_w_ref, bf16[2048,2048]{1,0:T(8,128)(2,1)} %get-tuple-element.158), kind=kOutput, calls=%fused_computation.41 | convolution fusion | flops 6442450944 | bytes 16777216 | tf_op jit(solution)/shard_map/dot_general | solution.py:30
  543.0 11.9 %fusion.18 = f32[1024,1536]{1,0:T(8,128)} fusion(bf16[1536,2048]{1,0:T(8,128)(2,1)} %core_columns.2.gate_w_ref, bf16[2048,2048]{1,0:T(8,128)(2,1)} %get-tuple-element.158), kind=kOutput, calls=%fused_computation.44 | convolution fusion | flops 6442450944 | bytes 16777216 | tf_op jit(solution)/shard_map/dot_general | solution.py:30
  555.0 18.1 %multiply_reduce_fusion = (bf16[1536]{0:T(1024)(128)(2,1)}, f32[1024]{0:T(1024)S(1)}, f32[1024,1536]{1,0:T(8,128)}) fusion(f32[1024,1536]{1,0:T(8,128)} %copy-done.50, f32[1024]{0:T(1024)S(1)} %copy-done.84, f32[1536]{0:T(1024)S(1)} %copy-done.78, f32[1024,1536]{1,0:T(8,128)} %fusion.47, bf16[1024,1536]{1,0:T(8,128)(2,1)} %collective-permute-done.27, ...), kind=kOutput, calls=%fused_computation.26 | convolution fusion | flops 6458177024 | bytes 38814720 | tf_op jit(solution)/shard_map/dot_general | solution.py:30
  604.7 25.6 %attend_backward.4 = bf16[320,2048]{1,0:T(8,128)(2,1)S(1)} custom-call(s32[8,4]{1,0:T(8,128)S(1)} %pad_add_fusion.2.ranges, bf16[1280,2048]{1,0:T(8,128)(2,1)S(1)} %bitcast.134, bf16[1280,2048]{1,0:T(8,128)(2,1)S(1)} %bitcast.134, bf16[1280,2048]{1,0:T(8,128)(2,1)S(1)} %bitcast.134, bf16[1280,2048]{1,0:T(8,128)(2,1)S(1)} %bitcast.134, ...), custom_call_target="tpu_custom_call" | custom-call | flops 1048576 | bytes 1048576 | tf_op jit(solution)/shard_map/attend_backward/pallas_call | solution.py:214
  648.5 25.6 %attend_backward.5 = bf16[320,2048]{1,0:T(8,128)(2,1)S(1)} custom-call(s32[8,4]{1,0:T(8,128)S(1)} %pad_add_fusion.2.ranges, bf16[1280,2048]{1,0:T(8,128)(2,1)S(1)} %copy-done.3, bf16[1280,2048]{1,0:T(8,128)(2,1)S(1)} %copy-done.3, bf16[1280,2048]{1,0:T(8,128)(2,1)S(1)} %copy-done.3, bf16[1280,2048]{1,0:T(8,128)(2,1)S(1)} %copy-done.3, ...), custom_call_target="tpu_custom_call" | custom-call | flops 1048576 | bytes 1048576 | tf_op jit(solution)/shard_map/attend_backward/pallas_call | solution.py:214
  693.8 25.6 %attend_backward.6 = bf16[320,2048]{1,0:T(8,128)(2,1)S(1)} custom-call(s32[8,4]{1,0:T(8,128)S(1)} %pad_add_fusion.2.ranges, bf16[1280,2048]{1,0:T(8,128)(2,1)S(1)} %bitcast.136, bf16[1280,2048]{1,0:T(8,128)(2,1)S(1)} %bitcast.136, bf16[1280,2048]{1,0:T(8,128)(2,1)S(1)} %bitcast.136, bf16[1280,2048]{1,0:T(8,128)(2,1)S(1)} %bitcast.136, ...), custom_call_target="tpu_custom_call" | custom-call | flops 1048576 | bytes 1048576 | tf_op jit(solution)/shard_map/attend_backward/pallas_call | solution.py:214
  726.2 25.6 %attend_backward.7 = bf16[320,2048]{1,0:T(8,128)(2,1)S(1)} custom-call(s32[8,4]{1,0:T(8,128)S(1)} %pad_add_fusion.2.ranges, bf16[1280,2048]{1,0:T(8,128)(2,1)S(1)} %copy-done.4, bf16[1280,2048]{1,0:T(8,128)(2,1)S(1)} %copy-done.4, bf16[1280,2048]{1,0:T(8,128)(2,1)S(1)} %copy-done.4, bf16[1280,2048]{1,0:T(8,128)(2,1)S(1)} %copy-done.4, ...), custom_call_target="tpu_custom_call" | custom-call | flops 1048576 | bytes 1048576 | tf_op jit(solution)/shard_map/attend_backward/pallas_call | solution.py:214
  811.6 47.6 %all-to-all-done.4.in_ref = bf16[4,320,1536]{2,1,0:T(8,128)(2,1)} async-done(((bf16[4,320,1536]{2,1,0:T(8,128)(2,1)}), bf16[4,320,1536]{2,1,0:T(8,128)(2,1)}, u32[]{:S(2)}, u32[]{:S(2)}) %all-to-all-start.4) | async-done | bytes 3932192 | tf_op jit(solution)/shard_map/all_to_all | solution.py:430
  872.8 36.1 %collective-permute-done.40 = bf16[336,384]{1,0:T(8,128)(2,1)S(1)} collective-permute-done((bf16[336,384]{1,0:T(8,128)(2,1)S(1)}, bf16[336,384]{1,0:T(8,128)(2,1)S(1)}, u32[]{:S(2)}, u32[]{:S(2)}) %collective-permute-start.40) | collective-permute-done | bytes 258080 | tf_op jit(solution)/shard_map/ppermute | solution.py:356
  908.9 14.0 %collective-permute-done.41 = bf16[336,384]{1,0:T(8,128)(2,1)S(1)} collective-permute-done((bf16[336,384]{1,0:T(8,128)(2,1)S(1)}, bf16[336,384]{1,0:T(8,128)(2,1)S(1)}, u32[]{:S(2)}, u32[]{:S(2)}) %collective-permute-start.41) | collective-permute-done | bytes 258080 | tf_op jit(solution)/shard_map/ppermute | solution.py:356
  (472 shorter events, 421.5 us)
Async XLA Ops:
  7.2 302.1 %all-gather.10.cloned.1.call-start = ((), (), s32[]{:S(2)}) async-start(), calls=%async_computation.14 | async-start | bytes 25952256 | tf_op jit(solution)/shard_map/all_gather | solution.py:427
  146.5 111.9 %collective-permute-start.8 = (bf16[1536,768]{1,0:T(8,128)(2,1)}, bf16[1536,768]{1,0:T(8,128)(2,1)}, u32[]{:S(2)}, u32[]{:S(2)}) collective-permute-start(bf16[1536,768]{1,0:T(8,128)(2,1)} %bitcast.16), channel_id=1, source_target_pairs={{0,4},{4,0},{1,5},{5,1},{2,6},{6,2},{3,7},{7,3},{8,12},{12,8},{9,1... | collective-permute-start | bytes 7077896 | tf_op jit(solution)/shard_map/ppermute | solution.py:255
  149.9 58.8 %collective-permute-start.15 = (bf16[4,32,1536]{2,1,0:T(8,128)(2,1)S(1)}, bf16[4,32,1536]{2,1,0:T(8,128)(2,1)S(1)}, u32[]{:S(2)}, u32[]{:S(2)}) collective-permute-start(bf16[4,32,1536]{2,1,0:T(8,128)(2,1)S(1)} %dynamic-slice_bitcast_fusion.1), channel_id=1, source_target_pairs={{0,3},{1,0},{2,1},{3,2},{4,7},{5,4},{6,5},{7,6},{8,11},{9,8},{10,9... | collective-permute-start | bytes 1179656 | tf_op jit(solution)/shard_map/ppermute | solution.py:356
  150.9 60.4 %collective-permute-start.14 = (bf16[4,32,1536]{2,1,0:T(8,128)(2,1)S(1)}, bf16[4,32,1536]{2,1,0:T(8,128)(2,1)S(1)}, u32[]{:S(2)}, u32[]{:S(2)}) collective-permute-start(bf16[4,32,1536]{2,1,0:T(8,128)(2,1)S(1)} %dynamic-slice_bitcast_fusion.1), channel_id=1, source_target_pairs={{0,2},{1,3},{2,0},{3,1},{4,6},{5,7},{6,4},{7,5},{8,10},{9,11},{10,... | collective-permute-start | bytes 1179656 | tf_op jit(solution)/shard_map/ppermute | solution.py:356
  152.2 59.1 %collective-permute-start.13 = (bf16[4,32,1536]{2,1,0:T(8,128)(2,1)S(1)}, bf16[4,32,1536]{2,1,0:T(8,128)(2,1)S(1)}, u32[]{:S(2)}, u32[]{:S(2)}) collective-permute-start(bf16[4,32,1536]{2,1,0:T(8,128)(2,1)S(1)} %dynamic-slice_bitcast_fusion.1), channel_id=1, source_target_pairs={{0,1},{1,2},{2,3},{3,0},{4,5},{5,6},{6,7},{7,4},{8,9},{9,10},{10,1... | collective-permute-start | bytes 1179656 | tf_op jit(solution)/shard_map/ppermute | solution.py:356
  191.0 57.9 %collective-permute-start.16 = (bf16[192,1024]{1,0:T(8,128)(2,1)}, bf16[192,1024]{1,0:T(8,128)(2,1)}, u32[]{:S(2)}, u32[]{:S(2)}) collective-permute-start(bf16[192,1024]{1,0:T(8,128)(2,1)} %constant_dynamic-slice_fusion.16), channel_id=1, source_target_pairs={{0,4},{4,0},{1,5},{5,1},{2,6},{6,2},{3,7},{7,3},{8,12},{12,8},{9,1... | collective-permute-start | bytes 1179656 | tf_op jit(solution)/shard_map/ppermute | solution.py:255
  313.1 65.5 %collective-permute-start.21 = (bf16[512,1536]{1,0:T(8,128)(2,1)}, bf16[512,1536]{1,0:T(8,128)(2,1)}, u32[]{:S(2)}, u32[]{:S(2)}) collective-permute-start(bf16[512,1536]{1,0:T(8,128)(2,1)} %get-tuple-element.277), channel_id=1, source_target_pairs={{1,2},{2,4},{3,6},{4,1},{5,3},{6,5},{9,10},{10,12},{11,14},{12,9},... | collective-permute-start | bytes 4718600 | tf_op jit(solution)/shard_map/ppermute | solution.py:287
  315.0 63.7 %collective-permute-start.22 = (bf16[512,1536]{1,0:T(8,128)(2,1)}, bf16[512,1536]{1,0:T(8,128)(2,1)}, u32[]{:S(2)}, u32[]{:S(2)}) collective-permute-start(bf16[512,1536]{1,0:T(8,128)(2,1)} %get-tuple-element.278), channel_id=1, source_target_pairs={{0,2},{1,0},{2,6},{3,4},{4,3},{5,1},{6,7},{7,5},{8,10},{9,8},{10,1... | collective-permute-start | bytes 4718600 | tf_op jit(solution)/shard_map/ppermute | solution.py:287
  393.3 211.4 %collective-permute-start.34 = (bf16[1536,1280]{1,0:T(8,128)(2,1)}, bf16[1536,1280]{1,0:T(8,128)(2,1)}, u32[]{:S(2)}, u32[]{:S(2)}) collective-permute-start(bf16[1536,1280]{1,0:T(8,128)(2,1)} %bitcast.161), channel_id=1, source_target_pairs={{0,4},{4,0},{1,5},{5,1},{2,6},{6,2},{3,7},{7,3},{8,12},{12,8},{9,1... | collective-permute-start | bytes 11796488 | tf_op jit(solution)/shard_map/ppermute | solution.py:255
  411.6 184.1 %collective-permute-start.32 = (bf16[512,1536]{1,0:T(8,128)(2,1)}, bf16[512,1536]{1,0:T(8,128)(2,1)}, u32[]{:S(2)}, u32[]{:S(2)}) collective-permute-start(bf16[512,1536]{1,0:T(8,128)(2,1)} %get-tuple-element.273), channel_id=1, source_target_pairs={{2,1},{4,2},{6,3},{1,4},{3,5},{5,6},{10,9},{12,10},{14,11},{9,12},... | collective-permute-start | bytes 4718600 | tf_op jit(solution)/shard_map/ppermute | solution.py:309
  413.4 182.3 %collective-permute-start.31 = (bf16[512,1536]{1,0:T(8,128)(2,1)}, bf16[512,1536]{1,0:T(8,128)(2,1)}, u32[]{:S(2)}, u32[]{:S(2)}) collective-permute-start(bf16[512,1536]{1,0:T(8,128)(2,1)} %get-tuple-element.274), channel_id=1, source_target_pairs={{2,0},{0,1},{6,2},{4,3},{3,4},{1,5},{7,6},{5,7},{10,8},{8,9},{14,1... | collective-permute-start | bytes 4718600 | tf_op jit(solution)/shard_map/ppermute | solution.py:309
  436.2 76.4 %all-to-all-start = ((bf16[4,4,128,1536]{3,2,1,0:T(8,128)(2,1)}), bf16[4,4,128,1536]{3,2,1,0:T(8,128)(2,1)}, u32[]{:S(2)}, u32[]{:S(2)}) async-start(bf16[4,4,128,1536]{3,2,1,0:T(8,128)(2,1)} %bitcast.177), calls=%async_computation | async-start | bytes 12582912 | tf_op jit(solution)/shard_map/all_to_all | solution.py:430
  468.1 65.3 %collective-permute-start.28 = (f32[1024,4]{1,0:T(8,128)S(1)}, f32[1024,4]{1,0:T(8,128)S(1)}, u32[]{:S(2)}, u32[]{:S(2)}) collective-permute-start(f32[1024,4]{1,0:T(8,128)S(1)} %slice.156), channel_id=1, source_target_pairs={{0,4},{4,0},{1,5},{5,1},{2,6},{6,2},{3,7},{7,3},{8,12},{12,8},{9,1... | collective-permute-start | bytes 49160 | tf_op jit(solution)/shard_map/ppermute | solution.py:255
  537.7 92.6 %all-to-all-start.1 = ((bf16[4,512,1536]{2,1,0:T(8,128)(2,1)}), bf16[4,512,1536]{2,1,0:T(8,128)(2,1)}, u32[]{:S(2)}, u32[]{:S(2)}) async-start(bf16[4,512,1536]{2,1,0:T(8,128)(2,1)} %bitcast.176), calls=%async_computation.1 | async-start | bytes 12582912 | tf_op jit(solution)/shard_map/all_to_all | solution.py:430
  543.0 131.1 %reduce-scatter.5.cloned.1.call-start = ((), (), s32[]{:S(2)}) async-start(), calls=%async_computation.9 | async-start | bytes 1966080 | tf_op jit(solution)/shard_map/reduce_scatter | solution.py:442
  640.2 129.4 %reduce-scatter.11.cloned.1.call-start = ((), (), s32[]{:S(2)}) async-start(), calls=%async_computation.12 | async-start | bytes 1966080 | tf_op jit(solution)/shard_map/reduce_scatter | solution.py:442
  675.1 89.5 %all-to-all-start.3 = ((bf16[4,512,1536]{2,1,0:T(8,128)(2,1)}), bf16[4,512,1536]{2,1,0:T(8,128)(2,1)}, u32[]{:S(2)}, u32[]{:S(2)}) async-start(bf16[4,512,1536]{2,1,0:T(8,128)(2,1)} %bitcast.175), calls=%async_computation.4 | async-start | bytes 12582912 | tf_op jit(solution)/shard_map/all_to_all | solution.py:430
  680.7 182.6 %reduce-scatter.9.cloned.1.call-start = ((), (), s32[]{:S(2)}) async-start(), calls=%async_computation.11 | async-start | bytes 737280 | tf_op jit(solution)/shard_map/reduce_scatter | solution.py:442
  723.6 139.7 %reduce-scatter.7.cloned.1.call-start = ((), (), s32[]{:S(2)}) async-start(), calls=%async_computation.10 | async-start | bytes 1966080 | tf_op jit(solution)/shard_map/reduce_scatter | solution.py:442
  769.5 158.9 %all-gather.8.cloned.1.call-start = ((), (), s32[]{:S(2)}) async-start(), calls=%async_computation.13 | async-start | bytes 3538944 | tf_op jit(solution)/shard_map/all_gather | solution.py:445
  770.1 163.8 %all-gather.14.cloned.1.call-start = ((), (), s32[]{:S(2)}) async-start(), calls=%async_computation.16 | async-start | bytes 3538944 | tf_op jit(solution)/shard_map/all_gather | solution.py:445
  796.2 63.0 %all-to-all-start.4 = ((bf16[4,320,1536]{2,1,0:T(8,128)(2,1)}), bf16[4,320,1536]{2,1,0:T(8,128)(2,1)}, u32[]{:S(2)}, u32[]{:S(2)}) async-start(bf16[4,320,1536]{2,1,0:T(8,128)(2,1)} %maximum_bitcast_fusion), calls=%async_computation.5 | async-start | bytes 7864320 | tf_op jit(solution)/shard_map/all_to_all | solution.py:430
  801.5 150.1 %all-gather.12.cloned.1.call-start = ((), (), s32[]{:S(2)}) async-start(), calls=%async_computation.15 | async-start | bytes 4866048 | tf_op jit(solution)/shard_map/all_gather | solution.py:445
  865.3 58.8 %collective-permute-start.43 = (bf16[512,1536]{1,0:T(8,128)(2,1)}, bf16[512,1536]{1,0:T(8,128)(2,1)}, u32[]{:S(2)}, u32[]{:S(2)}) collective-permute-start(bf16[512,1536]{1,0:T(8,128)(2,1)} %get-tuple-element.268), channel_id=1, source_target_pairs={{2,0},{0,1},{6,2},{4,3},{3,4},{1,5},{7,6},{5,7},{10,8},{8,9},{14,1... | collective-permute-start | bytes 4718600 | tf_op jit(solution)/shard_map/ppermute | solution.py:309
  (136 other events, 2454.5 us)
Sparse Core Ops, SparseCore 0:
  129.7 179.5 all-gather.9
  635.8 34.2 reduce-scatter.4
  672.9 34.2 reduce-scatter.10
  723.7 21.3 reduce-scatter.8
  769.6 35.0 reduce-scatter.6
  806.5 52.5 all-gather.7
  861.0 32.7 all-gather.13
  896.2 49.6 all-gather.11

commit v5 on v4

--- a/solution.py
+++ b/solution.py
@@ -860,9 +860,11 @@
     chosen = jnp.sum(logits[:, None, :] * route_hot, axis=2)
     gate_share = jax.nn.softmax(chosen, axis=1)
     shares = jnp.sum(gate_share[:, :, None] * route_hot, axis=1)
-    packed, b_all, shares = together(packed, b_all, shares)
-    cotangent, packed = together(cotangent, packed)
-    dy_blocks = here.send_streams(cotangent[:, 0])
+    dy_parts = here.leaving(cotangent[:, 0])
+    packed, b_all, shares, *dy_parts = together(packed, b_all, shares, *dy_parts)
+    dy_blocks = [
+        lax.ppermute(part, BOTH, here.moves(turn, False)) for turn, part in enumerate(dy_parts)
+    ]
     gate_w = core_columns(packed, 0, core, shards, experts)
     up_w = core_columns(packed, 1, core, shards, experts)
 

time: 974 us -> 970 us (level)
    unnamed x209 -> x205, local copies, waits for them, and re-layouts: 28.8 us -> 31.8 us
  transfers between devices with their start and end apart: 61 -> 61, of which waited for: 18 -> 17; matrix products, arithmetic and copies ran while one was open for 31% -> 32% of each run, Pallas kernels for 29% -> 29%
where the time goes in v5:
time: 970 us; the launch traced here: 962 us
  Pallas kernels  294 us (30%)
  waiting for transfers between devices  225 us (23%)
  matrix products  202 us (21%)
  other arithmetic  90.1 us (9%)
  starting transfers between devices  79.7 us (8%)
  local copies, waits for them, and re-layouts  55.6 us (6%)
  between operations  16 us (2%)
    dot_general x22, matrix products, dot(): lax.dot_general(left, right, (((left_dim,), (right_dim,)), ((), ())), pre...  202 us
    pallas_call x4, Pallas kernels, attend_backward(): pl.pallas_call(functools.partial(backward_kernel, group=group, wide=wide)...  103 us
    ppermute x9, waiting for transfers between devices, along(): lax.ppermute(array, 'shard', [(i, (i + step) % self.shards) for i in rang...  90.9 us
    pallas_call x4, Pallas kernels, attend_forward(): pl.pallas_call(functools.partial(forward_kernel, group=group, wide=wide),...  66.7 us
    all_to_all x5, waiting for transfers between devices, exchange(): return lax.all_to_all(grad, 'chip', 0, 0, tiled=True)  57.1 us
    ppermute x9, waiting for transfers between devices, across(): lax.ppermute(array, 'chip', [(i, i ^ key) for i in range(self.quarters)])  43.2 us
    pallas_call x1, Pallas kernels, experts_forward(): pl.pallas_call(kernel, out_shape=(jax.ShapeDtypeStruct((count, columns),...  34.7 us
    unnamed x205, local copies, waits for them, and re-layouts  31.8 us
  transfers between devices with their start and end apart: 61, of which 17 were waited for; matrix products, arithmetic and copies ran while one was open for 32% of the time, Pallas kernels for 29%

profile of v5, /device:TPU:0, one launch (start us, length us, event | category | flops | bytes accessed | tf_op | source)
XLA Modules:
  0.0 962.1 jit_solution(9587448420591255732)
XLA Ops:
  30.9 36.9 %collective-permute-done.3 = bf16[1,96,2176]{2,1,0:T(8,128)(2,1)} collective-permute-done((bf16[1,96,2176]{2,1,0:T(8,128)(2,1)}, bf16[1,96,2176]{2,1,0:T(8,128)(2,1)}, u32[]{:S(2)}, u32[]{:S(2)}) %collective-permute-start.3) | collective-permute-done | bytes 417824 | tf_op jit(solution)/shard_map/ppermute | solution.py:356
  82.5 19.4 %collective-permute-done.7.refs_3_ = bf16[3,1,96,2176]{3,2,1,0:T(8,128)(2,1)} collective-permute-done((bf16[3,1,96,2176]{3,2,1,0:T(8,128)(2,1)}, bf16[3,1,96,2176]{3,2,1,0:T(8,128)(2,1)}, u32[]{:S(2)}, u32[]{:S(2)}) %collective-permute-start.7) | collective-permute-done | bytes 1253408 | tf_op jit(solution)/shard_map/ppermute | solution.py:252
  102.0 21.4 %collective-permute-done.6.refs_2_ = bf16[3,1,96,2176]{3,2,1,0:T(8,128)(2,1)} collective-permute-done((bf16[3,1,96,2176]{3,2,1,0:T(8,128)(2,1)}, bf16[3,1,96,2176]{3,2,1,0:T(8,128)(2,1)}, u32[]{:S(2)}, u32[]{:S(2)}) %collective-permute-start.6) | collective-permute-done | bytes 1253408 | tf_op jit(solution)/shard_map/ppermute | solution.py:252
  172.9 16.5 %attend_forward.4 = (bf16[192,2048]{1,0:T(8,128)(2,1)S(1)}, f32[1,3,2048]{2,1,0:T(4,128)S(1)}) custom-call(s32[4,4]{1,0:T(4,128)S(1)} %pad_add_fusion.3.ranges, bf16[1280,2048]{1,0:T(8,128)(2,1)S(1)} %convolution_convert_fusion.1.refs_0_.refs_1_.refs_2_.refs_3_.refs_4_, ...), custom_call_target="tpu_custom_call" | custom-call | flops 1048576 | bytes 1048576 | tf_op jit(solution)/shard_map/attend_forward/pallas_call | solution.py:188
  191.4 16.7 %attend_forward.5 = (bf16[192,2048]{1,0:T(8,128)(2,1)S(1)}, f32[1,3,2048]{2,1,0:T(4,128)S(1)}) custom-call(s32[4,4]{1,0:T(4,128)S(1)} %pad_add_fusion.3.ranges, bf16[1280,2048]{1,0:T(8,128)(2,1)S(1)} %convolution_convert_fusion.1.refs_0_.refs_1_.refs_2_.refs_3_.refs_4_, ...), custom_call_target="tpu_custom_call" | custom-call | flops 1048576 | bytes 1048576 | tf_op jit(solution)/shard_map/attend_forward/pallas_call | solution.py:188
  212.2 16.5 %attend_forward.6 = (bf16[192,2048]{1,0:T(8,128)(2,1)S(1)}, f32[1,3,2048]{2,1,0:T(4,128)S(1)}) custom-call(s32[4,4]{1,0:T(4,128)S(1)} %pad_add_fusion.3.ranges, bf16[1280,2048]{1,0:T(8,128)(2,1)S(1)} %convolution_convert_fusion.1.refs_0_.refs_1_.refs_2_.refs_3_.refs_4_, ...), custom_call_target="tpu_custom_call" | custom-call | flops 1048576 | bytes 1048576 | tf_op jit(solution)/shard_map/attend_forward/pallas_call | solution.py:188
  230.7 17.0 %attend_forward.7 = (bf16[192,2048]{1,0:T(8,128)(2,1)S(1)}, f32[1,3,2048]{2,1,0:T(4,128)S(1)}) custom-call(s32[4,4]{1,0:T(4,128)S(1)} %pad_add_fusion.3.ranges, bf16[1280,2048]{1,0:T(8,128)(2,1)S(1)} %convolution_convert_fusion.1.refs_0_.refs_1_.refs_2_.refs_3_.refs_4_, ...), custom_call_target="tpu_custom_call" | custom-call | flops 1048576 | bytes 1048576 | tf_op jit(solution)/shard_map/attend_forward/pallas_call | solution.py:188
  260.6 10.7 %multiply_reduce_fusion.2 = (f32[1024]{0:T(1024)S(1)}, f32[1024,1536]{1,0:T(8,128)S(1)}) fusion(bf16[1536,768]{1,0:T(8,128)(2,1)} %collective-permute-done.8, bf16[1536,768]{1,0:T(8,128)(2,1)} %bitcast.16, pred[]{:T(512)S(6)} %eq.41, bf16[1536,1024]{1,0:T(8,128)(2,1)} %copy-done.79, bf16[1536,1024]{1,0:T(8,128)(2,1)S(1)} %get-tuple-element.292, ...), kind=kOutput, calls=%fused_computation.33 | convolution fusion | flops 4860935168 | bytes 20451328 | tf_op jit(solution)/shard_map/dot_general | solution.py:30
  288.8 20.4 %all-gather.10.cloned.1.call-done = bf16[12288,1024]{1,0:T(8,128)(2,1)} async-done(((bf16[384,1024]{1,0:T(8,128)(2,1)}), bf16[12288,1024]{1,0:T(8,128)(2,1)}) %all-gather.10.cloned.1.call-update) | async-done | bytes 25165840 | tf_op jit(solution)/shard_map/all_gather | solution.py:427
  337.8 34.7 %experts_forward.1 = (bf16[2048,2048]{1,0:T(8,128)(2,1)}, bf16[2048,2048]{1,0:T(8,128)(2,1)}, bf16[2048,2048]{1,0:T(8,128)(2,1)}) custom-call(bf16[2048,1536]{1,0:T(8,128)(2,1)} %pad_maximum_fusion.b_ref, bf16[1536,2048]{1,0:T(8,128)(2,1)} %core_columns.2.gate_w_ref, bf16[1536,2048]{1,0:T(8,128)(2,1)} %core_columns.3.up_w_ref, f32[2048,4]{1,0:T(8,128)S(1)} %copy.116.share_ref), custom_call_target="tpu_custom_call" | custom-call | flops 1048576 | bytes 1048576 | tf_op jit(solution)/shard_map/experts_forward/pallas_call | solution.py:643
  411.8 17.4 %convolution_convert_fusion.4 = bf16[2048,1536]{1,0:T(8,128)(2,1)} fusion(bf16[2048,2048]{1,0:T(8,128)(2,1)} %get-tuple-element.150, bf16[1024,1536]{1,0:T(8,128)(2,1)S(1)} %collective-permute-done.26, bf16[512,1536]{1,0:T(8,128)(2,1)S(1)} %get-tuple-element.264, bf16[512,1536]{1,0:T(8,128)(2,1)S(1)} %get-tuple-element.263), kind=kOutput, calls=%fused_computation.14 | convolution fusion | flops 12906921984 | bytes 20971520 | tf_op jit(solution)/shard_map/dot_general | solution.py:30
  437.8 26.4 %experts_backward.1 = (bf16[2048,2048]{1,0:T(8,128)(2,1)}, bf16[2048,2048]{1,0:T(8,128)(2,1)}, f32[2048,4]{1,0:T(8,128)S(1)}) custom-call(bf16[2048,1536]{1,0:T(8,128)(2,1)} %pad_maximum_fusion.1.dy_ref, bf16[2048,1536]{1,0:T(8,128)(2,1)} %bitcast.138, bf16[2048,2048]{1,0:T(8,128)(2,1)} %get-tuple-element.153.gate_ref, ...), custom_call_target="tpu_custom_call" | custom-call | flops 1048576 | bytes 1048576 | tf_op jit(solution)/shard_map/experts_backward/pallas_call | solution.py:684
  464.9 19.5 %convolution_convert_fusion.3 = bf16[2048,1536]{1,0:T(8,128)(2,1)} fusion(bf16[2048,2048]{1,0:T(8,128)(2,1)} %get-tuple-element.158, bf16[2048,1536]{1,0:T(8,128)(2,1)} %pad_maximum_fusion.b_ref), kind=kOutput, calls=%fused_computation.13 | convolution fusion | flops 12888047616 | bytes 20971520 | tf_op jit(solution)/shard_map/dot_general | solution.py:30
  484.5 15.2 %convolution_convert_fusion.2 = bf16[2048,1536]{1,0:T(8,128)(2,1)} fusion(bf16[2048,2048]{1,0:T(8,128)(2,1)S(1)} %bitcast.200, bf16[2048,1536]{1,0:T(8,128)(2,1)S(1)} %bitcast.173), kind=kOutput, calls=%fused_computation.12 | convolution fusion | flops 12888047616 | bytes 20971520 | tf_op jit(solution)/shard_map/dot_general | solution.py:30
  508.8 10.6 %fusion.15 = f32[1024,1536]{1,0:T(8,128)S(1)} fusion(bf16[1536,2048]{1,0:T(8,128)(2,1)} %core_columns.2.gate_w_ref, bf16[2048,2048]{1,0:T(8,128)(2,1)} %get-tuple-element.158), kind=kOutput, calls=%fused_computation.41 | convolution fusion | flops 6442450944 | bytes 16777216 | tf_op jit(solution)/shard_map/dot_general | solution.py:30
  539.1 11.9 %fusion.18 = f32[1024,1536]{1,0:T(8,128)} fusion(bf16[1536,2048]{1,0:T(8,128)(2,1)} %core_columns.2.gate_w_ref, bf16[2048,2048]{1,0:T(8,128)(2,1)} %get-tuple-element.158), kind=kOutput, calls=%fused_computation.44 | convolution fusion | flops 6442450944 | bytes 16777216 | tf_op jit(solution)/shard_map/dot_general | solution.py:30
  551.0 18.1 %multiply_reduce_fusion = (bf16[1536]{0:T(1024)(128)(2,1)}, f32[1024]{0:T(1024)S(1)}, f32[1024,1536]{1,0:T(8,128)}) fusion(f32[1024,1536]{1,0:T(8,128)} %copy-done.50, f32[1024]{0:T(1024)S(1)} %copy-done.82, f32[1536]{0:T(1024)S(1)} %copy-done.76, f32[1024,1536]{1,0:T(8,128)} %fusion.47, bf16[1024,1536]{1,0:T(8,128)(2,1)} %collective-permute-done.27, ...), kind=kOutput, calls=%fused_computation.26 | convolution fusion | flops 6458177024 | bytes 38814720 | tf_op jit(solution)/shard_map/dot_general | solution.py:30
  600.8 25.7 %attend_backward.4 = bf16[320,2048]{1,0:T(8,128)(2,1)S(1)} custom-call(s32[8,4]{1,0:T(8,128)S(1)} %pad_add_fusion.2.ranges, bf16[1280,2048]{1,0:T(8,128)(2,1)S(1)} %bitcast.134, bf16[1280,2048]{1,0:T(8,128)(2,1)S(1)} %bitcast.134, bf16[1280,2048]{1,0:T(8,128)(2,1)S(1)} %bitcast.134, bf16[1280,2048]{1,0:T(8,128)(2,1)S(1)} %bitcast.134, ...), custom_call_target="tpu_custom_call" | custom-call | flops 1048576 | bytes 1048576 | tf_op jit(solution)/shard_map/attend_backward/pallas_call | solution.py:214
  644.5 25.6 %attend_backward.5 = bf16[320,2048]{1,0:T(8,128)(2,1)S(1)} custom-call(s32[8,4]{1,0:T(8,128)S(1)} %pad_add_fusion.2.ranges, bf16[1280,2048]{1,0:T(8,128)(2,1)S(1)} %copy-done.3, bf16[1280,2048]{1,0:T(8,128)(2,1)S(1)} %copy-done.3, bf16[1280,2048]{1,0:T(8,128)(2,1)S(1)} %copy-done.3, bf16[1280,2048]{1,0:T(8,128)(2,1)S(1)} %copy-done.3, ...), custom_call_target="tpu_custom_call" | custom-call | flops 1048576 | bytes 1048576 | tf_op jit(solution)/shard_map/attend_backward/pallas_call | solution.py:214
  689.8 25.6 %attend_backward.6 = bf16[320,2048]{1,0:T(8,128)(2,1)S(1)} custom-call(s32[8,4]{1,0:T(8,128)S(1)} %pad_add_fusion.2.ranges, bf16[1280,2048]{1,0:T(8,128)(2,1)S(1)} %bitcast.136, bf16[1280,2048]{1,0:T(8,128)(2,1)S(1)} %bitcast.136, bf16[1280,2048]{1,0:T(8,128)(2,1)S(1)} %bitcast.136, bf16[1280,2048]{1,0:T(8,128)(2,1)S(1)} %bitcast.136, ...), custom_call_target="tpu_custom_call" | custom-call | flops 1048576 | bytes 1048576 | tf_op jit(solution)/shard_map/attend_backward/pallas_call | solution.py:214
  722.2 25.6 %attend_backward.7 = bf16[320,2048]{1,0:T(8,128)(2,1)S(1)} custom-call(s32[8,4]{1,0:T(8,128)S(1)} %pad_add_fusion.2.ranges, bf16[1280,2048]{1,0:T(8,128)(2,1)S(1)} %copy-done.4, bf16[1280,2048]{1,0:T(8,128)(2,1)S(1)} %copy-done.4, bf16[1280,2048]{1,0:T(8,128)(2,1)S(1)} %copy-done.4, bf16[1280,2048]{1,0:T(8,128)(2,1)S(1)} %copy-done.4, ...), custom_call_target="tpu_custom_call" | custom-call | flops 1048576 | bytes 1048576 | tf_op jit(solution)/shard_map/attend_backward/pallas_call | solution.py:214
  807.2 48.0 %all-to-all-done.4.in_ref = bf16[4,320,1536]{2,1,0:T(8,128)(2,1)} async-done(((bf16[4,320,1536]{2,1,0:T(8,128)(2,1)}), bf16[4,320,1536]{2,1,0:T(8,128)(2,1)}, u32[]{:S(2)}, u32[]{:S(2)}) %all-to-all-start.4) | async-done | bytes 3932192 | tf_op jit(solution)/shard_map/all_to_all | solution.py:430
  868.8 34.8 %collective-permute-done.40 = bf16[336,384]{1,0:T(8,128)(2,1)S(1)} collective-permute-done((bf16[336,384]{1,0:T(8,128)(2,1)S(1)}, bf16[336,384]{1,0:T(8,128)(2,1)S(1)}, u32[]{:S(2)}, u32[]{:S(2)}) %collective-permute-start.40) | collective-permute-done | bytes 258080 | tf_op jit(solution)/shard_map/ppermute | solution.py:356
  903.6 15.5 %collective-permute-done.41 = bf16[336,384]{1,0:T(8,128)(2,1)S(1)} collective-permute-done((bf16[336,384]{1,0:T(8,128)(2,1)S(1)}, bf16[336,384]{1,0:T(8,128)(2,1)S(1)}, u32[]{:S(2)}, u32[]{:S(2)}) %collective-permute-start.41) | collective-permute-done | bytes 258080 | tf_op jit(solution)/shard_map/ppermute | solution.py:356
  (468 shorter events, 415.9 us)
Async XLA Ops:
  7.2 302.0 %all-gather.10.cloned.1.call-start = ((), (), s32[]{:S(2)}) async-start(), calls=%async_computation.14 | async-start | bytes 25952256 | tf_op jit(solution)/shard_map/all_gather | solution.py:427
  146.5 112.4 %collective-permute-start.8 = (bf16[1536,768]{1,0:T(8,128)(2,1)}, bf16[1536,768]{1,0:T(8,128)(2,1)}, u32[]{:S(2)}, u32[]{:S(2)}) collective-permute-start(bf16[1536,768]{1,0:T(8,128)(2,1)} %bitcast.16), channel_id=1, source_target_pairs={{0,4},{4,0},{1,5},{5,1},{2,6},{6,2},{3,7},{7,3},{8,12},{12,8},{9,1... | collective-permute-start | bytes 7077896 | tf_op jit(solution)/shard_map/ppermute | solution.py:255
  149.9 58.9 %collective-permute-start.15 = (bf16[4,32,1536]{2,1,0:T(8,128)(2,1)S(1)}, bf16[4,32,1536]{2,1,0:T(8,128)(2,1)S(1)}, u32[]{:S(2)}, u32[]{:S(2)}) collective-permute-start(bf16[4,32,1536]{2,1,0:T(8,128)(2,1)S(1)} %dynamic-slice_bitcast_fusion.1), channel_id=1, source_target_pairs={{0,3},{1,0},{2,1},{3,2},{4,7},{5,4},{6,5},{7,6},{8,11},{9,8},{10,9... | collective-permute-start | bytes 1179656 | tf_op jit(solution)/shard_map/ppermute | solution.py:356
  150.9 60.4 %collective-permute-start.14 = (bf16[4,32,1536]{2,1,0:T(8,128)(2,1)S(1)}, bf16[4,32,1536]{2,1,0:T(8,128)(2,1)S(1)}, u32[]{:S(2)}, u32[]{:S(2)}) collective-permute-start(bf16[4,32,1536]{2,1,0:T(8,128)(2,1)S(1)} %dynamic-slice_bitcast_fusion.1), channel_id=1, source_target_pairs={{0,2},{1,3},{2,0},{3,1},{4,6},{5,7},{6,4},{7,5},{8,10},{9,11},{10,... | collective-permute-start | bytes 1179656 | tf_op jit(solution)/shard_map/ppermute | solution.py:356
  152.2 59.1 %collective-permute-start.13 = (bf16[4,32,1536]{2,1,0:T(8,128)(2,1)S(1)}, bf16[4,32,1536]{2,1,0:T(8,128)(2,1)S(1)}, u32[]{:S(2)}, u32[]{:S(2)}) collective-permute-start(bf16[4,32,1536]{2,1,0:T(8,128)(2,1)S(1)} %dynamic-slice_bitcast_fusion.1), channel_id=1, source_target_pairs={{0,1},{1,2},{2,3},{3,0},{4,5},{5,6},{6,7},{7,4},{8,9},{9,10},{10,1... | collective-permute-start | bytes 1179656 | tf_op jit(solution)/shard_map/ppermute | solution.py:356
  191.0 58.0 %collective-permute-start.16 = (bf16[192,1024]{1,0:T(8,128)(2,1)}, bf16[192,1024]{1,0:T(8,128)(2,1)}, u32[]{:S(2)}, u32[]{:S(2)}) collective-permute-start(bf16[192,1024]{1,0:T(8,128)(2,1)} %constant_dynamic-slice_fusion.16), channel_id=1, source_target_pairs={{0,4},{4,0},{1,5},{5,1},{2,6},{6,2},{3,7},{7,3},{8,12},{12,8},{9,1... | collective-permute-start | bytes 1179656 | tf_op jit(solution)/shard_map/ppermute | solution.py:255
  309.2 67.3 %collective-permute-start.21 = (bf16[512,1536]{1,0:T(8,128)(2,1)}, bf16[512,1536]{1,0:T(8,128)(2,1)}, u32[]{:S(2)}, u32[]{:S(2)}) collective-permute-start(bf16[512,1536]{1,0:T(8,128)(2,1)} %get-tuple-element.134), channel_id=1, source_target_pairs={{1,2},{2,4},{3,6},{4,1},{5,3},{6,5},{9,10},{10,12},{11,14},{12,9},... | collective-permute-start | bytes 4718600 | tf_op jit(solution)/shard_map/ppermute | solution.py:866
  311.0 65.5 %collective-permute-start.22 = (bf16[512,1536]{1,0:T(8,128)(2,1)}, bf16[512,1536]{1,0:T(8,128)(2,1)}, u32[]{:S(2)}, u32[]{:S(2)}) collective-permute-start(bf16[512,1536]{1,0:T(8,128)(2,1)} %get-tuple-element.135), channel_id=1, source_target_pairs={{0,2},{1,0},{2,6},{3,4},{4,3},{5,1},{6,7},{7,5},{8,10},{9,8},{10,1... | collective-permute-start | bytes 4718600 | tf_op jit(solution)/shard_map/ppermute | solution.py:866
  389.4 211.4 %collective-permute-start.34 = (bf16[1536,1280]{1,0:T(8,128)(2,1)}, bf16[1536,1280]{1,0:T(8,128)(2,1)}, u32[]{:S(2)}, u32[]{:S(2)}) collective-permute-start(bf16[1536,1280]{1,0:T(8,128)(2,1)} %bitcast.161), channel_id=1, source_target_pairs={{0,4},{4,0},{1,5},{5,1},{2,6},{6,2},{3,7},{7,3},{8,12},{12,8},{9,1... | collective-permute-start | bytes 11796488 | tf_op jit(solution)/shard_map/ppermute | solution.py:255
  407.8 184.0 %collective-permute-start.32 = (bf16[512,1536]{1,0:T(8,128)(2,1)}, bf16[512,1536]{1,0:T(8,128)(2,1)}, u32[]{:S(2)}, u32[]{:S(2)}) collective-permute-start(bf16[512,1536]{1,0:T(8,128)(2,1)} %get-tuple-element.273), channel_id=1, source_target_pairs={{2,1},{4,2},{6,3},{1,4},{3,5},{5,6},{10,9},{12,10},{14,11},{9,12},... | collective-permute-start | bytes 4718600 | tf_op jit(solution)/shard_map/ppermute | solution.py:309
  409.6 182.2 %collective-permute-start.31 = (bf16[512,1536]{1,0:T(8,128)(2,1)}, bf16[512,1536]{1,0:T(8,128)(2,1)}, u32[]{:S(2)}, u32[]{:S(2)}) collective-permute-start(bf16[512,1536]{1,0:T(8,128)(2,1)} %get-tuple-element.274), channel_id=1, source_target_pairs={{2,0},{0,1},{6,2},{4,3},{3,4},{1,5},{7,6},{5,7},{10,8},{8,9},{14,1... | collective-permute-start | bytes 4718600 | tf_op jit(solution)/shard_map/ppermute | solution.py:309
  432.3 76.4 %all-to-all-start = ((bf16[4,4,128,1536]{3,2,1,0:T(8,128)(2,1)}), bf16[4,4,128,1536]{3,2,1,0:T(8,128)(2,1)}, u32[]{:S(2)}, u32[]{:S(2)}) async-start(bf16[4,4,128,1536]{3,2,1,0:T(8,128)(2,1)} %bitcast.177), calls=%async_computation | async-start | bytes 12582912 | tf_op jit(solution)/shard_map/all_to_all | solution.py:430
  464.2 65.3 %collective-permute-start.28 = (f32[1024,4]{1,0:T(8,128)S(1)}, f32[1024,4]{1,0:T(8,128)S(1)}, u32[]{:S(2)}, u32[]{:S(2)}) collective-permute-start(f32[1024,4]{1,0:T(8,128)S(1)} %slice.156), channel_id=1, source_target_pairs={{0,4},{4,0},{1,5},{5,1},{2,6},{6,2},{3,7},{7,3},{8,12},{12,8},{9,1... | collective-permute-start | bytes 49160 | tf_op jit(solution)/shard_map/ppermute | solution.py:255
  533.8 92.7 %all-to-all-start.1 = ((bf16[4,512,1536]{2,1,0:T(8,128)(2,1)}), bf16[4,512,1536]{2,1,0:T(8,128)(2,1)}, u32[]{:S(2)}, u32[]{:S(2)}) async-start(bf16[4,512,1536]{2,1,0:T(8,128)(2,1)} %bitcast.176), calls=%async_computation.1 | async-start | bytes 12582912 | tf_op jit(solution)/shard_map/all_to_all | solution.py:430
  539.0 131.1 %reduce-scatter.5.cloned.1.call-start = ((), (), s32[]{:S(2)}) async-start(), calls=%async_computation.9 | async-start | bytes 1966080 | tf_op jit(solution)/shard_map/reduce_scatter | solution.py:442
  636.3 129.3 %reduce-scatter.11.cloned.1.call-start = ((), (), s32[]{:S(2)}) async-start(), calls=%async_computation.12 | async-start | bytes 1966080 | tf_op jit(solution)/shard_map/reduce_scatter | solution.py:442
  671.2 89.5 %all-to-all-start.3 = ((bf16[4,512,1536]{2,1,0:T(8,128)(2,1)}), bf16[4,512,1536]{2,1,0:T(8,128)(2,1)}, u32[]{:S(2)}, u32[]{:S(2)}) async-start(bf16[4,512,1536]{2,1,0:T(8,128)(2,1)} %bitcast.175), calls=%async_computation.4 | async-start | bytes 12582912 | tf_op jit(solution)/shard_map/all_to_all | solution.py:430
  676.6 182.7 %reduce-scatter.9.cloned.1.call-start = ((), (), s32[]{:S(2)}) async-start(), calls=%async_computation.11 | async-start | bytes 737280 | tf_op jit(solution)/shard_map/reduce_scatter | solution.py:442
  719.6 139.7 %reduce-scatter.7.cloned.1.call-start = ((), (), s32[]{:S(2)}) async-start(), calls=%async_computation.10 | async-start | bytes 1966080 | tf_op jit(solution)/shard_map/reduce_scatter | solution.py:442
  765.6 158.2 %all-gather.8.cloned.1.call-start = ((), (), s32[]{:S(2)}) async-start(), calls=%async_computation.13 | async-start | bytes 3538944 | tf_op jit(solution)/shard_map/all_gather | solution.py:445
  766.2 163.1 %all-gather.14.cloned.1.call-start = ((), (), s32[]{:S(2)}) async-start(), calls=%async_computation.16 | async-start | bytes 3538944 | tf_op jit(solution)/shard_map/all_gather | solution.py:445
  792.2 63.0 %all-to-all-start.4 = ((bf16[4,320,1536]{2,1,0:T(8,128)(2,1)}), bf16[4,320,1536]{2,1,0:T(8,128)(2,1)}, u32[]{:S(2)}, u32[]{:S(2)}) async-start(bf16[4,320,1536]{2,1,0:T(8,128)(2,1)} %maximum_bitcast_fusion), calls=%async_computation.5 | async-start | bytes 7864320 | tf_op jit(solution)/shard_map/all_to_all | solution.py:430
  797.1 148.5 %all-gather.12.cloned.1.call-start = ((), (), s32[]{:S(2)}) async-start(), calls=%async_computation.15 | async-start | bytes 4866048 | tf_op jit(solution)/shard_map/all_gather | solution.py:445
  861.3 58.9 %collective-permute-start.43 = (bf16[512,1536]{1,0:T(8,128)(2,1)}, bf16[512,1536]{1,0:T(8,128)(2,1)}, u32[]{:S(2)}, u32[]{:S(2)}) collective-permute-start(bf16[512,1536]{1,0:T(8,128)(2,1)} %get-tuple-element.268), channel_id=1, source_target_pairs={{2,0},{0,1},{6,2},{4,3},{3,4},{1,5},{7,6},{5,7},{10,8},{8,9},{14,1... | collective-permute-start | bytes 4718600 | tf_op jit(solution)/shard_map/ppermute | solution.py:309
  (134 other events, 2379.5 us)
Sparse Core Ops, SparseCore 0:
  129.7 179.5 all-gather.9
  631.9 33.7 reduce-scatter.4
  668.6 34.2 reduce-scatter.10
  719.7 21.2 reduce-scatter.8
  765.7 34.9 reduce-scatter.6
  802.5 53.7 all-gather.7
  858.1 31.1 all-gather.13
  891.8 48.1 all-gather.11
